TPU v7x, 512 devices: a whole 4x8x8 slice. The times are simulated.
512 devices in a mesh: row: 32 (over x, y_lo, core), col: 16 (over y_hi, z).
Axes of the slice: x: 4, y: 8 (y_hi: 2, y_lo: 4; y = y_hi * 4 + y_lo), z: 8, core: 2. Of those that a mesh axis runs over, the one named last changes fastest.
Arguments:
- objects: float32 [2, 2, 4096, 4096], P(None, None, 'row', 'col'), as said below
- probe_modes: float32 [4, 2, 128, 128], replicated, may hold values from -3 to 3
- intensities: float32 [32, 16, 2, 128, 128], P('row', 'col'), may hold values from 0 to 2
- positions: int32 [32, 16, 2, 2], P('row', 'col'), may hold values from 0 to 3968, as said below
- counts: int32 [32, 16], P('row', 'col'), may hold values from 0 to 2, as said below
Outputs:
- refined_object: float32 [2, 2, 4096, 4096], P(None, None, 'row', 'col')
- refined_probe: float32 [4, 2, 128, 128], replicated
Inputs may be any that keep to these rules, and one draw needn't show every extreme that they name: `positions`: for the pattern slot [i, j, k], the row of its top-left pixel plus 128 / 2 lies in [i * 128, (i + 1) * 128) and the column plus 128 / 2 in [j * 256, (j + 1) * 256); every patch lies inside the object; slot 0 of the first tile starts at pixel (0, 0) and slot 0 of the last tile ends at the object's last row and column. The live slots of a tile are its first counts[i, j] slots; some tile has all 2 live and some tile has none. `objects`: every entry lies in [-1.5, 1.5].
All inputs are finite; a program needn't handle non-finite values.
Results may differ from a plain program's by a relative error of at most 0.0003.
Values sent between devices are 32-bit elements; how exact they have to be, the bound alone decides.
No kernel may reach another device: no remote copies, remote signals or barrier semaphores. Data moves between devices by JAX's collectives and lax.ppermute only.
A program may use at most 64 MiB of HBM per device.

v0:
```python
import math

import jax
import jax.numpy as jnp
from jax import lax
from jax.sharding import PartitionSpec as P

ITERS = 2


highest = lax.Precision.HIGHEST


def extended_2(value, sides, width):
    for axis, dim in sides:
        size, length = (lax.axis_size(axis), value.shape[dim])
        up = [(i, (i + 1) % size) for i in range(size - 1)]
        down = [(j, i) for i, j in up]
        last = lax.slice_in_dim(value, length - width, length, axis=dim)
        initial = lax.slice_in_dim(value, 0, width, axis=dim)
        before = lax.ppermute(last, axis, up)
        after = lax.ppermute(initial, axis, down)
        value = jnp.concatenate([before, value, after], axis=dim)
    return value


def block_table(upper_left, upper_right, lower_left, lower_right):
    return jnp.stack([jnp.stack([upper_left, upper_right]), jnp.stack([lower_left, lower_right])])


def fourier_tables(width):
    index = jnp.arange(width, dtype=jnp.int32)
    product = index[:, None] * index[None, :] % width
    angle = product.astype(jnp.float32) * (-2.0 * math.pi / width)
    scale = 1.0 / math.sqrt(width)
    middle = width // 2
    frequency = ((index + middle) % width - middle).astype(jnp.float32)
    phase = (frequency[:, None] ** 2 + frequency[None, :] ** 2) * (-4.0 * math.pi / (width * width))
    cosine = jnp.cos(angle) * scale
    sine = jnp.sin(angle) * scale
    forward_left = block_table(cosine, -sine, sine, cosine)
    forward_right = block_table(cosine, sine, -sine, cosine)
    inverse_left = block_table(cosine, sine, -sine, cosine)
    inverse_right = block_table(cosine, -sine, sine, cosine)
    return (
        forward_left,
        forward_right,
        inverse_left,
        inverse_right,
        jnp.cos(phase),
        jnp.sin(phase),
    )


def fourier_field(field, tables, direction):
    if direction > 0:
        left_table, right_table = (tables[0], tables[1])
    else:
        left_table, right_table = (tables[2], tables[3])
    upper = jnp.einsum("pqab,kmqbc->kmpac", left_table, field, precision=highest)
    return jnp.einsum("kmqab,qpbc->kmpac", upper, right_table, precision=highest)


def complex_product(first, second):
    real_part = first[:, :, 0] * second[:, :, 0] - first[:, :, 1] * second[:, :, 1]
    imag_part = first[:, :, 0] * second[:, :, 1] + first[:, :, 1] * second[:, :, 0]
    return jnp.stack([real_part, imag_part], axis=2)


def conj_product(first, second):
    real_part = first[:, :, 0] * second[:, :, 0] + first[:, :, 1] * second[:, :, 1]
    imag_part = first[:, :, 0] * second[:, :, 1] - first[:, :, 1] * second[:, :, 0]
    return jnp.stack([real_part, imag_part], axis=2)


def propagate(field, tables, direction):
    spectrum = fourier_field(field, tables, 1.0)
    kernel = jnp.stack([tables[4], tables[5] * direction])[None, None]
    return fourier_field(complex_product(spectrum, kernel), tables, -1.0)


def pattern_terms(probe_modes, patches, measured, live_mask, tables):
    slot_count = patches.shape[0]
    layers = patches.shape[1]
    wave = jnp.broadcast_to(probe_modes[None], (slot_count,) + probe_modes.shape)
    inputs = []
    for layer_index in range(layers):
        obj = patches[:, layer_index][:, None]
        inputs.append(wave)
        exit_wave = complex_product(wave, obj)
        if layer_index < layers - 1:
            wave = propagate(exit_wave, tables, 1.0)
        else:
            far = fourier_field(exit_wave, tables, 1.0)
    intensity = jnp.sum(far * far, axis=(1, 2))
    weight = (2.0 * (intensity - measured))[:, None, None]
    grad = fourier_field(weight * far, tables, -1.0)
    slice_grads = [None] * layers
    for layer_index in reversed(range(layers)):
        obj = patches[:, layer_index][:, None]
        slice_grads[layer_index] = jnp.sum(conj_product(inputs[layer_index], grad), axis=1)
        back = conj_product(obj, grad)
        if layer_index > 0:
            grad = propagate(back, tables, -1.0)
    weights = live_mask[:, None, None, None, None]
    object_grads = jnp.stack(slice_grads, axis=1) * weights
    probe_terms = jnp.sum(back * weights, axis=0)
    first = patches[:, 0]
    illumination = jnp.sum(jnp.sum(first * first, axis=1) * live_mask[:, None, None], axis=0)
    return (object_grads, probe_terms, illumination)


def fold_rims(padded, margin, offset, inner_rows, inner_cols):
    middle = padded[:, :, offset : offset + inner_rows, :]
    middle = middle.at[:, :, :margin, :].add(padded[:, :, :margin, :])
    middle = middle.at[:, :, inner_rows - margin :, :].add(
        padded[:, :, padded.shape[2] - margin :, :]
    )
    center = middle[:, :, :, offset : offset + inner_cols]
    center = center.at[:, :, :, :margin].add(middle[:, :, :, :margin])
    center = center.at[:, :, :, inner_cols - margin :].add(
        middle[:, :, :, middle.shape[3] - margin :]
    )
    return center


def fetch_bands(objects, margin):
    return extended_2(objects, (("row", 2), ("col", 3)), margin)


def return_rims(buffer, margin, tile_rows, tile_cols):
    padded = extended_2(buffer, (("row", 2), ("col", 3)), margin)
    return fold_rims(padded, margin, 2 * margin, tile_rows, tile_cols)


def local_pass(extended, probe_modes, measured, corners, live_mask, tables):
    layers = extended.shape[0]
    width = probe_modes.shape[-1]
    slot_count = corners.shape[0]

    def cut_patch(corner):
        start = (jnp.int32(0), jnp.int32(0), corner[0], corner[1])
        return lax.dynamic_slice(extended, start, (layers, 2, width, width))

    patches = jax.vmap(cut_patch)(corners)
    object_grads, probe_terms, illumination = pattern_terms(
        probe_modes, patches, measured, live_mask, tables
    )

    def place(slot_index, buffer):
        corner = corners[slot_index]
        start = (jnp.int32(0), jnp.int32(0), corner[0], corner[1])
        present = lax.dynamic_slice(buffer, start, (layers, 2, width, width))
        return lax.dynamic_update_slice(buffer, present + object_grads[slot_index], start)

    buffer = lax.fori_loop(0, slot_count, place, jnp.zeros(extended.shape, jnp.float32))
    probe_total, light_total = lax.psum((probe_terms, illumination), ("row", "col"))
    new_modes = probe_modes - 0.25 * probe_total / jnp.sqrt(light_total)
    return (buffer, new_modes)


def body(objects, probe_modes, intensities, positions, counts):
    width = probe_modes.shape[-1]
    margin = width // 2
    tile_rows = objects.shape[2]
    tile_cols = objects.shape[3]
    slot_count = intensities.shape[2]
    tables = fourier_tables(width)
    anchor = jnp.stack([lax.axis_index("row") * tile_rows, lax.axis_index("col") * tile_cols])
    corners = positions[0, 0] - anchor[None, :] + margin
    live_mask = (jnp.arange(slot_count, dtype=jnp.int32) < counts[0, 0]).astype(jnp.float32)
    measured = intensities[0, 0]
    for step_index in range(ITERS):
        extended = fetch_bands(objects, margin)
        buffer, probe_modes = local_pass(
            extended, probe_modes, measured, corners, live_mask, tables
        )
        objects = objects - 0.1 * return_rims(buffer, margin, tile_rows, tile_cols)
    return (objects, probe_modes)


def solution(mesh):
    return jax.shard_map(
        body,
        mesh=mesh,
        in_specs=(
            P(None, None, "row", "col"),
            P(),
            P("row", "col", None, None, None),
            P("row", "col", None, None),
            P("row", "col"),
        ),
        out_specs=(P(None, None, "row", "col"), P()),
        check_vma=False,
    )
```

profile of v0, /device:TPU:1, one launch (start us, length us, event | category | flops | bytes accessed | tf_op | source)
XLA Modules:
  0.0 826.7 jit_solution(8994471987461712167)
XLA Ops:
  7.2 1.8 fusion.62
  9.1 4.6 collective-permute-start
  13.6 5.5 collective-permute-start.1
  24.2 4.8 collective-permute-start.2
  29.0 1.3 collective-permute-start.3
  30.8 5.4 collective-permute-done.2
  36.2 4.9 collective-permute-done.3
  41.1 3.0 pad_maximum_fusion.2
  44.2 6.5 while.38
  44.8 2.5 bitcast_dynamic-update-slice_fusion.4
  47.9 2.5 bitcast_dynamic-update-slice_fusion.4
  62.7 1.6 convolution_bitcast_fusion.13
  66.9 15.6 %while.36 = (s32[]{:T(128)}, f32[2,2,256,384]{3,2,1,0:T(8,128)S(1)}, s32[2,2]{1,0:T(2,128)S(1)}, f32[2,2,2,128,128]{3,4,0,2,1:T(8,128)S(1)}, s32[]{:T(128)}, /*index=5*/s32[]{:T(128)}, s32[]{:T(128)}, s32[]{:T(128)}) while((s32[]{:T(128)}, f32[2,2,256,384]{3,2,1,0:T(8,128)S(1)}, s32[2,2]{1,0:T(2,128)S(1)}, ...), condition=%wide.region_4.5_spmd, body=%wide.region_3.4_spmd.sunk | while | flops 65544 | bytes 2359501 | solution.py:156
  71.5 3.3 dynamic_update_slice.16
  79.5 3.1 dynamic_update_slice.16
  83.5 6.7 collective-permute-start.4
  90.2 1.9 collective-permute-start.5
  92.7 2.6 collective-permute-done.4
  95.3 1.3 copy.150
  96.5 7.2 collective-permute-done.5
  103.8 1.3 copy.152
  105.0 1.2 pad_maximum_fusion.9
  106.3 3.9 collective-permute-start.6
  110.2 1.3 collective-permute-start.7
  111.5 2.0 copy.153
  113.6 1.7 collective-permute-done.6
  116.0 4.9 collective-permute-done.7
  120.9 2.9 pad_maximum_fusion
  126.0 5.3 scatter-add.26
  131.3 2.8 slice_add_fusion.2
  134.2 6.2 scatter-add.29
  144.5 6.9 collective-permute-start.8
  151.4 1.9 collective-permute-start.9
  153.3 4.5 collective-permute-done.8
  157.8 9.7 %collective-permute-done.9 = f32[2,2,64,256]{2,3,1,0:T(8,128)S(1)} collective-permute-done((f32[2,2,64,256]{2,3,1,0:T(8,128)S(1)}, f32[2,2,64,256]{2,3,1,0:T(8,128)S(1)}, u32[]{:S(2)}, u32[]{:S(2)}) %collective-permute-start.9) | collective-permute-done | bytes 262176 | tf_op jit(solution)/shard_map/ppermute | solution.py:22
  167.8 3.8 collective-permute-start.10
  171.6 1.3 collective-permute-start.11
  174.9 3.8 collective-permute-done.11
  178.7 1.5 pad_maximum_fusion.3
  180.3 4.5 while.39
  181.0 1.4 constant_dynamic-slice_fusion.20
  183.2 1.4 constant_dynamic-slice_fusion.20
  184.9 1.7 multiply_reduce_fusion.4
  187.5 293.5 %all-reduce.7.cloned.1.call-done = (f32[4,2,128,128]{2,3,0,1:T(8,128)}, f32[128,128]{1,0:T(8,128)}) async-done(((f32[4,2,128,128]{2,3,0,1:T(8,128)}, f32[128,128]{1,0:T(8,128)}), (f32[4,2,128,128]{2,3,0,1:T(8,128)}, f32[128,128]{1,0:T(8,128)})) %all-reduce.7.cloned.1.call-update) | async-done | bytes 589840 | tf_op jit(solution)/shard_map/psum | solution.py:157
  499.3 16.2 %while.37 = (s32[]{:T(128)}, f32[2,2,256,384]{3,2,1,0:T(8,128)S(1)}, s32[2,2]{1,0:T(2,128)S(1)}, f32[2,2,2,128,128]{3,4,0,2,1:T(8,128)S(1)}, s32[]{:T(128)}, /*index=5*/s32[]{:T(128)}, s32[]{:T(128)}, s32[]{:T(128)}) while((s32[]{:T(128)}, f32[2,2,256,384]{3,2,1,0:T(8,128)S(1)}, s32[2,2]{1,0:T(2,128)S(1)}, ...), condition=%wide.region_14.15_spmd, body=%wide.region_13.14_spmd.sunk | while | flops 65544 | bytes 2359501 | solution.py:156
  504.2 3.3 dynamic_update_slice.17
  512.4 3.1 dynamic_update_slice.17
  515.6 3.1 collective-permute-start.12
  518.6 2.1 collective-permute-start.13
  521.8 1.7 copy.183
  523.5 1.4 copy.182
  524.8 6.4 collective-permute-done.13
  531.2 2.2 copy.184
  533.4 2.2 pad_maximum_fusion.6
  535.6 2.1 collective-permute-start.14
  537.8 1.3 collective-permute-start.15
  539.1 258.6 %all-reduce.5.cloned.1.call-done = (f32[4,2,128,128]{2,3,0,1:T(8,128)}, f32[128,128]{1,0:T(8,128)}) async-done(((f32[4,2,128,128]{2,3,0,1:T(8,128)}, f32[128,128]{1,0:T(8,128)}), (f32[4,2,128,128]{2,3,0,1:T(8,128)}, f32[128,128]{1,0:T(8,128)})) %all-reduce.5.cloned.1.call-update) | async-done | bytes 589840 | tf_op jit(solution)/shard_map/psum | solution.py:157
  798.6 2.1 divide_subtract_fusion
  800.7 2.0 copy.188
  802.7 2.1 pad_maximum_fusion.1
  804.9 1.5 copy-done
  806.6 4.3 scatter-add.34
  810.8 1.8 slice_add_fusion
  812.7 5.8 scatter-add.35
  (225 shorter events, 58.5 us)
Async XLA Ops:
  7.2 13.6 %copy-start.20 = (f32[4,2,128,128]{3,2,1,0:T(8,128)S(1)}, f32[4,2,128,128]{3,2,1,0:T(8,128)}, u32[]{:S(2)}) copy-start(f32[4,2,128,128]{3,2,1,0:T(8,128)} %param.26) | copy-start | bytes 1572868
  7.2 473.8 %all-reduce.7.cloned.1.call-start = ((), (), s32[]{:S(2)}) async-start(), calls=%async_computation.1 | async-start | bytes 1179648 | tf_op jit(solution)/shard_map/psum | solution.py:157
  9.1 13.0 %collective-permute-start = (f32[2,2,64,256]{3,2,1,0:T(8,128)S(1)}, f32[2,2,64,256]{3,2,1,0:T(8,128)S(1)}, u32[]{:S(2)}, u32[]{:S(2)}) collective-permute-start(f32[2,2,64,256]{3,2,1,0:T(8,128)S(1)} %get-tuple-element.429), channel_id=1, source_target_pairs={{0,16},{16,32},{32,48},{48,64},{64,80},{80,96},{96,112},{112,128},... | collective-permute-start | bytes 786440 | tf_op jit(solution)/shard_map/ppermute | solution.py:21
  13.6 9.4 %collective-permute-start.1 = (f32[2,2,64,256]{3,2,1,0:T(8,128)}, f32[2,2,64,256]{3,2,1,0:T(8,128)S(1)}, u32[]{:S(2)}, u32[]{:S(2)}) collective-permute-start(f32[2,2,64,256]{3,2,1,0:T(8,128)} %get-tuple-element.428), channel_id=1, source_target_pairs={{16,0},{32,16},{48,32},{64,48},{80,64},{96,80},{112,96},{128,112},... | collective-permute-start | bytes 786440 | tf_op jit(solution)/shard_map/ppermute | solution.py:22
  20.9 1.3 copy-start.12
  21.3 41.4 %copy-start.5 = (f32[1,2,128,128]{3,2,1,0:T(8,128)}, f32[1,2,128,128]{3,2,1,0:T(8,128)S(1)}, u32[]{:S(2)}) copy-start(f32[1,2,128,128]{3,2,1,0:T(8,128)S(1)} %get-tuple-element.441) | copy-start | bytes 393220
  21.4 37.8 %copy-start.9 = (f32[2,2,128,128,1,1]{3,2,1,0,5,4:T(8,128)}, f32[2,2,128,128,1,1]{3,2,1,0,5,4:T(8,128)S(1)}, u32[]{:S(2)}) copy-start(f32[2,2,128,128,1,1]{3,2,1,0,5,4:T(8,128)S(1)} %get-tuple-element.451) | copy-start | bytes 786436
  21.4 40.1 %copy-start.3 = (f32[2,2,128,128,1,1]{3,2,1,0,5,4:T(8,128)}, f32[2,2,128,128,1,1]{3,2,1,0,5,4:T(8,128)S(1)}, u32[]{:S(2)}) copy-start(f32[2,2,128,128,1,1]{3,2,1,0,5,4:T(8,128)S(1)} %get-tuple-element.452) | copy-start | bytes 786436
  23.1 7.5 copy-start.34
  24.2 12.0 %collective-permute-start.2 = (f32[2,2,256,64]{3,2,1,0:T(8,128)}, f32[2,2,256,64]{3,2,1,0:T(8,128)}, u32[]{:S(2)}, u32[]{:S(2)}) collective-permute-start(f32[2,2,256,64]{3,2,1,0:T(8,128)} %get-tuple-element.408), channel_id=1, source_target_pairs={{0,1},{1,2},{2,3},{3,4},{4,5},{5,6},{6,7},{7,8},{8,9},{9,10},{10,1... | collective-permute-start | bytes 786440 | tf_op jit(solution)/shard_map/ppermute | solution.py:21
  29.0 12.1 %collective-permute-start.3 = (f32[2,2,256,64]{3,2,1,0:T(8,128)}, f32[2,2,256,64]{3,2,1,0:T(8,128)}, u32[]{:S(2)}, u32[]{:S(2)}) collective-permute-start(f32[2,2,256,64]{3,2,1,0:T(8,128)} %get-tuple-element.409), channel_id=1, source_target_pairs={{1,0},{2,1},{3,2},{4,3},{5,4},{6,5},{7,6},{8,7},{9,8},{10,9},{11,1... | collective-permute-start | bytes 786440 | tf_op jit(solution)/shard_map/ppermute | solution.py:22
  30.7 27.3 %copy-start.23 = (f32[1,1,2,128,128]{3,4,2,1,0:T(8,128)}, f32[1,1,2,128,128]{3,4,2,1,0:T(8,128)S(1)}, u32[]{:S(2)}) copy-start(f32[1,1,2,128,128]{3,4,2,1,0:T(8,128)S(1)} %copy.137) | copy-start | bytes 393220
  30.8 22.8 %copy-start.29 = (f32[128,128]{0,1:T(8,128)}, f32[128,128]{0,1:T(8,128)S(1)}, u32[]{:S(2)}) copy-start(f32[128,128]{0,1:T(8,128)S(1)} %get-tuple-element.453) | copy-start | bytes 196612
  30.8 22.8 %copy-start.31 = (f32[128,128]{0,1:T(8,128)}, f32[128,128]{0,1:T(8,128)S(1)}, u32[]{:S(2)}) copy-start(f32[128,128]{0,1:T(8,128)S(1)} %get-tuple-element.454) | copy-start | bytes 196612
  30.8 31.8 %copy-start.25 = (f32[128,128]{0,1:T(8,128)}, f32[128,128]{0,1:T(8,128)S(1)}, u32[]{:S(2)}) copy-start(f32[128,128]{0,1:T(8,128)S(1)} %get-tuple-element.430) | copy-start | bytes 196612
  30.8 31.8 %copy-start.27 = (f32[128,128]{0,1:T(8,128)}, f32[128,128]{0,1:T(8,128)S(1)}, u32[]{:S(2)}) copy-start(f32[128,128]{0,1:T(8,128)S(1)} %get-tuple-element.431) | copy-start | bytes 196612
  50.7 0.8 copy-start.13
  83.5 11.7 %collective-permute-start.4 = (f32[2,2,64,384]{3,2,1,0:T(8,128)}, f32[2,2,64,384]{3,2,1,0:T(8,128)}, u32[]{:S(2)}, u32[]{:S(2)}) collective-permute-start(f32[2,2,64,384]{3,2,1,0:T(8,128)} %get-tuple-element.376), channel_id=1, source_target_pairs={{0,16},{16,32},{32,48},{48,64},{64,80},{80,96},{96,112},{112,128},... | collective-permute-start | bytes 1179656 | tf_op jit(solution)/shard_map/ppermute | solution.py:21
  90.2 13.5 %collective-permute-start.5 = (f32[2,2,64,384]{3,2,1,0:T(8,128)}, f32[2,2,64,384]{3,2,1,0:T(8,128)}, u32[]{:S(2)}, u32[]{:S(2)}) collective-permute-start(f32[2,2,64,384]{3,2,1,0:T(8,128)} %get-tuple-element.377), channel_id=1, source_target_pairs={{16,0},{32,16},{48,32},{64,48},{80,64},{96,80},{112,96},{128,112},... | collective-permute-start | bytes 1179656 | tf_op jit(solution)/shard_map/ppermute | solution.py:22
  92.6 13.7 %copy-start.2 = (f32[2,2,256,384]{2,3,1,0:T(8,128)}, f32[2,2,256,384]{2,3,1,0:T(8,128)S(1)}, u32[]{:S(2)}) copy-start(f32[2,2,256,384]{2,3,1,0:T(8,128)S(1)} %copy.151) | copy-start | bytes 4718596
  96.5 9.8 %copy-start.7 = (f32[2,2,64,384]{2,3,1,0:T(8,128)}, f32[2,2,64,384]{2,3,1,0:T(8,128)S(1)}, u32[]{:S(2)}) copy-start(f32[2,2,64,384]{2,3,1,0:T(8,128)S(1)} %copy.150) | copy-start | bytes 1179652
  105.0 1.3 copy-start.8
  106.3 8.9 %collective-permute-start.6 = (f32[2,2,384,64]{2,3,1,0:T(8,128)}, f32[2,2,384,64]{2,3,1,0:T(8,128)S(1)}, u32[]{:S(2)}, u32[]{:S(2)}) collective-permute-start(f32[2,2,384,64]{2,3,1,0:T(8,128)} %get-tuple-element.364), channel_id=1, source_target_pairs={{0,1},{1,2},{2,3},{3,4},{4,5},{5,6},{6,7},{7,8},{8,9},{9,10},{10,1... | collective-permute-start | bytes 1179656 | tf_op jit(solution)/shard_map/ppermute | solution.py:21
  110.2 10.7 %collective-permute-start.7 = (f32[2,2,384,64]{2,3,1,0:T(8,128)}, f32[2,2,384,64]{2,3,1,0:T(8,128)}, u32[]{:S(2)}, u32[]{:S(2)}) collective-permute-start(f32[2,2,384,64]{2,3,1,0:T(8,128)} %get-tuple-element.365), channel_id=1, source_target_pairs={{1,0},{2,1},{3,2},{4,3},{5,4},{6,5},{7,6},{8,7},{9,8},{10,9},{11,1... | collective-permute-start | bytes 1179656 | tf_op jit(solution)/shard_map/ppermute | solution.py:22
  115.2 0.8 copy-start.33
  134.2 9.2 %copy-start.19 = (f32[2,2,128,256]{2,3,1,0:T(8,128)S(1)}, f32[2,2,128,256]{2,3,1,0:T(8,128)}, u32[]{:S(2)}) copy-start(f32[2,2,128,256]{2,3,1,0:T(8,128)} %copy.153) | copy-start | bytes 1572868
  144.5 28.5 %copy-start.15 = (f32[2,4,1,128,128]{3,4,2,1,0:T(8,128)S(1)}, f32[2,4,1,128,128]{3,4,2,1,0:T(8,128)}, u32[]{:S(2)}) copy-start(f32[2,4,1,128,128]{3,4,2,1,0:T(8,128)} %get-tuple-element.386) | copy-start | bytes 1572868
  144.5 28.5 %copy-start.16 = (f32[2,4,1,128,128]{3,4,2,1,0:T(8,128)S(1)}, f32[2,4,1,128,128]{3,4,2,1,0:T(8,128)}, u32[]{:S(2)}) copy-start(f32[2,4,1,128,128]{3,4,2,1,0:T(8,128)} %get-tuple-element.387) | copy-start | bytes 1572868
  144.5 13.4 %collective-permute-start.8 = (f32[2,2,64,256]{2,3,1,0:T(8,128)}, f32[2,2,64,256]{2,3,1,0:T(8,128)S(1)}, u32[]{:S(2)}, u32[]{:S(2)}) collective-permute-start(f32[2,2,64,256]{2,3,1,0:T(8,128)} %get-tuple-element.420), channel_id=1, source_target_pairs={{0,16},{16,32},{32,48},{48,64},{64,80},{80,96},{96,112},{112,128},... | collective-permute-start | bytes 786440 | tf_op jit(solution)/shard_map/ppermute | solution.py:21
  151.4 16.1 %collective-permute-start.9 = (f32[2,2,64,256]{2,3,1,0:T(8,128)S(1)}, f32[2,2,64,256]{2,3,1,0:T(8,128)S(1)}, u32[]{:S(2)}, u32[]{:S(2)}) collective-permute-start(f32[2,2,64,256]{2,3,1,0:T(8,128)S(1)} %get-tuple-element.421), channel_id=1, source_target_pairs={{16,0},{32,16},{48,32},{64,48},{80,64},{96,80},{112,96},{128,112},... | collective-permute-start | bytes 786440 | tf_op jit(solution)/shard_map/ppermute | solution.py:22
  167.5 5.6 copy-start.22
  167.8 6.1 copy-start.14
  167.8 7.1 collective-permute-start.10
  171.6 7.1 collective-permute-start.11
  184.8 2.0 copy-start.21
  186.6 611.0 %all-reduce.5.cloned.1.call-start = ((), (), s32[]{:S(2)}) async-start(), calls=%async_computation | async-start | bytes 1179648 | tf_op jit(solution)/shard_map/psum | solution.py:157
  483.0 1.2 copy-start.11
  483.2 1.0 copy-start.4
  484.3 1.1 copy-start.30
  484.3 1.1 copy-start.32
  485.4 0.9 copy-start.6
  485.6 1.8 copy-start.10
  489.6 1.1 copy-start.24
  494.2 1.1 copy-start.26
  494.2 1.1 copy-start.28
  515.5 5.3 copy-start.17
  515.5 5.3 copy-start.18
  515.6 7.9 collective-permute-start.12
  518.6 12.6 %collective-permute-start.13 = (f32[2,2,64,384]{3,2,1,0:T(8,128)S(1)}, f32[2,2,64,384]{3,2,1,0:T(8,128)}, u32[]{:S(2)}, u32[]{:S(2)}) collective-permute-start(f32[2,2,64,384]{3,2,1,0:T(8,128)S(1)} %get-tuple-element.371), channel_id=1, source_target_pairs={{16,0},{32,16},{48,32},{64,48},{80,64},{96,80},{112,96},{128,112},... | collective-permute-start | bytes 1179656 | tf_op jit(solution)/shard_map/ppermute | solution.py:22
  523.5 10.0 %copy-start.1 = (f32[2,2,256,384]{2,3,1,0:T(8,128)S(1)}, f32[2,2,256,384]{2,3,1,0:T(8,128)}, u32[]{:S(2)}) copy-start(f32[2,2,256,384]{2,3,1,0:T(8,128)} %copy.183) | copy-start | bytes 4718596
  535.6 267.1 %collective-permute-start.14 = (f32[2,2,384,64]{2,3,1,0:T(8,128)}, f32[2,2,384,64]{2,3,1,0:T(8,128)S(1)}, u32[]{:S(2)}, u32[]{:S(2)}) collective-permute-start(f32[2,2,384,64]{2,3,1,0:T(8,128)} %get-tuple-element.362), channel_id=1, source_target_pairs={{0,1},{1,2},{2,3},{3,4},{4,5},{5,6},{6,7},{7,8},{8,9},{9,10},{10,1... | collective-permute-start | bytes 1179656 | tf_op jit(solution)/shard_map/ppermute | solution.py:21
  537.8 264.9 %collective-permute-start.15 = (f32[2,2,384,64]{2,3,1,0:T(8,128)}, f32[2,2,384,64]{2,3,1,0:T(8,128)}, u32[]{:S(2)}, u32[]{:S(2)}) collective-permute-start(f32[2,2,384,64]{2,3,1,0:T(8,128)} %get-tuple-element.363), channel_id=1, source_target_pairs={{1,0},{2,1},{3,2},{4,3},{5,4},{6,5},{7,6},{8,7},{9,8},{10,9},{11,1... | collective-permute-start | bytes 1179656 | tf_op jit(solution)/shard_map/ppermute | solution.py:22
  804.8 1.6 copy-start
Sparse Core Ops, SparseCore 0:
  186.7 294.2 all-reduce.6
  521.9 275.6 all-reduce.4
where the time goes:
time: 831 us; the launch traced here: 827 us
  waiting for transfers between devices  604 us (73%)
  local copies, waits for them, and re-layouts  77.4 us (9%)
  starting transfers between devices  52.8 us (6%)
  other arithmetic  34.5 us (4%)
  matrix products  25.5 us (3%)
  between operations  16.3 us (2%)
  loops' own time  15.8 us (2%)
    psum x2, waiting for transfers between devices, local_pass(): lax.psum((probe_terms, illumination), ('row', 'col'))  552 us
    ppermute x8, waiting for transfers between devices, extended_2(): after = lax.ppermute(initial, axis, down)  37.9 us
    ppermute x8, starting transfers between devices, extended_2(): before = lax.ppermute(last, axis, up)  36 us
  transfers between devices with their start and end apart: 18, of which 14 were waited for; matrix products, arithmetic and copies ran while one was open for 3% of the time, Pallas kernels for 0%

commit v1 on v0

v1 whole, which is shorter than its diff:
```python
import math

import jax
import jax.numpy as jnp
import ml_dtypes
import numpy as np
from jax import lax
from jax.experimental import pallas as pl
from jax.experimental.pallas import tpu as pltpu
from jax.sharding import Mesh, PartitionSpec as P

ROW = ("x", "yl", "c")
COL = ("yh", "z")
XZ = ("x", "z")
Y = ("yh", "yl")

W = 128
H = 64
TR = 128
TC = 256
EC = 384
M = 4
WIN = W + 8
F = 8
f32 = jnp.float32
bf16 = jnp.bfloat16


def split_np(a):
    out = []
    for _ in range(3):
        part = a.astype(ml_dtypes.bfloat16)
        out.append(part)
        a = a - part.astype(np.float64)
    return out


def tables_np():
    n = np.arange(W)
    ang = -2.0 * math.pi * ((n[:, None] * n[None, :]) % W) / W
    t = np.exp(1j * ang) / math.sqrt(W)
    f = ((n + H) % W - H).astype(np.float64)
    k = np.exp(-4j * math.pi * f * f / (W * W))
    a = np.conj(t) @ (k[:, None] * t)
    out = []
    for m in (t, a):
        u = np.block([[m.real, -m.imag], [m.imag, m.real]])
        for v in (u, u.T):
            out.extend(split_np(v))
    return np.stack(out)


def lanes(shape):
    return lax.broadcasted_iota(jnp.int32, shape, len(shape) - 1)


def split(x, parts):
    out = []
    for i in range(parts):
        h = x.astype(bf16)
        out.append(h)
        if i < parts - 1:
            x = x - h.astype(f32)
    return out


PAIRS = {2: ((0, 0), (0, 1), (1, 0)), 3: ((0, 0), (0, 1), (1, 0), (0, 2), (1, 1), (2, 0))}


def cmul(ar, ai, br, bi):
    return ar * br - ai * bi, ar * bi + ai * br


def cmulc(ar, ai, br, bi):
    return ar * br + ai * bi, ar * bi - ai * br


def right(z, lhs, tab, i, parts):
    x = jnp.concatenate([lhs[:, p * 2 * W : (p + 1) * 2 * W] for p, _ in PAIRS[parts]], axis=1)
    w = jnp.concatenate([tab[i + t] for _, t in PAIRS[parts]], axis=0)
    y = jnp.dot(x, w, preferred_element_type=f32)
    z[0] = y[:, :W].reshape(F, W, W)
    z[1] = y[:, W:].reshape(F, W, W)


def put_lhs(lhs, f, xr, xi, parts):
    rows = slice(f * W, (f + 1) * W)
    for q, x in enumerate((xr, xi)):
        for p, v in enumerate(split(x, parts)):
            at = (2 * p + q) * W
            lhs[rows, at : at + W] = v


def left(z, tab, i, f, parts):
    v = [split(jnp.concatenate([z[q, f], z[q, f + 1]], axis=1), parts) for q in range(2)]
    v = [jnp.concatenate([v[0][p], v[1][p]], axis=0) for p in range(parts)]
    x = jnp.concatenate([v[p] for p, _ in PAIRS[parts]], axis=0)
    w = jnp.concatenate([tab[i + t] for _, t in PAIRS[parts]], axis=1)
    y = jnp.dot(w, x, preferred_element_type=f32)
    return (
        (y[:W, :W], y[W:, :W]),
        (y[:W, W:], y[W:, W:]),
    )


U, UT, B, BT = 0, 3, 6, 9


def window(r0, s):
    r8 = r0 // 8
    q = s // W
    q1 = jnp.where(q == 2, 0, q + 1)
    rows = pl.ds(pl.multiple_of(r8 * 8, 8), WIN)
    at = [(rows, pl.ds(pl.multiple_of(t * W, W), W)) for t in (q, q1)]
    return at, r0 - r8 * 8, s - q * W


def cut(e, r0, s, plane):
    at, dr, dc = window(r0, s)
    low = lanes((WIN, W)) >= dc
    v = jnp.where(low, e[(plane,) + at[0]], e[(plane,) + at[1]])
    v = pltpu.roll(v, jnp.where(dc == 0, 0, W - dc), 1)
    v = pltpu.roll(v, jnp.where(dr == 0, 0, WIN - dr), 0)
    return v[:W]


def place(g, r0, s, plane, val):
    at, dr, dc = window(r0, s)
    v = jnp.concatenate([val, jnp.zeros((WIN - W, W), f32)], axis=0)
    v = pltpu.roll(v, dr, 0)
    v = pltpu.roll(v, dc, 1)
    low = lanes((WIN, W)) >= dc
    i0 = (plane,) + at[0]
    i1 = (plane,) + at[1]
    g[i0] = g[i0] + jnp.where(low, v, 0.0)
    g[i1] = g[i1] + jnp.where(low, 0.0, v)


def iteration(info, e, p, meas, tab, g, acc, z, lhs, o, psi1, parts):
    origin, positions, counts = info
    rows = [jnp.clip(positions[0, 0, n, 0] - origin[0] + H, 0, TR - 1) for n in range(2)]
    cols = [jnp.clip(positions[0, 0, n, 1] - origin[1] + W, H, TC + H - 1) for n in range(2)]
    live = [(counts[0, 0] > n).astype(f32) for n in range(2)]
    for n in range(2):
        for k in range(4):
            o[n, k] = cut(e, rows[n], cols[n], k)
    wsum = None
    for n in range(2):
        t = (o[n, 0] * o[n, 0] + o[n, 1] * o[n, 1]) * live[n]
        wsum = t if wsum is None else wsum + t
    acc[8] = wsum
    for n in range(2):
        for m in range(M):
            xr, xi = cmul(p[2 * m], p[2 * m + 1], o[n, 0], o[n, 1])
            put_lhs(lhs, n * M + m, xr, xi, parts)
    right(z, lhs, tab, BT, parts)
    for f in range(0, F, 2):
        n = f // M
        for j, (yr, yi) in enumerate(left(z, tab, B, f, parts)):
            psi1[0, f + j] = yr
            psi1[1, f + j] = yi
            xr, xi = cmul(yr, yi, o[n, 2], o[n, 3])
            put_lhs(lhs, f + j, xr, xi, parts)
    right(z, lhs, tab, UT, parts)
    for n in range(2):
        tot = None
        for f in range(n * M, (n + 1) * M, 2):
            for j, (yr, yi) in enumerate(left(z, tab, U, f, parts)):
                z[0, f + j] = yr
                z[1, f + j] = yi
                t = yr * yr + yi * yi
                tot = t if tot is None else tot + t
        wt = 2.0 * (tot - meas[n])
        for f in range(n * M, (n + 1) * M):
            put_lhs(lhs, f, wt * z[0, f], wt * z[1, f], parts)
    right(z, lhs, tab, U, parts)
    for n in range(2):
        sr = si = None
        for f in range(n * M, (n + 1) * M, 2):
            for j, (yr, yi) in enumerate(left(z, tab, UT, f, parts)):
                tr, ti = cmulc(psi1[0, f + j], psi1[1, f + j], yr, yi)
                sr = tr if sr is None else sr + tr
                si = ti if si is None else si + ti
                br, bi = cmulc(o[n, 2], o[n, 3], yr, yi)
                put_lhs(lhs, f + j, br, bi, parts)
        place(g, rows[n], cols[n], 2, sr * live[n])
        place(g, rows[n], cols[n], 3, si * live[n])
    right(z, lhs, tab, B, parts)
    for n in range(2):
        sr = si = None
        for f in range(n * M, (n + 1) * M, 2):
            for j, (yr, yi) in enumerate(left(z, tab, BT, f, parts)):
                m = f + j - n * M
                tr, ti = cmulc(p[2 * m], p[2 * m + 1], yr, yi)
                sr = tr if sr is None else sr + tr
                si = ti if si is None else si + ti
                br, bi = cmulc(o[n, 0], o[n, 1], yr, yi)
                if n == 0:
                    acc[2 * m] = br * live[n]
                    acc[2 * m + 1] = bi * live[n]
                else:
                    acc[2 * m] = acc[2 * m] + br * live[n]
                    acc[2 * m + 1] = acc[2 * m + 1] + bi * live[n]
        place(g, rows[n], cols[n], 0, sr * live[n])
        place(g, rows[n], cols[n], 1, si * live[n])


def first_kernel(origin, positions, counts, c, top, bot, p, meas, tab, e, gup, gdn, acc, g, z, lhs, o, psi1):
    e[:, 0:H, :] = top[...]
    e[:, H : H + TR, :] = c[...]
    e[:, H + TR :, :] = bot[...]
    g[...] = jnp.zeros_like(g)
    iteration((origin, positions, counts), e, p, meas, tab, g, acc, z, lhs, o, psi1, 3)
    gup[...] = g[:, 0:TR, :]
    gdn[...] = g[:, TR:, :]


def new_modes(p, s, out):
    inv = 0.25 / jnp.sqrt(s[8])
    for k in range(8):
        out[k] = p[k] - s[k] * inv


def second_kernel(origin, positions, counts, e0, r, rl, rr, p0, s, meas, tab, oc, gc, gu, gd, acc, p, g, e, z, lhs, o, psi1):
    low = lanes((256, W)) < H
    for k in range(4):
        a = rl[k]
        b = rr[k]
        e[k, :, 0:W] = e0[k, :, 0:W] - 0.1 * (r[k, :, 0:W] + jnp.where(low, b, a))
        e[k, :, W : 2 * W] = e0[k, :, W : 2 * W] - 0.1 * (r[k, :, W : 2 * W] + jnp.where(low, a, 0.0))
        e[k, :, 2 * W :] = e0[k, :, 2 * W :] - 0.1 * (r[k, :, 2 * W :] + jnp.where(low, 0.0, b))
    new_modes(p0, s, p)
    g[...] = jnp.zeros_like(g)
    iteration((origin, positions, counts), e, p, meas, tab, g, acc, z, lhs, o, psi1, 2)
    oc[...] = e[:, H : H + TR, W:]
    gc[...] = g[:, H : H + TR, :]
    gu[...] = g[:, 0:H, :]
    gd[...] = g[:, H + TR :, :]


def pack(a, b, hi):
    low = lanes(a.shape) < H
    if hi:
        return jnp.where(low, pltpu.roll(a, H, 1), b)
    return jnp.where(low, a, pltpu.roll(b, H, 1))


def strips_kernel(x, ml, mr):
    for k in range(2):
        ml[k] = pack(x[k, 0, :, 0:W], x[k, 1, :, 0:W], False)
        mr[k] = pack(x[k, 0, :, W:], x[k, 1, :, W:], True)


def widen_kernel(x, rl, rr, c, top, bot):
    low = lanes((TR, W)) < H
    for k in range(2):
        a = rl[k]
        b = rr[k]
        c[2 * k, :, 0:W] = jnp.where(low, b, pltpu.roll(a, H, 1))
        c[2 * k + 1, :, 0:W] = jnp.where(low, pltpu.roll(b, H, 1), a)
        for j in range(2):
            c[2 * k + j, :, W:] = x[k, j]
    top[...] = c[:, 0:H, :]
    bot[...] = c[:, H:, :]


def halves_kernel(gup, gdn, above, below, r, ml, mr):
    low = lanes((TR, W)) < H
    for h, (a, b) in enumerate(((gup, above), (gdn, below))):
        rows = slice(h * TR, (h + 1) * TR)
        for k in range(4):
            v = [a[k, :, j * W : (j + 1) * W] + b[k, :, j * W : (j + 1) * W] for j in range(3)]
            for j in range(3):
                r[k, rows, j * W : (j + 1) * W] = v[j]
            ml[k, rows, :] = jnp.where(low, v[1], v[0])
            mr[k, rows, :] = jnp.where(low, v[0], v[2])


def fold_kernel(gc, above, below, t, ml, mr):
    for half, b in enumerate((above, below)):
        rows = slice(half * H, (half + 1) * H)
        for k in range(2):
            v0 = gc[2 * k, rows, 0:W] + b[2 * k, :, 0:W]
            v1 = gc[2 * k + 1, rows, 0:W] + b[2 * k + 1, :, 0:W]
            ml[k, rows, :] = pack(v0, v1, True)
            mr[k, rows, :] = pack(v0, v1, False)
            for j in range(2):
                t[2 * k + j, rows, :] = gc[2 * k + j, rows, W:] + b[2 * k + j, :, W:]


def last_kernel(oc, t, rl, rr, out):
    low = lanes((TR, W)) < H
    for k in range(2):
        a = rl[k]
        b = rr[k]
        add = (
            (jnp.where(low, a, 0.0), jnp.where(low, 0.0, pltpu.roll(b, H, 1))),
            (jnp.where(low, pltpu.roll(a, H, 1), 0.0), jnp.where(low, 0.0, b)),
        )
        for j in range(2):
            for h in range(2):
                cs = slice(h * W, (h + 1) * W)
                out[k, j, :, cs] = oc[2 * k + j, :, cs] - 0.1 * (t[2 * k + j, :, cs] + add[j][h])


VM = pl.BlockSpec(memory_space=pltpu.VMEM)
SM = pl.BlockSpec(memory_space=pltpu.SMEM)


def sds(*shape):
    return jax.ShapeDtypeStruct(shape, f32)


def call(kernel, outs, *args, smem=0, scratch=(), cost=None, limit=8):
    specs = [VM] * len(args)
    for i in range(smem):
        specs[i] = SM
    return pl.pallas_call(
        kernel,
        out_shape=outs,
        in_specs=specs,
        out_specs=[VM] * len(outs) if isinstance(outs, (list, tuple)) else VM,
        scratch_shapes=list(scratch),
        compiler_params=pltpu.CompilerParams(vmem_limit_bytes=limit * 1024 * 1024),
        cost_estimate=cost,
    )(*args)


def shift(value, axes, size, step):
    if step > 0:
        perm = [(i, i + 1) for i in range(size - 1)]
    else:
        perm = [(i + 1, i) for i in range(size - 1)]
    return lax.ppermute(value, axes, perm)


def scatter_sum(v, axes, n):
    v = lax.all_to_all(v.reshape(n, 1, -1), axes, 0, 0, tiled=True)
    return jnp.sum(v, axis=(0, 1))


def spread(v, axes, n):
    w = jnp.broadcast_to(v[None, None], (n, 1) + v.shape)
    return lax.all_to_all(w, axes, 0, 0, tiled=True)


ITER_COST = pl.CostEstimate(flops=10_000_000_000, bytes_accessed=8_000_000, transcendentals=0)


def body(objects, probe_modes, intensities, positions, counts):
    tab = jnp.asarray(tables_np())
    origin = jnp.stack([lax.axis_index(ROW) * TR, lax.axis_index(COL) * TC]).astype(jnp.int32)
    modes = probe_modes.reshape(8, W, W)
    measured = intensities[0, 0]
    scratch = [
        pltpu.VMEM((4, 256, EC), f32),
        pltpu.VMEM((2, F, W, W), f32),
        pltpu.VMEM((F * W, 6 * W), bf16),
        pltpu.VMEM((2, 4, W, W), f32),
        pltpu.VMEM((2, F, W, W), f32),
    ]

    ml, mr = call(strips_kernel, [sds(2, TR, W)] * 2, objects)
    right_in = shift(ml, COL, 16, -1)
    left_in = shift(mr, COL, 16, 1)
    c, top, bot = call(
        widen_kernel, [sds(4, TR, EC), sds(4, H, EC), sds(4, H, EC)], objects, left_in, right_in
    )
    below = shift(top, ROW, 32, -1)
    above = shift(bot, ROW, 32, 1)
    e, gup, gdn, acc = call(
        first_kernel,
        [sds(4, 256, EC), sds(4, TR, EC), sds(4, TR, EC), sds(9, W, W)],
        origin, positions, counts, c, above, below, modes, measured, tab,
        smem=3, scratch=scratch, cost=ITER_COST, limit=24,
    )

    below = shift(gup, ROW, 32, -1)
    above = shift(gdn, ROW, 32, 1)
    v = scatter_sum(acc.reshape(-1), "c", 2)
    v = scatter_sum(v, XZ, 32)
    r, ml, mr = call(
        halves_kernel, [sds(4, 256, EC), sds(4, 256, W), sds(4, 256, W)], gup, gdn, above, below
    )
    v, ml, mr = lax.optimization_barrier((v, ml, mr))
    right_in = shift(ml, COL, 16, -1)
    left_in = shift(mr, COL, 16, 1)
    v = jnp.sum(spread(v, Y, 8), axis=(0, 1))
    v = spread(v, XZ, 32).reshape(-1)
    total = spread(v, "c", 2).reshape(9, W, W)
    oc, gc, gu, gd, acc, modes = call(
        second_kernel,
        [sds(4, TR, TC), sds(4, TR, EC), sds(4, H, EC), sds(4, H, EC), sds(9, W, W), sds(8, W, W)],
        origin, positions, counts, e, r, left_in, right_in, modes, total, measured, tab,
        smem=3, scratch=scratch[:1] + scratch, cost=ITER_COST, limit=24,
    )

    below = shift(gu, ROW, 32, -1)
    above = shift(gd, ROW, 32, 1)
    v = scatter_sum(acc.reshape(-1), "c", 2)
    v = scatter_sum(v, XZ, 32)
    t, ml, mr = call(
        fold_kernel, [sds(4, TR, TC), sds(2, TR, W), sds(2, TR, W)], gc, above, below
    )
    v, ml, mr = lax.optimization_barrier((v, ml, mr))
    right_in = shift(ml, COL, 16, -1)
    left_in = shift(mr, COL, 16, 1)
    v = jnp.sum(spread(v, Y, 8), axis=(0, 1))
    v = spread(v, XZ, 32).reshape(-1)
    total = spread(v, "c", 2).reshape(9, W, W)
    refined = call(last_kernel, sds(2, 2, TR, TC), oc, t, left_in, right_in)
    modes = modes - 0.25 * total[:8] / jnp.sqrt(total[8])[None]
    return refined, modes.reshape(M, 2, W, W)


def solution(mesh):
    fine = Mesh(mesh.devices.reshape(4, 4, 2, 2, 8), ("x", "yl", "c", "yh", "z"))
    return jax.shard_map(
        body,
        mesh=fine,
        in_specs=(
            P(None, None, ROW, COL),
            P(),
            P(ROW, COL, None, None, None),
            P(ROW, COL, None, None),
            P(ROW, COL),
        ),
        out_specs=(P(None, None, ROW, COL), P()),
        check_vma=False,
    )
```

time: 831 us -> 236 us (0.28)
  waiting for transfers between devices: 604 us -> 34.2 us
  blocking collectives: 0 us -> 67.1 us
  local copies, waits for them, and re-layouts: 77.4 us -> 20.7 us
  starting transfers between devices: 52.8 us -> 81.3 us
  other arithmetic: 34.5 us -> 6.16 us
  matrix products: 25.5 us -> 0 us
  Pallas kernels: 0 us -> 24.1 us
  loops' own time: 15.8 us -> 0 us
  between operations: 16.3 us -> 1.6 us
    psum x2 -> x0, waiting for transfers between devices: 552 us -> none  [local_pass(): lax.psum((probe_terms, illumination), ('row', 'col'))]
    all_to_all x0 -> x6, blocking collectives: none -> 67.1 us  [the longest x3 38.2 us: scatter_sum(): v = lax.all_to_all(v.reshape(n, 1, -1), axes, 0, 0, tiled=True)]
    all_to_all x0 -> x4, starting transfers between devices: none -> 37.1 us  [the longest x3 27.1 us: spread(): return lax.all_to_all(w, axes, 0, 0, tiled=True)]
    dot_general x24 -> x0, matrix products: 25.5 us -> none  [the longest x12 13 us: fourier_field(): jnp.einsum('pqab,kmqbc->kmpac', left_table, field, precision=highest)]
    ppermute x16 -> x12, waiting for transfers between devices: 52.4 us -> 28.2 us  [shift(): return lax.ppermute(value, axes, perm)]
    pallas_call x0 -> x7, Pallas kernels: none -> 24.1 us  [call(): pl.pallas_call(kernel, out_shape=outs, in_specs=specs, out_specs=[VM] * l...]
    scatter-add x4 -> x0, local copies, waits for them, and re-layouts: 21.6 us -> none  [the longest x2 12 us: fold_rims(): middle.at[:, :, inner_rows - margin:, :]]
    another operation x4 -> x0, loops' own time: 15.8 us -> none  [the longest x2 15.3 us: local_pass(): lax.fori_loop(0, slot_count, place, jnp.zeros(extended.shape, jnp.float32))]
  transfers between devices with their start and end apart: 18 -> 16, of which waited for: 14 -> 10; matrix products, arithmetic and copies ran while one was open for 3% -> 2% of each run, Pallas kernels for 0% -> 0%
where the time goes in v1:
time: 236 us; the launch traced here: 235 us
  starting transfers between devices  81.3 us (34%)
  blocking collectives  67.1 us (28%)
  waiting for transfers between devices  34.2 us (14%)
  Pallas kernels  24.1 us (10%)
  local copies, waits for them, and re-layouts  20.7 us (9%)
  other arithmetic  6.16 us (3%)
    ppermute x12, starting transfers between devices, shift(): return lax.ppermute(value, axes, perm)  44.2 us
    all_to_all x3, blocking collectives, scatter_sum(): v = lax.all_to_all(v.reshape(n, 1, -1), axes, 0, 0, tiled=True)  38.2 us
    all_to_all x3, blocking collectives, spread(): return lax.all_to_all(w, axes, 0, 0, tiled=True)  28.8 us
    ppermute x12, waiting for transfers between devices, shift(): return lax.ppermute(value, axes, perm)  28.2 us
    all_to_all x3, starting transfers between devices, spread(): return lax.all_to_all(w, axes, 0, 0, tiled=True)  27.1 us
    pallas_call x7, Pallas kernels, call(): pl.pallas_call(kernel, out_shape=outs, in_specs=specs, out_specs=[VM] * l...  24.1 us
    unnamed x42, local copies, waits for them, and re-layouts  17.4 us
    all_to_all x1, starting transfers between devices, scatter_sum(): v = lax.all_to_all(v.reshape(n, 1, -1), axes, 0, 0, tiled=True)  10.1 us
  transfers between devices with their start and end apart: 16, of which 10 were waited for; matrix products, arithmetic and copies ran while one was open for 2% of the time, Pallas kernels for 0%

profile of v1, /device:TPU:1, one launch (start us, length us, event | category | flops | bytes accessed | tf_op | source)
XLA Modules:
  0.0 235.1 jit_solution(1985816901465704018)
XLA Ops:
  0.6 1.0 copy-done
  1.8 4.8 %collective-permute-start = (f32[2,128,128]{2,1,0:T(8,128)S(1)}, f32[2,128,128]{2,1,0:T(8,128)S(1)}, u32[]{:S(2)}, u32[]{:S(2)}) collective-permute-start(f32[2,128,128]{2,1,0:T(8,128)S(1)} %get-tuple-element.29), channel_id=1, source_target_pairs={{0,1},{1,2},{2,3},{3,4},{4,5},{5,6},{6,7},{7,8},{8,9},{9,10},{10,1... | collective-permute-start | bytes 393224 | tf_op jit(solution)/shard_map/ppermute | solution.py:334
  6.7 1.3 collective-permute-start.1
  8.0 0.6 collective-permute-done.rl
  8.6 4.4 %collective-permute-done.1.rr = f32[2,128,128]{2,1,0:T(8,128)S(1)} collective-permute-done((f32[2,128,128]{2,1,0:T(8,128)S(1)}, f32[2,128,128]{2,1,0:T(8,128)S(1)}, u32[]{:S(2)}, u32[]{:S(2)}) %collective-permute-start.1) | collective-permute-done | bytes 131104 | tf_op jit(solution)/shard_map/ppermute | solution.py:334
  13.0 0.1 shard_map.78
  13.1 5.2 %collective-permute-start.2 = (f32[4,64,384]{2,1,0:T(8,128)S(1)}, f32[4,64,384]{2,1,0:T(8,128)S(1)}, u32[]{:S(2)}, u32[]{:S(2)}) collective-permute-start(f32[4,64,384]{2,1,0:T(8,128)S(1)} %get-tuple-element.32), channel_id=1, source_target_pairs={{0,16},{16,32},{32,48},{48,64},{64,80},{80,96},{96,112},{112,128},... | collective-permute-start | bytes 1179656 | tf_op jit(solution)/shard_map/ppermute | solution.py:334
  18.3 1.9 collective-permute-start.3
  21.0 2.1 collective-permute-done.2.top
  23.1 7.3 %collective-permute-done.3.bot = f32[4,64,384]{2,1,0:T(8,128)S(1)} collective-permute-done((f32[4,64,384]{2,1,0:T(8,128)S(1)}, f32[4,64,384]{2,1,0:T(8,128)S(1)}, u32[]{:S(2)}, u32[]{:S(2)}) %collective-permute-start.3) | collective-permute-done | bytes 393248 | tf_op jit(solution)/shard_map/ppermute | solution.py:334
  30.5 1.0 copy-done.3
  31.5 0.9 copy-done.13
  32.4 0.7 copy-done.15
  33.1 1.4 copy-done.17
  34.5 14.4 %shard_map.79 = (f32[4,256,384]{2,1,0:T(8,128)S(1)}, f32[4,128,384]{2,1,0:T(8,128)S(1)}, f32[4,128,384]{2,1,0:T(8,128)S(1)}, f32[9,128,128]{2,1,0:T(8,128)S(1)}) custom-call(s32[2]{0:T(128)S(1)} %pad_add_fusion.origin, s32[1,1,2,2]{3,2,1,0:T(2,128)S(1)} %copy-done.15, s32[1,1]{1,0:T(1,128)S(6)} %copy.22.counts, f32[4,128,384]{2,1,0:T(8,128)S(1)} %get-tuple-element.31.c, ...), custom_call_target="tpu_custom_call" | custom-call | flops 10000000000 | bytes 8000000 | tf_op jit(solution)/shard_map/pallas_call | solution.py:318
  49.0 1.2 copy-done.19
  50.1 1.9 collective-permute-start.5
  52.1 3.6 %collective-permute-start.4 = (f32[4,128,384]{2,1,0:T(8,128)S(1)}, f32[4,128,384]{2,1,0:T(8,128)S(1)}, u32[]{:S(2)}, u32[]{:S(2)}) collective-permute-start(f32[4,128,384]{2,1,0:T(8,128)S(1)} %get-tuple-element.36.gdn), channel_id=1, source_target_pairs={{0,16},{16,32},{32,48},{48,64},{64,80},{80,96},{96,112},{112,128},... | collective-permute-start | bytes 2359304 | tf_op jit(solution)/shard_map/ppermute | solution.py:334
  55.7 4.6 %all_to_all.50 = f32[2,1,73728]{2,1,0:T(1,128)} all-to-all(f32[2,1,73728]{2,1,0:T(1,128)S(1)} %bitcast.16), channel_id=1, replica_groups=mesh['x'=4,'yl'=4,'c'=2,'yh'=2,'z'=8] {'c'}, dimensions={0} | all-to-all | bytes 1179648 | tf_op jit(solution)/shard_map/all_to_all | solution.py:338
  60.3 1.9 reduce_sum.54
  62.3 29.3 %all_to_all.51 = f32[32,1,2304]{2,1,0:T(1,128)} all-to-all(f32[32,1,2304]{2,1,0:T(1,128)S(1)} %bitcast.27), channel_id=1, replica_groups=mesh['x'=4,'yl'=4,'c'=2,'yh'=2,'z'=8] {'x','z'}, dimensions={0} | all-to-all | bytes 589824 | tf_op jit(solution)/shard_map/all_to_all | solution.py:338
  91.5 1.1 reduce_sum.55
  92.7 0.2 shard_map.80
  92.9 1.1 copy-done.1
  94.0 0.8 copy-done.5
  94.8 0.8 copy-done.6
  95.7 12.3 %all_to_all.52 = f32[8,1,2304]{2,1,0:T(1,128)S(1)} all-to-all(f32[8,1,2304]{2,1,0:T(1,128)S(1)} %broadcast_in_dim.16), channel_id=1, replica_groups=mesh['x'=4,'yl'=4,'c'=2,'yh'=2,'z'=8] {'yh','yl'}, dimensions={0} | all-to-all | bytes 147456 | tf_op jit(solution)/shard_map/all_to_all | solution.py:344
  108.0 0.9 broadcast_in_dim.17
  108.9 7.1 %all-to-all-start.3 = ((f32[32,1,2304]{2,1,0:T(1,128)}), f32[32,1,2304]{2,1,0:T(1,128)S(1)}, u32[]{:S(2)}, u32[]{:S(2)}) async-start(f32[32,1,2304]{2,1,0:T(1,128)} %broadcast_in_dim.17), calls=%async_computation.3 | async-start | bytes 589824 | tf_op jit(solution)/shard_map/all_to_all | solution.py:344
  116.0 3.2 %collective-permute-start.6 = (f32[4,256,128]{2,1,0:T(8,128)}, f32[4,256,128]{2,1,0:T(8,128)S(1)}, u32[]{:S(2)}, u32[]{:S(2)}) collective-permute-start(f32[4,256,128]{2,1,0:T(8,128)} %copy-done.6), channel_id=1, source_target_pairs={{0,1},{1,2},{2,3},{3,4},{4,5},{5,6},{6,7},{7,8},{8,9},{9,10},{10,1... | collective-permute-start | bytes 1572872 | tf_op jit(solution)/shard_map/ppermute | solution.py:334
  119.2 1.3 collective-permute-start.7
  120.5 5.3 %all-to-all-done.3 = f32[32,1,2304]{2,1,0:T(1,128)S(1)} async-done(((f32[32,1,2304]{2,1,0:T(1,128)}), f32[32,1,2304]{2,1,0:T(1,128)S(1)}, u32[]{:S(2)}, u32[]{:S(2)}) %all-to-all-start.3) | async-done | bytes 294944 | tf_op jit(solution)/shard_map/all_to_all | solution.py:344
  125.8 1.1 broadcast_in_dim.19
  126.9 9.6 %all-to-all-start.4 = ((f32[2,1,73728]{2,1,0:T(1,128)}), f32[2,1,73728]{2,1,0:T(1,128)S(1)}, u32[]{:S(2)}, u32[]{:S(2)}) async-start(f32[2,1,73728]{2,1,0:T(1,128)} %broadcast_in_dim.19), calls=%async_computation.4 | async-start | bytes 1179648 | tf_op jit(solution)/shard_map/all_to_all | solution.py:344
  136.5 0.8 copy-done.7
  137.3 0.6 all-to-all-done.4
  137.9 1.4 copy-done.2
  139.3 1.0 copy-done.8
  140.4 0.9 copy-done.14
  141.3 1.4 copy-done.18
  142.7 1.4 copy-done.20
  144.1 8.1 %shard_map.81 = (f32[4,128,256]{2,1,0:T(8,128)S(1)}, f32[4,128,384]{2,1,0:T(8,128)S(1)}, f32[4,64,384]{2,1,0:T(8,128)S(1)}, f32[4,64,384]{2,1,0:T(8,128)S(1)}, f...) custom-call(s32[2]{0:T(128)S(1)} %pad_add_fusion.origin, s32[1,1,2,2]{3,2,1,0:T(2,128)S(1)} %copy-done.16, ...), custom_call_target="tpu_custom_call" | custom-call | flops 10000000000 | bytes 8000000 | tf_op jit(solution)/shard_map/pallas_call | solution.py:318
  152.2 0.7 copy-done.9
  153.0 0.7 copy-done.11
  153.7 4.3 %all_to_all.53 = f32[2,1,73728]{2,1,0:T(1,128)S(1)} all-to-all(f32[2,1,73728]{2,1,0:T(1,128)S(1)} %bitcast.17), channel_id=1, replica_groups=mesh['x'=4,'yl'=4,'c'=2,'yh'=2,'z'=8] {'c'}, dimensions={0} | all-to-all | bytes 1179648 | tf_op jit(solution)/shard_map/all_to_all | solution.py:338
  158.1 1.8 reduce_sum.57
  159.9 10.1 %all-to-all-start.6 = ((f32[32,1,2304]{2,1,0:T(1,128)}), f32[32,1,2304]{2,1,0:T(1,128)S(1)}, u32[]{:S(2)}, u32[]{:S(2)}) async-start(f32[32,1,2304]{2,1,0:T(1,128)} %bitcast.25), calls=%async_computation.6 | async-start | bytes 589824 | tf_op jit(solution)/shard_map/all_to_all | solution.py:338
  170.0 14.6 %collective-permute-start.8 = (f32[4,64,384]{2,1,0:T(8,128)S(1)}, f32[4,64,384]{2,1,0:T(8,128)S(1)}, u32[]{:S(2)}, u32[]{:S(2)}) collective-permute-start(f32[4,64,384]{2,1,0:T(8,128)S(1)} %copy-done.12), channel_id=1, source_target_pairs={{0,16},{16,32},{32,48},{48,64},{64,80},{80,96},{96,112},{112,128},... | collective-permute-start | bytes 1179656 | tf_op jit(solution)/shard_map/ppermute | solution.py:334
  184.5 1.9 collective-permute-start.9
  186.5 2.8 %collective-permute-done.8.above = f32[4,64,384]{2,1,0:T(8,128)S(1)} collective-permute-done((f32[4,64,384]{2,1,0:T(8,128)S(1)}, f32[4,64,384]{2,1,0:T(8,128)S(1)}, u32[]{:S(2)}, u32[]{:S(2)}) %collective-permute-start.8) | collective-permute-done | bytes 393248 | tf_op jit(solution)/shard_map/ppermute | solution.py:334
  189.2 4.4 %collective-permute-done.9.below = f32[4,64,384]{2,1,0:T(8,128)S(1)} collective-permute-done((f32[4,64,384]{2,1,0:T(8,128)S(1)}, f32[4,64,384]{2,1,0:T(8,128)S(1)}, u32[]{:S(2)}, u32[]{:S(2)}) %collective-permute-start.9) | collective-permute-done | bytes 393248 | tf_op jit(solution)/shard_map/ppermute | solution.py:334
  193.6 0.2 shard_map.82
  193.8 0.2 reduce_sum.58
  194.0 9.8 %all_to_all.54 = f32[8,1,2304]{2,1,0:T(1,128)S(1)} all-to-all(f32[8,1,2304]{2,1,0:T(1,128)S(1)} %broadcast_in_dim.20), channel_id=1, replica_groups=mesh['x'=4,'yl'=4,'c'=2,'yh'=2,'z'=8] {'yh','yl'}, dimensions={0} | all-to-all | bytes 147456 | tf_op jit(solution)/shard_map/all_to_all | solution.py:344
  203.9 0.9 broadcast_in_dim.21
  204.8 10.4 %all-to-all-start.8 = ((f32[32,1,2304]{2,1,0:T(1,128)}), f32[32,1,2304]{2,1,0:T(1,128)S(1)}, u32[]{:S(2)}, u32[]{:S(2)}) async-start(f32[32,1,2304]{2,1,0:T(1,128)} %broadcast_in_dim.21), calls=%async_computation.8 | async-start | bytes 589824 | tf_op jit(solution)/shard_map/all_to_all | solution.py:344
  215.2 3.1 %collective-permute-start.10 = (f32[2,128,128]{2,1,0:T(8,128)S(1)}, f32[2,128,128]{2,1,0:T(8,128)S(1)}, u32[]{:S(2)}, u32[]{:S(2)}) collective-permute-start(f32[2,128,128]{2,1,0:T(8,128)S(1)} %get-tuple-element.52), channel_id=1, source_target_pairs={{0,1},{1,2},{2,3},{3,4},{4,5},{5,6},{6,7},{7,8},{8,9},{9,10},{10,1... | collective-permute-start | bytes 393224 | tf_op jit(solution)/shard_map/ppermute | solution.py:334
  218.3 1.3 collective-permute-start.11
  219.6 4.3 %collective-permute-done.10.rl = f32[2,128,128]{2,1,0:T(8,128)S(1)} collective-permute-done((f32[2,128,128]{2,1,0:T(8,128)S(1)}, f32[2,128,128]{2,1,0:T(8,128)S(1)}, u32[]{:S(2)}, u32[]{:S(2)}) %collective-permute-start.10) | collective-permute-done | bytes 131104 | tf_op jit(solution)/shard_map/ppermute | solution.py:334
  223.9 2.2 collective-permute-done.11.rr
  226.2 0.9 shard_map.83
  227.1 0.3 broadcast_in_dim.46
  227.4 6.8 %all_to_all.55 = f32[2,1,73728]{2,1,0:T(1,128)S(1)} all-to-all(f32[2,1,73728]{2,1,0:T(1,128)S(1)} %broadcast_in_dim.46), channel_id=1, replica_groups=mesh['x'=4,'yl'=4,'c'=2,'yh'=2,'z'=8] {'c'}, dimensions={0} | all-to-all | bytes 1179648 | tf_op jit(solution)/shard_map/all_to_all | solution.py:344
  234.2 0.9 fusion.1
  (38 shorter events, 0.5 us)
Async XLA Ops:
  0.6 1.0 copy-start
  1.8 6.8 %collective-permute-start = (f32[2,128,128]{2,1,0:T(8,128)S(1)}, f32[2,128,128]{2,1,0:T(8,128)S(1)}, u32[]{:S(2)}, u32[]{:S(2)}) collective-permute-start(f32[2,128,128]{2,1,0:T(8,128)S(1)} %get-tuple-element.29), channel_id=1, source_target_pairs={{0,1},{1,2},{2,3},{3,4},{4,5},{5,6},{6,7},{7,8},{8,9},{9,10},{10,1... | collective-permute-start | bytes 393224 | tf_op jit(solution)/shard_map/ppermute | solution.py:334
  6.7 6.3 %collective-permute-start.1 = (f32[2,128,128]{2,1,0:T(8,128)S(1)}, f32[2,128,128]{2,1,0:T(8,128)S(1)}, u32[]{:S(2)}, u32[]{:S(2)}) collective-permute-start(f32[2,128,128]{2,1,0:T(8,128)S(1)} %get-tuple-element.30), channel_id=1, source_target_pairs={{1,0},{2,1},{3,2},{4,3},{5,4},{6,5},{7,6},{8,7},{9,8},{10,9},{11,1... | collective-permute-start | bytes 393224 | tf_op jit(solution)/shard_map/ppermute | solution.py:334
  13.1 10.0 %collective-permute-start.2 = (f32[4,64,384]{2,1,0:T(8,128)S(1)}, f32[4,64,384]{2,1,0:T(8,128)S(1)}, u32[]{:S(2)}, u32[]{:S(2)}) collective-permute-start(f32[4,64,384]{2,1,0:T(8,128)S(1)} %get-tuple-element.32), channel_id=1, source_target_pairs={{0,16},{16,32},{32,48},{48,64},{64,80},{80,96},{96,112},{112,128},... | collective-permute-start | bytes 1179656 | tf_op jit(solution)/shard_map/ppermute | solution.py:334
  18.3 12.1 %collective-permute-start.3 = (f32[4,64,384]{2,1,0:T(8,128)S(1)}, f32[4,64,384]{2,1,0:T(8,128)S(1)}, u32[]{:S(2)}, u32[]{:S(2)}) collective-permute-start(f32[4,64,384]{2,1,0:T(8,128)S(1)} %get-tuple-element.33), channel_id=1, source_target_pairs={{16,0},{32,16},{48,32},{64,48},{80,64},{96,80},{112,96},{128,112},... | collective-permute-start | bytes 1179656 | tf_op jit(solution)/shard_map/ppermute | solution.py:334
  30.5 1.0 copy-start.3
  31.5 0.9 copy-start.13
  32.4 0.7 copy-start.15
  33.1 1.4 copy-start.17
  49.0 1.2 copy-start.19
  50.1 42.5 %collective-permute-start.5 = (f32[4,128,384]{2,1,0:T(8,128)S(1)}, f32[4,128,384]{2,1,0:T(8,128)S(1)}, u32[]{:S(2)}, u32[]{:S(2)}) collective-permute-start(f32[4,128,384]{2,1,0:T(8,128)S(1)} %get-tuple-element.35.gup), channel_id=1, source_target_pairs={{16,0},{32,16},{48,32},{64,48},{80,64},{96,80},{112,96},{128,112},... | collective-permute-start | bytes 2359304 | tf_op jit(solution)/shard_map/ppermute | solution.py:334
  52.1 40.6 %collective-permute-start.4 = (f32[4,128,384]{2,1,0:T(8,128)S(1)}, f32[4,128,384]{2,1,0:T(8,128)S(1)}, u32[]{:S(2)}, u32[]{:S(2)}) collective-permute-start(f32[4,128,384]{2,1,0:T(8,128)S(1)} %get-tuple-element.36.gdn), channel_id=1, source_target_pairs={{0,16},{16,32},{32,48},{48,64},{64,80},{80,96},{96,112},{112,128},... | collective-permute-start | bytes 2359304 | tf_op jit(solution)/shard_map/ppermute | solution.py:334
  92.9 1.1 copy-start.1
  94.0 0.8 copy-start.5
  94.8 0.8 copy-start.6
  95.7 42.2 %copy-start.4 = (f32[4,2,128,128]{3,2,1,0:T(8,128)S(1)}, f32[4,2,128,128]{3,2,1,0:T(8,128)}, u32[]{:S(2)}) copy-start(f32[4,2,128,128]{3,2,1,0:T(8,128)} %param.7) | copy-start | bytes 1572868
  95.7 42.2 %copy-start.16 = (s32[1,1,2,2]{3,2,1,0:T(2,128)S(1)}, s32[1,1,2,2]{3,2,1,0:T(2,128)}, u32[]{:S(2)}) copy-start(s32[1,1,2,2]{3,2,1,0:T(2,128)} %positions.3) | copy-start | bytes 52
  108.9 16.9 %all-to-all-start.3 = ((f32[32,1,2304]{2,1,0:T(1,128)}), f32[32,1,2304]{2,1,0:T(1,128)S(1)}, u32[]{:S(2)}, u32[]{:S(2)}) async-start(f32[32,1,2304]{2,1,0:T(1,128)} %broadcast_in_dim.17), calls=%async_computation.3 | async-start | bytes 589824 | tf_op jit(solution)/shard_map/all_to_all | solution.py:344
  116.0 20.5 %collective-permute-start.6 = (f32[4,256,128]{2,1,0:T(8,128)}, f32[4,256,128]{2,1,0:T(8,128)S(1)}, u32[]{:S(2)}, u32[]{:S(2)}) collective-permute-start(f32[4,256,128]{2,1,0:T(8,128)} %copy-done.6), channel_id=1, source_target_pairs={{0,1},{1,2},{2,3},{3,4},{4,5},{5,6},{6,7},{7,8},{8,9},{9,10},{10,1... | collective-permute-start | bytes 1572872 | tf_op jit(solution)/shard_map/ppermute | solution.py:334
  119.2 17.3 %collective-permute-start.7 = (f32[4,256,128]{2,1,0:T(8,128)}, f32[4,256,128]{2,1,0:T(8,128)S(1)}, u32[]{:S(2)}, u32[]{:S(2)}) collective-permute-start(f32[4,256,128]{2,1,0:T(8,128)} %copy-done.5), channel_id=1, source_target_pairs={{1,0},{2,1},{3,2},{4,3},{5,4},{6,5},{7,6},{8,7},{9,8},{10,9},{11,1... | collective-permute-start | bytes 1572872 | tf_op jit(solution)/shard_map/ppermute | solution.py:334
  126.9 11.0 %all-to-all-start.4 = ((f32[2,1,73728]{2,1,0:T(1,128)}), f32[2,1,73728]{2,1,0:T(1,128)S(1)}, u32[]{:S(2)}, u32[]{:S(2)}) async-start(f32[2,1,73728]{2,1,0:T(1,128)} %broadcast_in_dim.19), calls=%async_computation.4 | async-start | bytes 1179648 | tf_op jit(solution)/shard_map/all_to_all | solution.py:344
  136.5 0.8 copy-start.7
  137.9 1.4 copy-start.2
  139.3 1.0 copy-start.8
  140.4 0.9 copy-start.14
  141.3 1.4 copy-start.18
  142.7 1.4 copy-start.20
  152.2 0.7 copy-start.9
  153.0 0.7 copy-start.11
  153.7 16.2 %copy-start.12 = (f32[4,64,384]{2,1,0:T(8,128)S(1)}, f32[4,64,384]{2,1,0:T(8,128)}, u32[]{:S(2)}) copy-start(f32[4,64,384]{2,1,0:T(8,128)} %copy-done.11) | copy-start | bytes 1179652
  153.7 30.8 %copy-start.10 = (f32[4,64,384]{2,1,0:T(8,128)S(1)}, f32[4,64,384]{2,1,0:T(8,128)}, u32[]{:S(2)}) copy-start(f32[4,64,384]{2,1,0:T(8,128)} %copy-done.9) | copy-start | bytes 1179652
  159.9 33.9 %all-to-all-start.6 = ((f32[32,1,2304]{2,1,0:T(1,128)}), f32[32,1,2304]{2,1,0:T(1,128)S(1)}, u32[]{:S(2)}, u32[]{:S(2)}) async-start(f32[32,1,2304]{2,1,0:T(1,128)} %bitcast.25), calls=%async_computation.6 | async-start | bytes 589824 | tf_op jit(solution)/shard_map/all_to_all | solution.py:338
  170.0 19.3 %collective-permute-start.8 = (f32[4,64,384]{2,1,0:T(8,128)S(1)}, f32[4,64,384]{2,1,0:T(8,128)S(1)}, u32[]{:S(2)}, u32[]{:S(2)}) collective-permute-start(f32[4,64,384]{2,1,0:T(8,128)S(1)} %copy-done.12), channel_id=1, source_target_pairs={{0,16},{16,32},{32,48},{48,64},{64,80},{80,96},{96,112},{112,128},... | collective-permute-start | bytes 1179656 | tf_op jit(solution)/shard_map/ppermute | solution.py:334
  184.5 9.1 %collective-permute-start.9 = (f32[4,64,384]{2,1,0:T(8,128)S(1)}, f32[4,64,384]{2,1,0:T(8,128)S(1)}, u32[]{:S(2)}, u32[]{:S(2)}) collective-permute-start(f32[4,64,384]{2,1,0:T(8,128)S(1)} %copy-done.10), channel_id=1, source_target_pairs={{16,0},{32,16},{48,32},{64,48},{80,64},{96,80},{112,96},{128,112},... | collective-permute-start | bytes 1179656 | tf_op jit(solution)/shard_map/ppermute | solution.py:334
  204.8 22.3 %all-to-all-start.8 = ((f32[32,1,2304]{2,1,0:T(1,128)}), f32[32,1,2304]{2,1,0:T(1,128)S(1)}, u32[]{:S(2)}, u32[]{:S(2)}) async-start(f32[32,1,2304]{2,1,0:T(1,128)} %broadcast_in_dim.21), calls=%async_computation.8 | async-start | bytes 589824 | tf_op jit(solution)/shard_map/all_to_all | solution.py:344
  215.2 8.8 %collective-permute-start.10 = (f32[2,128,128]{2,1,0:T(8,128)S(1)}, f32[2,128,128]{2,1,0:T(8,128)S(1)}, u32[]{:S(2)}, u32[]{:S(2)}) collective-permute-start(f32[2,128,128]{2,1,0:T(8,128)S(1)} %get-tuple-element.52), channel_id=1, source_target_pairs={{0,1},{1,2},{2,3},{3,4},{4,5},{5,6},{6,7},{7,8},{8,9},{9,10},{10,1... | collective-permute-start | bytes 393224 | tf_op jit(solution)/shard_map/ppermute | solution.py:334
  218.3 7.9 %collective-permute-start.11 = (f32[2,128,128]{2,1,0:T(8,128)S(1)}, f32[2,128,128]{2,1,0:T(8,128)S(1)}, u32[]{:S(2)}, u32[]{:S(2)}) collective-permute-start(f32[2,128,128]{2,1,0:T(8,128)S(1)} %get-tuple-element.53), channel_id=1, source_target_pairs={{1,0},{2,1},{3,2},{4,3},{5,4},{6,5},{7,6},{8,7},{9,8},{10,9},{11,1... | collective-permute-start | bytes 393224 | tf_op jit(solution)/shard_map/ppermute | solution.py:334

commit v2 on v1

v2 whole, which is shorter than its diff:
```python
import math

import jax
import jax.numpy as jnp
import ml_dtypes
import numpy as np
from jax import lax
from jax.experimental import pallas as pl
from jax.experimental.pallas import tpu as pltpu
from jax.sharding import Mesh, PartitionSpec as P

ROW = ("x", "yl", "c")
COL = ("yh", "z")
XZ = ("x", "z")
Y = ("yh", "yl")

W = 128
H = 64
TR = 128
TC = 256
EC = 384
M = 4
WIN = W + 8
F = 8
f32 = jnp.float32
bf16 = jnp.bfloat16


def split_np(a):
    out = []
    for _ in range(3):
        part = a.astype(ml_dtypes.bfloat16)
        out.append(part)
        a = a - part.astype(np.float64)
    return out


def tables_np():
    n = np.arange(W)
    ang = -2.0 * math.pi * ((n[:, None] * n[None, :]) % W) / W
    t = np.exp(1j * ang) / math.sqrt(W)
    f = ((n + H) % W - H).astype(np.float64)
    k = np.exp(-4j * math.pi * f * f / (W * W))
    a = np.conj(t) @ (k[:, None] * t)
    return np.stack([np.stack([np.stack(split_np(m.real)), np.stack(split_np(m.imag))], axis=1) for m in (t, a)])


def lanes(shape):
    return lax.broadcasted_iota(jnp.int32, shape, len(shape) - 1)


def split(x, parts):
    out = []
    for i in range(parts):
        h = x.astype(bf16)
        out.append(h)
        if i < parts - 1:
            x = x - h.astype(f32)
    return out


PAIRS = {2: ((0, 0), (0, 1), (1, 0)), 3: ((0, 0), (0, 1), (1, 0), (0, 2), (1, 1), (2, 0))}


def cmul(ar, ai, br, bi):
    return ar * br - ai * bi, ar * bi + ai * br


def cmulc(ar, ai, br, bi):
    return ar * br + ai * bi, ar * bi - ai * br


def right(z, lhs, tab, i, parts):
    w = jnp.concatenate([tab[i + t] for _, t in PAIRS[parts]], axis=0)
    fs = 256 // W
    for k in range(F // fs):
        rows = slice(k * 256, (k + 1) * 256)
        x = jnp.concatenate([lhs[rows, p * 2 * W : (p + 1) * 2 * W] for p, _ in PAIRS[parts]], axis=1)
        y = jnp.dot(x, w, preferred_element_type=f32)
        z[0, k * fs : (k + 1) * fs] = y[:, :W].reshape(fs, W, W)
        z[1, k * fs : (k + 1) * fs] = y[:, W:].reshape(fs, W, W)


def put_lhs(lhs, f, xr, xi, parts):
    rows = slice(f * W, (f + 1) * W)
    for q, x in enumerate((xr, xi)):
        for p, v in enumerate(split(x, parts)):
            at = (2 * p + q) * W
            lhs[rows, at : at + W] = v


def both(z, lhs, tab, i, parts):
    right(z, lhs, tab, i, parts)
    for f in range(F):
        put_lhs(lhs, f, z[0, f].T, z[1, f].T, parts)
    right(z, lhs, tab, i, parts)


U, UT, B, BT = 0, 3, 6, 9


def build_tables(tab, blocks):
    for j in range(2):
        for part in range(3):
            re = blocks[j, part, 0]
            im = blocks[j, part, 1]
            for i, (ur, ll) in enumerate(((-im, im), (im, -im))):
                k = 6 * j + 3 * i + part
                tab[k, :W, :W] = re
                tab[k, :W, W:] = ur
                tab[k, W:, :W] = ll
                tab[k, W:, W:] = re


def window(r0, s):
    r8 = r0 // 8
    q = s // W
    q1 = jnp.where(q == 2, 0, q + 1)
    rows = pl.ds(pl.multiple_of(r8 * 8, 8), WIN)
    at = [(rows, pl.ds(pl.multiple_of(t * W, W), W)) for t in (q, q1)]
    return at, r0 - r8 * 8, s - q * W


def cut(e, r0, s, plane):
    at, dr, dc = window(r0, s)
    low = lanes((WIN, W)) >= dc
    v = jnp.where(low, e[(plane,) + at[0]], e[(plane,) + at[1]])
    v = pltpu.roll(v, jnp.where(dc == 0, 0, W - dc), 1)
    v = pltpu.roll(v, jnp.where(dr == 0, 0, WIN - dr), 0)
    return v[:W]


def place(g, r0, s, plane, val):
    at, dr, dc = window(r0, s)
    v = jnp.concatenate([val, jnp.zeros((WIN - W, W), f32)], axis=0)
    v = pltpu.roll(v, dr, 0)
    v = pltpu.roll(v, dc, 1)
    low = lanes((WIN, W)) >= dc
    i0 = (plane,) + at[0]
    i1 = (plane,) + at[1]
    g[i0] = g[i0] + jnp.where(low, v, 0.0)
    g[i1] = g[i1] + jnp.where(low, 0.0, v)


def iteration(info, e, p, meas, blocks, g, acc, s, parts, waits):
    tab, z, lhs, o, psi1 = s
    where, positions, counts = info
    rows = [jnp.clip(positions[0, 0, n, 0] - where[0] + H, 0, TR - 1) for n in range(2)]
    cols = [jnp.clip(positions[0, 0, n, 1] - where[1] + W, H, TC + H - 1) for n in range(2)]
    live = [(counts[0, 0] > n).astype(f32) for n in range(2)]
    for k in range(4):
        waits[2](k)
        g[k] = jnp.zeros_like(g[k])
        for n in range(2):
            v = cut(e, rows[n], cols[n], k)
            o[n, k] = v if k < 2 else v.T
    waits[3]()
    wsum = None
    for n in range(2):
        t = (o[n, 0] * o[n, 0] + o[n, 1] * o[n, 1]) * live[n]
        wsum = t if wsum is None else wsum + t
    acc[8 * W :] = wsum
    for f in range(F):
        n, m = divmod(f, M)
        put_lhs(lhs, f, *cmul(p[2 * m], p[2 * m + 1], o[n, 0], o[n, 1]), parts)
    waits[0].wait()
    build_tables(tab, blocks)
    both(psi1, lhs, tab, BT, parts)
    for f in range(F):
        n = f // M
        put_lhs(lhs, f, *cmul(psi1[0, f], psi1[1, f], o[n, 2], o[n, 3]), parts)
    both(z, lhs, tab, UT, parts)
    for n in range(2):
        tot = None
        for f in range(n * M, (n + 1) * M):
            t = z[0, f] * z[0, f] + z[1, f] * z[1, f]
            tot = t if tot is None else tot + t
        if n == 0:
            waits[1].wait()
        wt = 2.0 * (tot - meas[n])
        for f in range(n * M, (n + 1) * M):
            put_lhs(lhs, f, wt * z[0, f], wt * z[1, f], parts)
    both(z, lhs, tab, U, parts)
    for n in range(2):
        sr = si = None
        for f in range(n * M, (n + 1) * M):
            tr, ti = cmulc(psi1[0, f], psi1[1, f], z[0, f], z[1, f])
            sr = tr if sr is None else sr + tr
            si = ti if si is None else si + ti
            put_lhs(lhs, f, *cmulc(o[n, 2], o[n, 3], z[0, f], z[1, f]), parts)
        place(g, rows[n], cols[n], 2, sr.T * live[n])
        place(g, rows[n], cols[n], 3, si.T * live[n])
    waits[4]()
    both(z, lhs, tab, B, parts)
    for n in range(2):
        sr = si = None
        for f in range(n * M, (n + 1) * M):
            m = f - n * M
            tr, ti = cmulc(p[2 * m], p[2 * m + 1], z[0, f], z[1, f])
            sr = tr if sr is None else sr + tr
            si = ti if si is None else si + ti
            for i, v in enumerate(cmulc(o[n, 0], o[n, 1], z[0, f], z[1, f])):
                at = slice((2 * m + i) * W, (2 * m + i + 1) * W)
                acc[at] = v * live[n] if n == 0 else acc[at] + v * live[n]
        place(g, rows[n], cols[n], 0, sr * live[n])
        place(g, rows[n], cols[n], 1, si * live[n])


def start(src, dst, sem):
    c = pltpu.make_async_copy(src, dst, sem)
    c.start()
    return c


def done(copies):
    for c in copies:
        c.wait()


def eight(i):
    return pl.multiple_of(i, 8)


HALF = 576


def send_sums(where, acc, keep, give, sems, i):
    mine = pl.ds(eight(where[2] * HALF), HALF)
    theirs = pl.ds(eight((1 - where[2]) * HALF), HALF)
    return [start(acc.at[mine], keep, sems.at[i]), start(acc.at[theirs], give, sems.at[i + 1])]


def col_messages(where, g, a, b, planes):
    low = lanes((256, W)) < H
    first = where[3] == 0
    for k in planes:
        v = [g[k, :, j * W : (j + 1) * W] for j in range(3)]
        ml = jnp.where(low, v[1], v[0])
        mr = jnp.where(low, v[0], v[2])
        a[k] = jnp.where(first, mr, ml)
        b[k] = jnp.where(first, ml, mr)


def first_kernel(
    where, positions, counts, x, ce, co, even, odd, p_in, meas_in, blocks_in,
    e_out, g_out, me, mo, keep, give,
    e, p, meas, blocks, g, acc, a, b, sems, *s,
):
    up = where[2] == 0
    at = eight(jnp.where(up, H + TR, 0))
    below = eight(H + TR - at)
    strips = [start(ce, a.at[0:2, 0:TR, :], sems.at[0]), start(co, b.at[0:2, 0:TR, :], sems.at[1])]
    ins = [
        [
            start(x.at[k], e.at[k, H : H + TR, W:], sems.at[2 + k]),
            start(even.at[k], e.at[k, pl.ds(at, H), :], sems.at[6 + k]),
            start(odd.at[k], e.at[k, pl.ds(below, H), :], sems.at[10 + k]),
        ]
        for k in range(4)
    ]
    modes_copy = start(p_in, p, sems.at[14])
    tables = start(blocks_in, blocks, sems.at[15])
    measured = start(meas_in, meas, sems.at[16])
    outs = []

    def plane(k):
        if k == 0:
            done(strips)
        done(ins[k])
        low = lanes((TR, W)) < H
        first = where[3] == 0
        left_in = jnp.where(first, b[k // 2, 0:TR], a[k // 2, 0:TR])
        right_in = jnp.where(first, a[k // 2, 0:TR], b[k // 2, 0:TR])
        e[k, H : H + TR, 0:W] = widened(left_in, right_in, k % 2, low)

    def whole():
        modes_copy.wait()
        outs.append(start(e, e_out, sems.at[17]))

    def ready(planes, i):
        col_messages(where, g, a, b, planes)
        ps = slice(planes[0], planes[-1] + 1)
        outs.append(start(a.at[ps], me.at[ps], sems.at[i]))
        outs.append(start(b.at[ps], mo.at[ps], sems.at[i + 1]))
        outs.append(start(g.at[ps], g_out.at[ps], sems.at[i + 2]))

    iteration(
        (where, positions, counts), e, p, meas, blocks, g, acc, s, 3,
        (tables, measured, plane, whole, lambda: ready((2, 3), 18)),
    )
    outs += send_sums(where, acc, keep, give, sems, 21)
    ready((0, 1), 23)
    done(outs)


def sum_copies(where, own, other, s, sems, i):
    mine = pl.ds(eight(where[2] * HALF), HALF)
    theirs = pl.ds(eight((1 - where[2]) * HALF), HALF)
    return [start(own, s.at[mine], sems.at[i]), start(other, s.at[theirs], sems.at[i + 1])]


def new_modes(p, s):
    inv = 0.25 / jnp.sqrt(s[8 * W :])
    for k in range(8):
        p[k] = p[k] - s[k * W : (k + 1) * W] * inv


def second_kernel(
    where, positions, counts, e_in, ge_in, go_in, even, odd, p_in, own, other, meas_in, blocks_in,
    oc, gc, give, go, keep, p_out,
    e, p, meas, blocks, g, acc, r, sums, sems, *s,
):
    at = eight(jnp.where(where[2] == 0, TR, 0))
    hi = pl.ds(at, TR)
    lo = pl.ds(eight(TR - at), TR)
    ins = [
        [
            start(e_in.at[k], e.at[k], sems.at[5 * k]),
            start(ge_in.at[k], g.at[k, hi, :], sems.at[5 * k + 1]),
            start(go_in.at[k], g.at[k, lo, :], sems.at[5 * k + 2]),
            start(even.at[k], r.at[k, hi, :], sems.at[5 * k + 3]),
            start(odd.at[k], r.at[k, lo, :], sems.at[5 * k + 4]),
        ]
        for k in range(4)
    ]
    sums_copies = [start(p_in, p, sems.at[20])] + sum_copies(where, own, other, sums, sems, 21)
    tables = start(blocks_in, blocks, sems.at[23])
    measured = start(meas_in, meas, sems.at[24])
    outs = []
    up = eight(jnp.where(where[2] == 0, H + TR, 0))
    down = eight(H + TR - up)

    def plane(k):
        done(ins[k])
        e[k] = e[k] - 0.1 * (g[k] + r[k])

    def whole():
        outs.append(start(e.at[:, H : H + TR, W:], oc, sems.at[25]))
        done(sums_copies)
        new_modes(p, sums)
        outs.append(start(p, p_out, sems.at[26]))

    def ready(planes, i):
        ps = slice(planes[0], planes[-1] + 1)
        outs.append(start(g.at[ps, pl.ds(down, H), :], go.at[ps], sems.at[i]))
        outs.append(start(g.at[ps, H : H + TR, :], gc.at[ps], sems.at[i + 1]))
        for k in planes:
            for j in range(3):
                rows = pl.ds(HALF + (3 * k + j) * H, H)
                outs.append(start(g.at[k, pl.ds(up, H), j * W : (j + 1) * W], give.at[rows], sems.at[30 + 3 * k + j]))

    iteration(
        (where, positions, counts), e, p, meas, blocks, g, acc, s, 2,
        (tables, measured, plane, whole, lambda: ready((2, 3), 27)),
    )
    outs += send_sums(where, acc, keep, give.at[pl.ds(0, HALF)], sems, 42)
    ready((0, 1), 44)
    done(outs)


def widened(left_in, right_in, part, low):
    if part == 0:
        return jnp.where(low, right_in, pltpu.roll(left_in, H, 1))
    return jnp.where(low, pltpu.roll(right_in, H, 1), left_in)


def pack(a, b, hi):
    low = lanes(a.shape) < H
    if hi:
        return jnp.where(low, pltpu.roll(a, H, 1), b)
    return jnp.where(low, a, pltpu.roll(b, H, 1))


def strips_kernel(where, x, even, odd):
    first = where[3] == 0
    for k in range(2):
        ml = pack(x[k, 0, :, 0:W], x[k, 1, :, 0:W], False)
        mr = pack(x[k, 0, :, W:], x[k, 1, :, W:], True)
        even[k] = jnp.where(first, mr, ml)
        odd[k] = jnp.where(first, ml, mr)


def widen_kernel(where, x, even, odd, be, bo):
    low = lanes((H, W)) < H
    first = where[3] == 0
    at = eight(jnp.where(where[2] == 0, H, 0))
    for out, rows in ((be, pl.ds(at, H)), (bo, pl.ds(eight(H - at), H))):
        for k in range(2):
            left_in = jnp.where(first, odd[k, rows], even[k, rows])
            right_in = jnp.where(first, even[k, rows], odd[k, rows])
            for j in range(2):
                out[2 * k + j, :, 0:W] = widened(left_in, right_in, j, low)
                out[2 * k + j, :, W:] = x[k, j, rows]


def halves_kernel(where, g_in, even, odd, ge, go, g, a, b, sems):
    ins = [
        [
            start(g_in.at[k], g.at[k], sems.at[3 * k]),
            start(even.at[k], a.at[k], sems.at[3 * k + 1]),
            start(odd.at[k], b.at[k], sems.at[3 * k + 2]),
        ]
        for k in range(4)
    ]
    low = lanes((256, W)) < H
    first = where[3] == 0
    at = eight(jnp.where(where[2] == 0, TR, 0))
    outs = []
    for k in range(4):
        done(ins[k])
        rl = jnp.where(first, b[k], a[k])
        rr = jnp.where(first, a[k], b[k])
        g[k, :, 0:W] = g[k, :, 0:W] + jnp.where(low, rr, rl)
        g[k, :, W : 2 * W] = g[k, :, W : 2 * W] + jnp.where(low, rl, 0.0)
        g[k, :, 2 * W :] = g[k, :, 2 * W :] + jnp.where(low, 0.0, rr)
        outs.append(start(g.at[k, pl.ds(at, TR), :], ge.at[k], sems.at[12 + 2 * k]))
        outs.append(start(g.at[k, pl.ds(eight(TR - at), TR), :], go.at[k], sems.at[13 + 2 * k]))
    done(outs)


def fold_kernel(where, oc, gc, even, odd, t, me, mo, r):
    at = eight(jnp.where(where[2] == 0, H, 0))
    for k in range(4):
        for j in range(3):
            r[k, pl.ds(at, H), j * W : (j + 1) * W] = even[HALF + (3 * k + j) * H : HALF + (3 * k + j + 1) * H]
    r[:, pl.ds(eight(H - at), H), :] = odd[...]
    first = where[3] == 0
    for k in range(4):
        t[k] = oc[k] - 0.1 * (gc[k, :, W:] + r[k, :, W:])
    for k in range(2):
        v0 = gc[2 * k, :, 0:W] + r[2 * k, :, 0:W]
        v1 = gc[2 * k + 1, :, 0:W] + r[2 * k + 1, :, 0:W]
        ml = pack(v0, v1, True)
        mr = pack(v0, v1, False)
        me[k] = jnp.where(first, mr, ml)
        mo[k] = jnp.where(first, ml, mr)


def last_kernel(where, t, even, odd, out):
    low = lanes((TR, W)) < H
    first = where[3] == 0
    for k in range(2):
        rl = jnp.where(first, odd[k], even[k])
        rr = jnp.where(first, even[k], odd[k])
        add = (
            (jnp.where(low, rl, 0.0), jnp.where(low, 0.0, pltpu.roll(rr, H, 1))),
            (jnp.where(low, pltpu.roll(rl, H, 1), 0.0), jnp.where(low, 0.0, rr)),
        )
        for j in range(2):
            for h in range(2):
                cs = slice(h * W, (h + 1) * W)
                out[k, j, :, cs] = t[2 * k + j, :, cs] - 0.1 * add[j][h]


def modes_kernel(where, p, own, other, out, s):
    s[pl.ds(eight(where[2] * HALF), HALF)] = own[...]
    s[pl.ds(eight((1 - where[2]) * HALF), HALF)] = other[...]
    out[...] = p[...]
    new_modes(out, s)


HB = pl.BlockSpec(memory_space=pltpu.HBM)
VM = pl.BlockSpec(memory_space=pltpu.VMEM)
SM = pl.BlockSpec(memory_space=pltpu.SMEM)


def sds(*shape):
    return jax.ShapeDtypeStruct(shape, f32)


def vm(*shape):
    return pltpu.VMEM(shape, f32)


def sem(n):
    return pltpu.SemaphoreType.DMA((n,))


def call(kernel, outs, smem, args, scratch=(), cost=None, big=False):
    spec = HB if big else VM
    return pl.pallas_call(
        kernel,
        out_shape=outs,
        in_specs=[SM] * len(smem) + [spec] * len(args),
        out_specs=[spec] * len(outs),
        scratch_shapes=list(scratch),
        compiler_params=pltpu.CompilerParams(vmem_limit_bytes=(63 if big else 12) * 1024 * 1024),
        cost_estimate=cost,
    )(*smem, *args)


def odd_swap(odd, axes, size):
    return lax.ppermute(odd, axes, [(i, ((i + 1) ^ 1) - 1) for i in range(1, size - 1)])


def swap(even, odd, axes, size):
    return lax.ppermute(even, axes, [(i, i ^ 1) for i in range(size)]), odd_swap(odd, axes, size)


def other_core(v):
    return lax.ppermute(v, "c", [(0, 1), (1, 0)])


def scatter_sum(v, axes, n):
    v = lax.all_to_all(v.reshape(n, 1, -1), axes, 0, 0, tiled=True)
    return jnp.sum(v, axis=(0, 1))


def spread(v, axes, n):
    w = jnp.broadcast_to(v[None, None], (n, 1) + v.shape)
    return lax.all_to_all(w, axes, 0, 0, tiled=True)


def apart(yes, f, shape):
    return lax.cond(yes, f, lambda: jnp.zeros(shape, f32))


def reduce_out(yes, keep, got):
    def step():
        v = scatter_sum(keep + got[:HALF], XZ, 32)
        return jnp.sum(spread(v, Y, 8), axis=(0, 1))

    return apart(yes, step, (2304,))


def gather_back(yes, v):
    return apart(yes, lambda: spread(v, XZ, 32).reshape(HALF, W), (HALF, W))


ITER_COST = pl.CostEstimate(flops=10_000_000_000, bytes_accessed=8_000_000, transcendentals=0)


def body(objects, probe_modes, intensities, positions, counts):
    blocks = jnp.asarray(tables_np())
    where = jnp.stack([
        lax.axis_index(ROW) * TR,
        lax.axis_index(COL) * TC,
        lax.axis_index("c"),
        lax.axis_index("z") % 2,
    ]).astype(jnp.int32)
    modes = probe_modes.reshape(8, W, W)
    measured = intensities[0, 0]
    info = (where, positions, counts)
    yes = counts[0, 0] >= 0
    shared = [
        vm(4, 256, EC), vm(8, W, W), vm(2, W, W), pltpu.VMEM((2, 3, 2, W, W), bf16), vm(4, 256, EC), vm(9 * W, W),
    ]
    scratch = [
        pltpu.VMEM((12, 2 * W, 2 * W), bf16),
        vm(2, F, W, W),
        pltpu.VMEM((F * W, 6 * W), bf16),
        vm(2, 4, W, W),
        vm(2, F, W, W),
    ]

    me, mo = call(strips_kernel, [sds(2, TR, W)] * 2, (where,), (objects,))
    ce, co = swap(me, mo, COL, 16)
    be, bo = call(widen_kernel, [sds(4, H, EC), sds(4, H, EC)], (where,), (objects, ce, co))
    re, ro = swap(be, bo, ROW, 32)
    e, g, me, mo, keep, give = call(
        first_kernel,
        [sds(4, 256, EC), sds(4, 256, EC), sds(4, 256, W), sds(4, 256, W), sds(HALF, W), sds(HALF, W)],
        info, (objects.reshape(4, TR, TC), ce, co, re, ro, modes, measured, blocks),
        shared + [vm(4, 256, W), vm(4, 256, W), sem(26)] + scratch, cost=ITER_COST, big=True,
    )

    got = other_core(give)
    ce, co = swap(me, mo, COL, 16)
    v = reduce_out(yes, keep, got)
    v, ce, co = lax.optimization_barrier((v, ce, co))
    ge, go = call(
        halves_kernel, [sds(4, TR, EC), sds(4, TR, EC)], (where,), (g, ce, co),
        [vm(4, 256, EC), vm(4, 256, W), vm(4, 256, W), sem(20)], big=True,
    )
    v, ge, go = lax.optimization_barrier((v, ge, go))
    re, ro = swap(ge, go, ROW, 32)
    own = gather_back(yes, v)
    own, re, ro = lax.optimization_barrier((own, re, ro))
    other = other_core(own)
    oc, gc, give, go, keep, modes = call(
        second_kernel,
        [sds(4, TR, TC), sds(4, TR, EC), sds(HALF + 12 * H, W), sds(4, H, EC), sds(HALF, W), sds(8, W, W)],
        info, (e, ge, go, re, ro, modes, own, other, measured, blocks),
        shared + [vm(4, 256, EC), vm(9 * W, W), sem(46)] + scratch, cost=ITER_COST, big=True,
    )

    got = other_core(give)
    ro = odd_swap(go, ROW, 32)
    v = reduce_out(yes, keep, got)
    v, got, ro = lax.optimization_barrier((v, got, ro))
    t, me, mo = call(
        fold_kernel, [sds(4, TR, TC), sds(2, TR, W), sds(2, TR, W)], (where,), (oc, gc, got, ro), [vm(4, TR, EC)],
    )
    v, me, mo = lax.optimization_barrier((v, me, mo))
    ce, co = swap(me, mo, COL, 16)
    own = gather_back(yes, v)
    own, ce, co = lax.optimization_barrier((own, ce, co))
    other = other_core(own)
    (refined,) = call(last_kernel, [sds(2, 2, TR, TC)], (where,), (t, ce, co))
    (modes,) = call(modes_kernel, [sds(8, W, W)], (where,), (modes, own, other), [vm(9 * W, W)])
    return refined, modes.reshape(M, 2, W, W)


def solution(mesh):
    fine = Mesh(mesh.devices.reshape(4, 4, 2, 2, 8), ("x", "yl", "c", "yh", "z"))
    return jax.shard_map(
        body,
        mesh=fine,
        in_specs=(
            P(None, None, ROW, COL),
            P(),
            P(ROW, COL, None, None, None),
            P(ROW, COL, None, None),
            P(ROW, COL),
        ),
        out_specs=(P(None, None, ROW, COL), P()),
        check_vma=False,
    )
```

time: 236 us -> 217 us (0.919)
  blocking collectives: 67.1 us -> 109 us
  starting transfers between devices: 81.3 us -> 53.2 us
  local copies, waits for them, and re-layouts: 20.7 us -> 3.72 us
  waiting for transfers between devices: 34.2 us -> 17.7 us
  Pallas kernels: 24.1 us -> 30 us
  other arithmetic: 6.16 us -> 0.63 us
    all_to_all x3 -> x4, blocking collectives: 28.8 us -> 67.6 us  [spread(): return lax.all_to_all(w, axes, 0, 0, tiled=True)]
    all_to_all x4 -> x0, starting transfers between devices: 37.1 us -> none  [the longest x3 27.1 us: spread(): return lax.all_to_all(w, axes, 0, 0, tiled=True)]
    unnamed x42 -> x28, local copies, waits for them, and re-layouts: 17.4 us -> 3.33 us
    ppermute x12 -> x15, waiting for transfers between devices: 28.2 us -> 17.7 us  [the longest x6 12.9 us: odd_swap(): lax.ppermute(odd, axes, [(i, (i + 1 ^ 1) - 1) for i in range(1, size - 1)])]
    ppermute x12 -> x15, starting transfers between devices: 44.2 us -> 53.2 us  [the longest x5 31.6 us: swap(): lax.ppermute(even, axes, [(i, i ^ 1) for i in range(size)])]
    all_to_all x4 -> x0, waiting for transfers between devices: 5.94 us -> none  [the longest x3 5.93 us: spread(): return lax.all_to_all(w, axes, 0, 0, tiled=True)]
    pallas_call x7 -> x8, Pallas kernels: 24.1 us -> 30 us  [call(): pl.pallas_call(kernel, out_shape=outs, in_specs=[SM] * len(smem) + [spec]...]
    reduce_sum x4 -> x2, other arithmetic: 5.08 us -> 0.36 us  [scatter_sum(): return jnp.sum(v, axis=(0, 1))]
  transfers between devices with their start and end apart: 16 -> 15, of which waited for: 10 -> 5; matrix products, arithmetic and copies ran while one was open for 2% -> 0% of each run, Pallas kernels for 0% -> 1%
where the time goes in v2:
time: 217 us; the launch traced here: 216 us
  blocking collectives  109 us (50%)
  starting transfers between devices  53.2 us (25%)
  Pallas kernels  30 us (14%)
  waiting for transfers between devices  17.7 us (8%)
  local copies, waits for them, and re-layouts  3.72 us (2%)
    all_to_all x4, blocking collectives, spread(): return lax.all_to_all(w, axes, 0, 0, tiled=True)  67.6 us
    all_to_all x2, blocking collectives, scatter_sum(): v = lax.all_to_all(v.reshape(n, 1, -1), axes, 0, 0, tiled=True)  41.4 us
    ppermute x5, starting transfers between devices, swap(): lax.ppermute(even, axes, [(i, i ^ 1) for i in range(size)])  31.6 us
    pallas_call x8, Pallas kernels, call(): pl.pallas_call(kernel, out_shape=outs, in_specs=[SM] * len(smem) + [spec]...  30 us
    ppermute x6, waiting for transfers between devices, odd_swap(): lax.ppermute(odd, axes, [(i, (i + 1 ^ 1) - 1) for i in range(1, size - 1)])  12.9 us
    ppermute x4, starting transfers between devices, other_core(): return lax.ppermute(v, 'c', [(0, 1), (1, 0)])  12.3 us
    ppermute x6, starting transfers between devices, odd_swap(): lax.ppermute(odd, axes, [(i, (i + 1 ^ 1) - 1) for i in range(1, size - 1)])  9.26 us
  transfers between devices with their start and end apart: 15, of which 5 were waited for; matrix products, arithmetic and copies ran while one was open for 0% of the time, Pallas kernels for 1%

profile of v2, /device:TPU:1, one launch (start us, length us, event | category | flops | bytes accessed | tf_op | source)
XLA Modules:
  0.0 216.0 jit_solution(10034911967254343711)
XLA Ops:
  0.6 0.1 pad_add_fusion.where
  0.7 1.0 copy-done
  1.8 0.7 shard_map.77
  2.4 4.8 %collective-permute-start = (f32[2,128,128]{2,1,0:T(8,128)S(1)}, f32[2,128,128]{2,1,0:T(8,128)S(1)}, u32[]{:S(2)}, u32[]{:S(2)}) collective-permute-start(f32[2,128,128]{2,1,0:T(8,128)S(1)} %get-tuple-element.67), channel_id=1, source_target_pairs={{0,1},{1,0},{2,3},{3,2},{4,5},{5,4},{6,7},{7,6},{8,9},{9,8},{10,11... | collective-permute-start | bytes 393224 | tf_op jit(solution)/shard_map/ppermute | solution.py:497
  7.3 0.7 collective-permute-start.1
  8.0 1.7 collective-permute-done.even.ce
  9.6 0.0 collective-permute-done.1.odd.co
  9.6 0.7 shard_map.78
  10.3 8.5 %collective-permute-start.2 = (f32[4,64,384]{2,1,0:T(8,128)S(1)}, f32[4,64,384]{2,1,0:T(8,128)S(1)}, u32[]{:S(2)}, u32[]{:S(2)}) collective-permute-start(f32[4,64,384]{2,1,0:T(8,128)S(1)} %get-tuple-element.69), channel_id=1, source_target_pairs={{0,16},{16,0},{32,48},{48,32},{64,80},{80,64},{96,112},{112,96},{1... | collective-permute-start | bytes 1179656 | tf_op jit(solution)/shard_map/ppermute | solution.py:497
  18.8 1.9 collective-permute-start.3
  21.4 0.0 collective-permute-done.2.even
  21.4 8.3 %collective-permute-done.3.odd = f32[4,64,384]{2,1,0:T(8,128)S(1)} collective-permute-done((f32[4,64,384]{2,1,0:T(8,128)S(1)}, f32[4,64,384]{2,1,0:T(8,128)S(1)}, u32[]{:S(2)}, u32[]{:S(2)}) %collective-permute-start.3) | collective-permute-done | bytes 393248 | tf_op jit(solution)/shard_map/ppermute | solution.py:493
  29.8 0.7 copy-done.12
  30.5 0.0 copy-done.4
  30.5 12.3 %shard_map.79 = (f32[4,256,384]{2,1,0:T(8,128)}, f32[4,256,384]{2,1,0:T(8,128)}, f32[4,256,128]{2,1,0:T(8,128)}, f32[4,256,128]{2,1,0:T(8,128)}, f32[576,128]{1,0:T(8,128)S(1)}, /*index=5*/f32[576,128]{1,0:T(8,128)}) custom-call(s32[4]{0:T(128)} %copy-done.6, s32[1,1,2,2]{3,2,1,0:T(2,128)} %positions.3, s32[1,1]{1,0:T(1,128)S(6)} %copy.20.counts, ...), custom_call_target="tpu_custom_call" | custom-call | flops 10000000000 | bytes 8000000 | tf_op jit(solution)/shard_map/pallas_call | solution.py:481
  42.8 7.9 %collective-permute-start.5 = (f32[4,256,128]{2,1,0:T(8,128)}, f32[4,256,128]{2,1,0:T(8,128)S(1)}, u32[]{:S(2)}, u32[]{:S(2)}) collective-permute-start(f32[4,256,128]{2,1,0:T(8,128)} %get-tuple-element.74), channel_id=1, source_target_pairs={{0,1},{1,0},{2,3},{3,2},{4,5},{5,4},{6,7},{7,6},{8,9},{9,8},{10,11... | collective-permute-start | bytes 1572872 | tf_op jit(solution)/shard_map/ppermute | solution.py:497
  50.7 1.5 collective-permute-start.6
  52.2 1.9 collective-permute-start.4
  54.1 1.8 collective-permute-done.4
  55.8 48.2 %conditional.4 = (f32[2304]{0:T(1024)S(1)}) conditional(s32[]{:T(128)} %bitcast.11, () %tuple.38, (f32[576,128]{1,0:T(8,128)S(1)}, f32[576,128]{1,0:T(8,128)S(1)}) %tuple.39), branch_computations={%region_0.1_spmd, %region_1.4_spmd} | conditional | flops 161280 | bytes 2092048 | solution.py:515
  55.9 27.0 %all_to_all.24 = f32[32,1,2304]{2,1,0:T(1,128)S(1)} all-to-all(f32[32,1,2304]{2,1,0:T(1,128)S(1)} %bitcast.14), channel_id=1, replica_groups=mesh['x'=4,'yl'=4,'c'=2,'yh'=2,'z'=8] {'x','z'}, dimensions={0} | all-to-all | bytes 589824 | tf_op jit(solution)/shard_map/cond/branch_1_fun/all_to_all | solution.py:505
  82.9 0.2 reduce_sum.32
  83.2 20.8 %all_to_all.25 = f32[8,1,2304]{2,1,0:T(1,128)S(1)} all-to-all(f32[8,1,2304]{2,1,0:T(1,128)S(1)} %broadcast_in_dim.8), channel_id=1, replica_groups=mesh['x'=4,'yl'=4,'c'=2,'yh'=2,'z'=8] {'yh','yl'}, dimensions={0} | all-to-all | bytes 147456 | tf_op jit(solution)/shard_map/cond/branch_1_fun/all_to_all | solution.py:511
  104.0 0.1 reduce_sum.33
  104.1 0.0 collective-permute-done.5.even
  104.1 0.0 copy-start.8
  104.1 0.0 collective-permute-done.6.odd
  104.1 0.8 copy-done.8
  104.9 3.3 %shard_map.80 = (f32[4,128,384]{2,1,0:T(8,128)}, f32[4,128,384]{2,1,0:T(8,128)}) custom-call(s32[4]{0:T(128)} %copy-done.6, f32[4,256,384]{2,1,0:T(8,128)} %get-tuple-element.77.g_in, f32[4,256,128]{2,1,0:T(8,128)} %copy-done.8, f32[4,256,128]{2,1,0:T(8,128)} %collective-permute-done.6.odd), custom_call_target="tpu_custom_call" | custom-call | tf_op jit(solution)/shard_map/pallas_call | solution.py:481
  108.2 7.0 %collective-permute-start.7 = (f32[4,128,384]{2,1,0:T(8,128)}, f32[4,128,384]{2,1,0:T(8,128)S(1)}, u32[]{:S(2)}, u32[]{:S(2)}) collective-permute-start(f32[4,128,384]{2,1,0:T(8,128)} %get-tuple-element.82.ge_in), channel_id=1, source_target_pairs={{0,16},{16,0},{32,48},{48,32},{64,80},{80,64},{96,112},{112,96},{1... | collective-permute-start | bytes 2359304 | tf_op jit(solution)/shard_map/ppermute | solution.py:497
  115.2 2.1 collective-permute-start.8
  117.3 15.3 %conditional.5 = (f32[576,128]{1,0:T(8,128)S(1)}) conditional(s32[]{:T(128)} %bitcast.11, () %tuple.42, f32[2304]{0:T(1024)S(1)} %get-tuple-element.106), branch_computations={%region_4.5_spmd, %region_5.6_spmd} | conditional | bytes 893960 | solution.py:515
  117.3 0.2 broadcast_in_dim.9
  117.5 15.1 %all_to_all.26 = f32[32,1,2304]{2,1,0:T(1,128)S(1)} all-to-all(f32[32,1,2304]{2,1,0:T(1,128)S(1)} %broadcast_in_dim.9), channel_id=1, replica_groups=mesh['x'=4,'yl'=4,'c'=2,'yh'=2,'z'=8] {'x','z'}, dimensions={0} | all-to-all | bytes 589824 | tf_op jit(solution)/shard_map/cond/branch_1_fun/all_to_all | solution.py:511
  132.6 0.0 collective-permute-done.7.even
  132.6 4.6 %collective-permute-done.8.odd = f32[4,128,384]{2,1,0:T(8,128)S(1)} collective-permute-done((f32[4,128,384]{2,1,0:T(8,128)}, f32[4,128,384]{2,1,0:T(8,128)S(1)}, u32[]{:S(2)}, u32[]{:S(2)}) %collective-permute-start.8) | collective-permute-done | bytes 786464 | tf_op jit(solution)/shard_map/ppermute | solution.py:493
  137.1 2.1 collective-permute-start.9
  139.2 1.4 collective-permute-done.9.other
  140.6 0.7 copy-done.13
  141.3 9.4 %shard_map.81 = (f32[4,128,256]{2,1,0:T(8,128)}, f32[4,128,384]{2,1,0:T(8,128)}, f32[1344,128]{1,0:T(8,128)}, f32[4,64,384]{2,1,0:T(8,128)}, f32[576,128]{1,0:T(8,128)S(1)}, /*index=5*/f32[8,128,128]{2,1,0:T(8,128)}) custom-call(s32[4]{0:T(128)} %copy-done.6, s32[1,1,2,2]{3,2,1,0:T(2,128)} %positions.3, s32[1,1]{1,0:T(1,128)S(6)} %copy.20.counts, ...), custom_call_target="tpu_custom_call" | custom-call | flops 10000000000 | bytes 8000000 | tf_op jit(solution)/shard_map/pallas_call | solution.py:481
  150.7 0.0 copy-start.1
  150.8 0.0 copy-start.3
  150.8 2.2 %collective-permute-start.10 = (f32[1344,128]{1,0:T(8,128)}, f32[1344,128]{1,0:T(8,128)S(1)}, u32[]{:S(2)}, u32[]{:S(2)}) collective-permute-start(f32[1344,128]{1,0:T(8,128)} %get-tuple-element.90), channel_id=1, source_target_pairs={{0,16},{16,0},{1,17},{17,1},{2,18},{18,2},{3,19},{19,3},{4,20},{20... | collective-permute-start | bytes 2064392 | tf_op jit(solution)/shard_map/ppermute | solution.py:501
  153.0 2.4 %collective-permute-start.11 = (f32[4,64,384]{2,1,0:T(8,128)}, f32[4,64,384]{2,1,0:T(8,128)S(1)}, u32[]{:S(2)}, u32[]{:S(2)}) collective-permute-start(f32[4,64,384]{2,1,0:T(8,128)} %get-tuple-element.92), channel_id=1, source_target_pairs={{16,32},{32,16},{48,64},{64,48},{80,96},{96,80},{112,128},{128,112... | collective-permute-start | bytes 1179656 | tf_op jit(solution)/shard_map/ppermute | solution.py:493
  155.4 0.0 collective-permute-done.10.even
  155.4 29.1 %conditional.6 = (f32[2304]{0:T(1024)S(1)}) conditional(s32[]{:T(128)} %bitcast.11, () %tuple.44, (f32[1344,128]{1,0:T(8,128)S(1)}, f32[576,128]{1,0:T(8,128)S(1)}) %tuple.45), branch_computations={%region_6.7_spmd, %region_7.10_spmd} | conditional | flops 161280 | bytes 2092048 | solution.py:515
  155.5 14.4 %all_to_all.27 = f32[32,1,2304]{2,1,0:T(1,128)S(1)} all-to-all(f32[32,1,2304]{2,1,0:T(1,128)S(1)} %bitcast.15), channel_id=1, replica_groups=mesh['x'=4,'yl'=4,'c'=2,'yh'=2,'z'=8] {'x','z'}, dimensions={0} | all-to-all | bytes 589824 | tf_op jit(solution)/shard_map/cond/branch_1_fun/all_to_all | solution.py:505
  169.9 0.2 reduce_sum.34
  170.1 14.4 %all_to_all.28 = f32[8,1,2304]{2,1,0:T(1,128)S(1)} all-to-all(f32[8,1,2304]{2,1,0:T(1,128)S(1)} %broadcast_in_dim.10), channel_id=1, replica_groups=mesh['x'=4,'yl'=4,'c'=2,'yh'=2,'z'=8] {'yh','yl'}, dimensions={0} | all-to-all | bytes 147456 | tf_op jit(solution)/shard_map/cond/branch_1_fun/all_to_all | solution.py:511
  184.5 0.1 reduce_sum.35
  184.6 0.0 collective-permute-done.11.odd
  184.6 0.8 shard_map.82
  185.4 0.0 copy-start.2
  185.4 3.4 %collective-permute-start.12 = (f32[2,128,128]{2,1,0:T(8,128)S(1)}, f32[2,128,128]{2,1,0:T(8,128)S(1)}, u32[]{:S(2)}, u32[]{:S(2)}) collective-permute-start(f32[2,128,128]{2,1,0:T(8,128)S(1)} %get-tuple-element.100), channel_id=1, source_target_pairs={{0,1},{1,0},{2,3},{3,2},{4,5},{5,4},{6,7},{7,6},{8,9},{9,8},{10,11... | collective-permute-start | bytes 393224 | tf_op jit(solution)/shard_map/ppermute | solution.py:497
  188.8 0.7 collective-permute-start.13
  189.5 17.4 %conditional.7 = (f32[576,128]{1,0:T(8,128)S(1)}) conditional(s32[]{:T(128)} %bitcast.11, () %tuple.47, f32[2304]{0:T(1024)S(1)} %get-tuple-element.108), branch_computations={%region_10.11_spmd, %region_11.12_spmd} | conditional | bytes 893960 | solution.py:515
  189.5 0.2 broadcast_in_dim.11
  189.7 17.2 %all_to_all.29 = f32[32,1,2304]{2,1,0:T(1,128)S(1)} all-to-all(f32[32,1,2304]{2,1,0:T(1,128)S(1)} %broadcast_in_dim.11), channel_id=1, replica_groups=mesh['x'=4,'yl'=4,'c'=2,'yh'=2,'z'=8] {'x','z'}, dimensions={0} | all-to-all | bytes 589824 | tf_op jit(solution)/shard_map/cond/branch_1_fun/all_to_all | solution.py:511
  206.9 0.0 collective-permute-done.12.even
  206.9 0.0 collective-permute-done.13.odd
  206.9 6.1 %collective-permute-start.14 = (f32[576,128]{1,0:T(8,128)S(1)}, f32[576,128]{1,0:T(8,128)S(1)}, u32[]{:S(2)}, u32[]{:S(2)}) collective-permute-start(f32[576,128]{1,0:T(8,128)S(1)} %get-tuple-element.109.own), channel_id=1, source_target_pairs={{0,16},{16,0},{1,17},{17,1},{2,18},{18,2},{3,19},{19,3},{4,20},{20... | collective-permute-start | bytes 884744 | tf_op jit(solution)/shard_map/ppermute | solution.py:501
  213.0 1.5 shard_map.83
  214.5 0.0 collective-permute-done.14.other
  214.5 1.5 shard_map.84
  (23 shorter events, 0.2 us)
Async XLA Ops:
  0.7 1.0 copy-start
  1.8 28.7 %copy-start.6 = (s32[4]{0:T(128)}, s32[4]{0:T(128)S(1)}, u32[]{:S(2)}) copy-start(s32[4]{0:T(128)S(1)} %pad_add_fusion.where) | copy-start | bytes 52
  2.4 7.2 %collective-permute-start = (f32[2,128,128]{2,1,0:T(8,128)S(1)}, f32[2,128,128]{2,1,0:T(8,128)S(1)}, u32[]{:S(2)}, u32[]{:S(2)}) collective-permute-start(f32[2,128,128]{2,1,0:T(8,128)S(1)} %get-tuple-element.67), channel_id=1, source_target_pairs={{0,1},{1,0},{2,3},{3,2},{4,5},{5,4},{6,7},{7,6},{8,9},{9,8},{10,11... | collective-permute-start | bytes 393224 | tf_op jit(solution)/shard_map/ppermute | solution.py:497
  7.3 2.3 %collective-permute-start.1 = (f32[2,128,128]{2,1,0:T(8,128)S(1)}, f32[2,128,128]{2,1,0:T(8,128)S(1)}, u32[]{:S(2)}, u32[]{:S(2)}) collective-permute-start(f32[2,128,128]{2,1,0:T(8,128)S(1)} %get-tuple-element.68), channel_id=1, source_target_pairs={{1,2},{2,1},{3,4},{4,3},{5,6},{6,5},{7,8},{8,7},{9,10},{10,9},{11,... | collective-permute-start | bytes 393224 | tf_op jit(solution)/shard_map/ppermute | solution.py:493
  9.6 20.9 %copy-start.4 = (f32[2,128,128]{2,1,0:T(8,128)}, f32[2,128,128]{2,1,0:T(8,128)S(1)}, u32[]{:S(2)}) copy-start(f32[2,128,128]{2,1,0:T(8,128)S(1)} %collective-permute-done.even.ce) | copy-start | bytes 393220
  9.6 20.9 %copy-start.5 = (f32[2,128,128]{2,1,0:T(8,128)}, f32[2,128,128]{2,1,0:T(8,128)S(1)}, u32[]{:S(2)}) copy-start(f32[2,128,128]{2,1,0:T(8,128)S(1)} %collective-permute-done.1.odd.co) | copy-start | bytes 393220
  10.3 11.1 %collective-permute-start.2 = (f32[4,64,384]{2,1,0:T(8,128)S(1)}, f32[4,64,384]{2,1,0:T(8,128)S(1)}, u32[]{:S(2)}, u32[]{:S(2)}) collective-permute-start(f32[4,64,384]{2,1,0:T(8,128)S(1)} %get-tuple-element.69), channel_id=1, source_target_pairs={{0,16},{16,0},{32,48},{48,32},{64,80},{80,64},{96,112},{112,96},{1... | collective-permute-start | bytes 1179656 | tf_op jit(solution)/shard_map/ppermute | solution.py:497
  18.8 10.9 %collective-permute-start.3 = (f32[4,64,384]{2,1,0:T(8,128)S(1)}, f32[4,64,384]{2,1,0:T(8,128)S(1)}, u32[]{:S(2)}, u32[]{:S(2)}) collective-permute-start(f32[4,64,384]{2,1,0:T(8,128)S(1)} %get-tuple-element.70), channel_id=1, source_target_pairs={{16,32},{32,16},{48,64},{64,48},{80,96},{96,80},{112,128},{128,112... | collective-permute-start | bytes 1179656 | tf_op jit(solution)/shard_map/ppermute | solution.py:493
  21.4 8.3 %copy-start.11 = (f32[4,64,384]{2,1,0:T(8,128)}, f32[4,64,384]{2,1,0:T(8,128)S(1)}, u32[]{:S(2)}) copy-start(f32[4,64,384]{2,1,0:T(8,128)S(1)} %collective-permute-done.2.even) | copy-start | bytes 1179652
  29.7 0.7 copy-start.12
  42.8 61.3 %collective-permute-start.5 = (f32[4,256,128]{2,1,0:T(8,128)}, f32[4,256,128]{2,1,0:T(8,128)S(1)}, u32[]{:S(2)}, u32[]{:S(2)}) collective-permute-start(f32[4,256,128]{2,1,0:T(8,128)} %get-tuple-element.74), channel_id=1, source_target_pairs={{0,1},{1,0},{2,3},{3,2},{4,5},{5,4},{6,7},{7,6},{8,9},{9,8},{10,11... | collective-permute-start | bytes 1572872 | tf_op jit(solution)/shard_map/ppermute | solution.py:497
  50.7 53.4 %collective-permute-start.6 = (f32[4,256,128]{2,1,0:T(8,128)}, f32[4,256,128]{2,1,0:T(8,128)}, u32[]{:S(2)}, u32[]{:S(2)}) collective-permute-start(f32[4,256,128]{2,1,0:T(8,128)} %get-tuple-element.75), channel_id=1, source_target_pairs={{1,2},{2,1},{3,4},{4,3},{5,6},{6,5},{7,8},{8,7},{9,10},{10,9},{11,... | collective-permute-start | bytes 1572872 | tf_op jit(solution)/shard_map/ppermute | solution.py:493
  52.2 3.7 %collective-permute-start.4 = (f32[576,128]{1,0:T(8,128)}, f32[576,128]{1,0:T(8,128)S(1)}, u32[]{:S(2)}, u32[]{:S(2)}) collective-permute-start(f32[576,128]{1,0:T(8,128)} %get-tuple-element.73), channel_id=1, source_target_pairs={{0,16},{16,0},{1,17},{17,1},{2,18},{18,2},{3,19},{19,3},{4,20},{20... | collective-permute-start | bytes 884744 | tf_op jit(solution)/shard_map/ppermute | solution.py:501
  104.1 0.8 copy-start.8
  108.2 24.4 %collective-permute-start.7 = (f32[4,128,384]{2,1,0:T(8,128)}, f32[4,128,384]{2,1,0:T(8,128)S(1)}, u32[]{:S(2)}, u32[]{:S(2)}) collective-permute-start(f32[4,128,384]{2,1,0:T(8,128)} %get-tuple-element.82.ge_in), channel_id=1, source_target_pairs={{0,16},{16,0},{32,48},{48,32},{64,80},{80,64},{96,112},{112,96},{1... | collective-permute-start | bytes 2359304 | tf_op jit(solution)/shard_map/ppermute | solution.py:497
  115.2 21.9 %collective-permute-start.8 = (f32[4,128,384]{2,1,0:T(8,128)}, f32[4,128,384]{2,1,0:T(8,128)S(1)}, u32[]{:S(2)}, u32[]{:S(2)}) collective-permute-start(f32[4,128,384]{2,1,0:T(8,128)} %get-tuple-element.83.go_in), channel_id=1, source_target_pairs={{16,32},{32,16},{48,64},{64,48},{80,96},{96,80},{112,128},{128,112... | collective-permute-start | bytes 2359304 | tf_op jit(solution)/shard_map/ppermute | solution.py:493
  132.6 8.0 %copy-start.9 = (f32[4,128,384]{2,1,0:T(8,128)}, f32[4,128,384]{2,1,0:T(8,128)S(1)}, u32[]{:S(2)}) copy-start(f32[4,128,384]{2,1,0:T(8,128)S(1)} %collective-permute-done.7.even) | copy-start | bytes 2359300
  137.1 3.5 %copy-start.10 = (f32[4,128,384]{2,1,0:T(8,128)}, f32[4,128,384]{2,1,0:T(8,128)S(1)}, u32[]{:S(2)}) copy-start(f32[4,128,384]{2,1,0:T(8,128)S(1)} %collective-permute-done.8.odd) | copy-start | bytes 2359300
  137.1 3.5 %collective-permute-start.9 = (f32[576,128]{1,0:T(8,128)S(1)}, f32[576,128]{1,0:T(8,128)S(1)}, u32[]{:S(2)}, u32[]{:S(2)}) collective-permute-start(f32[576,128]{1,0:T(8,128)S(1)} %get-tuple-element.107.own), channel_id=1, source_target_pairs={{0,16},{16,0},{1,17},{17,1},{2,18},{18,2},{3,19},{19,3},{4,20},{20... | collective-permute-start | bytes 884744 | tf_op jit(solution)/shard_map/ppermute | solution.py:501
  140.6 0.7 copy-start.13
  150.7 33.8 %copy-start.1 = (f32[4,128,384]{2,1,0:T(8,128)S(1)}, f32[4,128,384]{2,1,0:T(8,128)}, u32[]{:S(2)}) copy-start(f32[4,128,384]{2,1,0:T(8,128)} %get-tuple-element.89.gc) | copy-start | bytes 2359300
  150.8 33.8 %copy-start.3 = (f32[4,128,256]{2,1,0:T(8,128)S(1)}, f32[4,128,256]{2,1,0:T(8,128)}, u32[]{:S(2)}) copy-start(f32[4,128,256]{2,1,0:T(8,128)} %get-tuple-element.88.oc) | copy-start | bytes 1572868
  150.8 33.8 %copy-start.7 = (s32[4]{0:T(128)S(1)}, s32[4]{0:T(128)}, u32[]{:S(2)}) copy-start(s32[4]{0:T(128)} %copy-done.6) | copy-start | bytes 52
  150.8 4.6 %collective-permute-start.10 = (f32[1344,128]{1,0:T(8,128)}, f32[1344,128]{1,0:T(8,128)S(1)}, u32[]{:S(2)}, u32[]{:S(2)}) collective-permute-start(f32[1344,128]{1,0:T(8,128)} %get-tuple-element.90), channel_id=1, source_target_pairs={{0,16},{16,0},{1,17},{17,1},{2,18},{18,2},{3,19},{19,3},{4,20},{20... | collective-permute-start | bytes 2064392 | tf_op jit(solution)/shard_map/ppermute | solution.py:501
  153.0 31.6 %collective-permute-start.11 = (f32[4,64,384]{2,1,0:T(8,128)}, f32[4,64,384]{2,1,0:T(8,128)S(1)}, u32[]{:S(2)}, u32[]{:S(2)}) collective-permute-start(f32[4,64,384]{2,1,0:T(8,128)} %get-tuple-element.92), channel_id=1, source_target_pairs={{16,32},{32,16},{48,64},{64,48},{80,96},{96,80},{112,128},{128,112... | collective-permute-start | bytes 1179656 | tf_op jit(solution)/shard_map/ppermute | solution.py:493
  185.4 29.1 %copy-start.2 = (f32[8,128,128]{2,1,0:T(8,128)S(1)}, f32[8,128,128]{2,1,0:T(8,128)}, u32[]{:S(2)}) copy-start(f32[8,128,128]{2,1,0:T(8,128)} %get-tuple-element.104.p) | copy-start | bytes 1572868
  185.4 21.5 %collective-permute-start.12 = (f32[2,128,128]{2,1,0:T(8,128)S(1)}, f32[2,128,128]{2,1,0:T(8,128)S(1)}, u32[]{:S(2)}, u32[]{:S(2)}) collective-permute-start(f32[2,128,128]{2,1,0:T(8,128)S(1)} %get-tuple-element.100), channel_id=1, source_target_pairs={{0,1},{1,0},{2,3},{3,2},{4,5},{5,4},{6,7},{7,6},{8,9},{9,8},{10,11... | collective-permute-start | bytes 393224 | tf_op jit(solution)/shard_map/ppermute | solution.py:497
  188.8 18.1 %collective-permute-start.13 = (f32[2,128,128]{2,1,0:T(8,128)S(1)}, f32[2,128,128]{2,1,0:T(8,128)S(1)}, u32[]{:S(2)}, u32[]{:S(2)}) collective-permute-start(f32[2,128,128]{2,1,0:T(8,128)S(1)} %get-tuple-element.101), channel_id=1, source_target_pairs={{1,2},{2,1},{3,4},{4,3},{5,6},{6,5},{7,8},{8,7},{9,10},{10,9},{11,... | collective-permute-start | bytes 393224 | tf_op jit(solution)/shard_map/ppermute | solution.py:493
  206.9 7.6 %collective-permute-start.14 = (f32[576,128]{1,0:T(8,128)S(1)}, f32[576,128]{1,0:T(8,128)S(1)}, u32[]{:S(2)}, u32[]{:S(2)}) collective-permute-start(f32[576,128]{1,0:T(8,128)S(1)} %get-tuple-element.109.own), channel_id=1, source_target_pairs={{0,16},{16,0},{1,17},{17,1},{2,18},{18,2},{3,19},{19,3},{4,20},{20... | collective-permute-start | bytes 884744 | tf_op jit(solution)/shard_map/ppermute | solution.py:501

commit v3 on v2

--- a/solution.py
+++ b/solution.py
@@ -242,19 +242,24 @@
 
 
 def first_kernel(
-    where, positions, counts, x, ce, co, even, odd, p_in, meas_in, blocks_in,
+    where, positions, counts, x, ce, co, ke, ko, even, odd, p_in, meas_in, blocks_in,
     e_out, g_out, me, mo, keep, give,
     e, p, meas, blocks, g, acc, a, b, sems, *s,
 ):
     up = where[2] == 0
     at = eight(jnp.where(up, H + TR, 0))
     below = eight(H + TR - at)
-    strips = [start(ce, a.at[0:2, 0:TR, :], sems.at[0]), start(co, b.at[0:2, 0:TR, :], sems.at[1])]
+    strips = [
+        start(ce, a.at[0:2, 0:TR, :], sems.at[0]),
+        start(co, b.at[0:2, 0:TR, :], sems.at[1]),
+        start(ke, a.at[0:2, TR : TR + H, :], sems.at[26]),
+        start(ko, b.at[0:2, TR : TR + H, :], sems.at[27]),
+    ]
     ins = [
         [
             start(x.at[k], e.at[k, H : H + TR, W:], sems.at[2 + k]),
             start(even.at[k], e.at[k, pl.ds(at, H), :], sems.at[6 + k]),
-            start(odd.at[k], e.at[k, pl.ds(below, H), :], sems.at[10 + k]),
+            start(odd.at[k], e.at[k, pl.ds(below, H), W:], sems.at[10 + k]),
         ]
         for k in range(4)
     ]
@@ -267,11 +272,12 @@
         if k == 0:
             done(strips)
         done(ins[k])
-        low = lanes((TR, W)) < H
         first = where[3] == 0
-        left_in = jnp.where(first, b[k // 2, 0:TR], a[k // 2, 0:TR])
-        right_in = jnp.where(first, a[k // 2, 0:TR], b[k // 2, 0:TR])
-        e[k, H : H + TR, 0:W] = widened(left_in, right_in, k % 2, low)
+        for src, dst, n in ((slice(0, TR), slice(H, H + TR), TR), (slice(TR, TR + H), pl.ds(below, H), H)):
+            va, vb = a[k // 2, src], b[k // 2, src]
+            left_in = jnp.where(first, vb, va)
+            right_in = jnp.where(first, va, vb)
+            e[k, dst, 0:W] = widened(left_in, right_in, k % 2, lanes((n, W)) < H)
 
     def whole():
         modes_copy.wait()
@@ -371,26 +377,30 @@
     return jnp.where(low, a, pltpu.roll(b, H, 1))
 
 
-def strips_kernel(where, x, even, odd):
+def strips_kernel(where, x, even, odd, rows_odd, corner_even, corner_odd):
     first = where[3] == 0
+    at = pl.ds(eight(jnp.where(where[2] == 0, 0, H)), H)
     for k in range(2):
         ml = pack(x[k, 0, :, 0:W], x[k, 1, :, 0:W], False)
         mr = pack(x[k, 0, :, W:], x[k, 1, :, W:], True)
         even[k] = jnp.where(first, mr, ml)
         odd[k] = jnp.where(first, ml, mr)
-
-
-def widen_kernel(where, x, even, odd, be, bo):
+        corner_even[k] = even[k, at]
+        corner_odd[k] = odd[k, at]
+        for j in range(2):
+            rows_odd[2 * k + j] = x[k, j, at]
+
+
+def widen_kernel(where, x, even, odd, out):
     low = lanes((H, W)) < H
     first = where[3] == 0
-    at = eight(jnp.where(where[2] == 0, H, 0))
-    for out, rows in ((be, pl.ds(at, H)), (bo, pl.ds(eight(H - at), H))):
-        for k in range(2):
-            left_in = jnp.where(first, odd[k, rows], even[k, rows])
-            right_in = jnp.where(first, even[k, rows], odd[k, rows])
-            for j in range(2):
-                out[2 * k + j, :, 0:W] = widened(left_in, right_in, j, low)
-                out[2 * k + j, :, W:] = x[k, j, rows]
+    rows = pl.ds(eight(jnp.where(where[2] == 0, H, 0)), H)
+    for k in range(2):
+        left_in = jnp.where(first, odd[k, rows], even[k, rows])
+        right_in = jnp.where(first, even[k, rows], odd[k, rows])
+        for j in range(2):
+            out[2 * k + j, :, 0:W] = widened(left_in, right_in, j, low)
+            out[2 * k + j, :, W:] = x[k, j, rows]
 
 
 def halves_kernel(where, g_in, even, odd, ge, go, g, a, b, sems):
@@ -484,17 +494,32 @@
         in_specs=[SM] * len(smem) + [spec] * len(args),
         out_specs=[spec] * len(outs),
         scratch_shapes=list(scratch),
-        compiler_params=pltpu.CompilerParams(vmem_limit_bytes=(63 if big else 12) * 1024 * 1024),
+        compiler_params=pltpu.CompilerParams(vmem_limit_bytes=(52 if big else 12) * 1024 * 1024),
         cost_estimate=cost,
     )(*smem, *args)
 
 
+def even_partner(i):
+    return i ^ 1
+
+
+def odd_partner(i):
+    return ((i + 1) ^ 1) - 1
+
+
 def odd_swap(odd, axes, size):
-    return lax.ppermute(odd, axes, [(i, ((i + 1) ^ 1) - 1) for i in range(1, size - 1)])
+    return lax.ppermute(odd, axes, [(i, odd_partner(i)) for i in range(1, size - 1)])
 
 
 def swap(even, odd, axes, size):
-    return lax.ppermute(even, axes, [(i, i ^ 1) for i in range(size)]), odd_swap(odd, axes, size)
+    return lax.ppermute(even, axes, [(i, even_partner(i)) for i in range(size)]), odd_swap(odd, axes, size)
+
+
+def corner_swap(v, partner, skip):
+    pairs = [
+        (16 * i + j, 16 * odd_partner(i) + partner(j)) for i in range(1, 31) for j in range(skip, 16 - skip)
+    ]
+    return lax.ppermute(v, ROW + COL, pairs)
 
 
 def other_core(v):
@@ -553,15 +578,21 @@
         vm(2, F, W, W),
     ]
 
-    me, mo = call(strips_kernel, [sds(2, TR, W)] * 2, (where,), (objects,))
+    me, mo, rows_odd, ke, ko = call(
+        strips_kernel, [sds(2, TR, W)] * 2 + [sds(4, H, TC)] + [sds(2, H, W)] * 2, (where,), (objects,)
+    )
     ce, co = swap(me, mo, COL, 16)
-    be, bo = call(widen_kernel, [sds(4, H, EC), sds(4, H, EC)], (where,), (objects, ce, co))
-    re, ro = swap(be, bo, ROW, 32)
+    ro = odd_swap(rows_odd, ROW, 32)
+    ke = corner_swap(ke, even_partner, 0)
+    ko = corner_swap(ko, odd_partner, 1)
+    ce, co, ro, ke, ko = lax.optimization_barrier((ce, co, ro, ke, ko))
+    (be,) = call(widen_kernel, [sds(4, H, EC)], (where,), (objects, ce, co))
+    re = lax.ppermute(be, ROW, [(i, even_partner(i)) for i in range(32)])
     e, g, me, mo, keep, give = call(
         first_kernel,
         [sds(4, 256, EC), sds(4, 256, EC), sds(4, 256, W), sds(4, 256, W), sds(HALF, W), sds(HALF, W)],
-        info, (objects.reshape(4, TR, TC), ce, co, re, ro, modes, measured, blocks),
-        shared + [vm(4, 256, W), vm(4, 256, W), sem(26)] + scratch, cost=ITER_COST, big=True,
+        info, (objects.reshape(4, TR, TC), ce, co, ke, ko, re, ro, modes, measured, blocks),
+        shared + [vm(4, 256, W), vm(4, 256, W), sem(28)] + scratch, cost=ITER_COST, big=True,
     )
 
     got = other_core(give)

time: 217 us -> 215 us (level)
  waiting for transfers between devices: 17.7 us -> 4.52 us
  starting transfers between devices: 53.2 us -> 60 us
  blocking collectives: 109 us -> 114 us
  local copies, waits for them, and re-layouts: 3.72 us -> 1.46 us
    ppermute x11 -> x13, waiting for transfers between devices: 14.6 us -> 2.33 us  [the longest x2 1.26 us: corner_swap(): return lax.ppermute(v, ROW + COL, pairs)]
    all_to_all x2, blocking collectives: 41.4 us -> 45.7 us  [scatter_sum(): v = lax.all_to_all(v.reshape(n, 1, -1), axes, 0, 0, tiled=True)]
    ppermute x4, starting transfers between devices: 12.3 us -> 16.3 us  [other_core(): return lax.ppermute(v, 'c', [(0, 1), (1, 0)])]
    ppermute x11 -> x13, starting transfers between devices: 40.9 us -> 43.7 us  [the longest x4 22 us: swap(): lax.ppermute(even, axes, [(i, even_partner(i)) for i in range(size)])]
    unnamed x28 -> x14, local copies, waits for them, and re-layouts: 3.33 us -> 1.07 us
  transfers between devices with their start and end apart: 15 -> 17, of which waited for: 5 -> 4; matrix products, arithmetic and copies ran while one was open for 0% -> 0% of each run, Pallas kernels for 1% -> 1%
where the time goes in v3:
time: 215 us; the launch traced here: 214 us
  blocking collectives  114 us (53%)
  starting transfers between devices  60 us (28%)
  Pallas kernels  31.3 us (15%)
  waiting for transfers between devices  4.52 us (2%)
    all_to_all x4, blocking collectives, spread(): return lax.all_to_all(w, axes, 0, 0, tiled=True)  68.6 us
    all_to_all x2, blocking collectives, scatter_sum(): v = lax.all_to_all(v.reshape(n, 1, -1), axes, 0, 0, tiled=True)  45.7 us
    pallas_call x8, Pallas kernels, call(): pl.pallas_call(kernel, out_shape=outs, in_specs=[SM] * len(smem) + [spec]...  31.3 us
    ppermute x4, starting transfers between devices, swap(): lax.ppermute(even, axes, [(i, even_partner(i)) for i in range(size)])  22 us
    ppermute x4, starting transfers between devices, other_core(): return lax.ppermute(v, 'c', [(0, 1), (1, 0)])  16.3 us
    ppermute x6, starting transfers between devices, odd_swap(): lax.ppermute(odd, axes, [(i, odd_partner(i)) for i in range(1, size - 1)])  11.5 us
    ppermute x2, starting transfers between devices, corner_swap(): return lax.ppermute(v, ROW + COL, pairs)  8.29 us
  transfers between devices with their start and end apart: 17, of which 4 were waited for; matrix products, arithmetic and copies ran while one was open for 0% of the time, Pallas kernels for 1%

profile of v3, /device:TPU:1, one launch (start us, length us, event | category | flops | bytes accessed | tf_op | source)
XLA Modules:
  0.0 213.8 jit_solution(9416670865773503025)
XLA Ops:
  0.6 0.0 copy-start.5
  0.7 0.1 pad_add_fusion.where
  0.7 1.0 copy-done
  1.8 0.7 shard_map.77
  2.5 4.6 %collective-permute-start.2 = (f32[4,64,256]{2,1,0:T(8,128)S(1)}, f32[4,64,256]{2,1,0:T(8,128)S(1)}, u32[]{:S(2)}, u32[]{:S(2)}) collective-permute-start(f32[4,64,256]{2,1,0:T(8,128)S(1)} %get-tuple-element.75), channel_id=1, source_target_pairs={{16,32},{32,16},{48,64},{64,48},{80,96},{96,80},{112,128},{128,112... | collective-permute-start | bytes 786440 | tf_op jit(solution)/shard_map/ppermute | solution.py:511
  7.1 4.0 %collective-permute-start = (f32[2,128,128]{2,1,0:T(8,128)S(1)}, f32[2,128,128]{2,1,0:T(8,128)S(1)}, u32[]{:S(2)}, u32[]{:S(2)}) collective-permute-start(f32[2,128,128]{2,1,0:T(8,128)S(1)} %get-tuple-element.73), channel_id=1, source_target_pairs={{0,1},{1,0},{2,3},{3,2},{4,5},{5,4},{6,7},{7,6},{8,9},{9,8},{10,11... | collective-permute-start | bytes 393224 | tf_op jit(solution)/shard_map/ppermute | solution.py:515
  11.1 0.7 collective-permute-start.1
  11.8 7.6 %collective-permute-start.3 = (f32[2,64,128]{2,1,0:T(8,128)S(1)}, f32[2,64,128]{2,1,0:T(8,128)S(1)}, u32[]{:S(2)}, u32[]{:S(2)}) collective-permute-start(f32[2,64,128]{2,1,0:T(8,128)S(1)} %get-tuple-element.76), channel_id=1, source_target_pairs={{16,33},{17,32},{18,35},{19,34},{20,37},{21,36},{22,39},{23,38},{2... | collective-permute-start | bytes 196616 | tf_op jit(solution)/shard_map/ppermute | solution.py:522
  19.4 0.7 collective-permute-start.4
  20.1 1.3 collective-permute-done.3.ke
  21.3 0.0 collective-permute-done.4.ko
  21.3 0.0 collective-permute-done.even.ce
  21.3 0.0 collective-permute-done.1.odd.co
  21.3 0.0 collective-permute-done.2.odd
  21.3 0.7 shard_map.78
  22.0 1.9 collective-permute-start.5
  24.6 1.0 collective-permute-done.5.even
  25.6 0.0 copy-done.6
  25.6 12.2 %shard_map.79 = (f32[4,256,384]{2,1,0:T(8,128)}, f32[4,256,384]{2,1,0:T(8,128)}, f32[4,256,128]{2,1,0:T(8,128)}, f32[4,256,128]{2,1,0:T(8,128)}, f32[576,128]{1,0:T(8,128)S(1)}, /*index=5*/f32[576,128]{1,0:T(8,128)S(1)}) custom-call(s32[4]{0:T(128)S(1)} %pad_add_fusion.where, s32[1,1,2,2]{3,2,1,0:T(2,128)S(1)} %copy-done.5, s32[1,1]{1,0:T(1,128)S(6)} %copy.20.counts, ...), custom_call_target="tpu_custom_call" | custom-call | flops 10000000000 | bytes 8000000 | tf_op jit(solution)/shard_map/pallas_call | solution.py:491
  37.9 9.2 %collective-permute-start.7 = (f32[4,256,128]{2,1,0:T(8,128)}, f32[4,256,128]{2,1,0:T(8,128)S(1)}, u32[]{:S(2)}, u32[]{:S(2)}) collective-permute-start(f32[4,256,128]{2,1,0:T(8,128)} %get-tuple-element.86), channel_id=1, source_target_pairs={{0,1},{1,0},{2,3},{3,2},{4,5},{5,4},{6,7},{7,6},{8,9},{9,8},{10,11... | collective-permute-start | bytes 1572872 | tf_op jit(solution)/shard_map/ppermute | solution.py:515
  47.1 0.7 collective-permute-start.8
  47.8 2.3 %collective-permute-start.6 = (f32[576,128]{1,0:T(8,128)S(1)}, f32[576,128]{1,0:T(8,128)S(1)}, u32[]{:S(2)}, u32[]{:S(2)}) collective-permute-start(f32[576,128]{1,0:T(8,128)S(1)} %get-tuple-element.85), channel_id=1, source_target_pairs={{0,16},{16,0},{1,17},{17,1},{2,18},{18,2},{3,19},{19,3},{4,20},{20... | collective-permute-start | bytes 884744 | tf_op jit(solution)/shard_map/ppermute | solution.py:526
  50.1 1.2 collective-permute-done.6
  51.3 46.4 %conditional.4 = (f32[2304]{0:T(1024)S(1)}) conditional(s32[]{:T(128)} %bitcast.11, () %tuple.40, (f32[576,128]{1,0:T(8,128)S(1)}, f32[576,128]{1,0:T(8,128)S(1)}) %tuple.41), branch_computations={%region_0.1_spmd, %region_1.4_spmd} | conditional | flops 161280 | bytes 2092048 | solution.py:540
  51.4 29.8 %all_to_all.24 = f32[32,1,2304]{2,1,0:T(1,128)S(1)} all-to-all(f32[32,1,2304]{2,1,0:T(1,128)S(1)} %bitcast.16), channel_id=1, replica_groups=mesh['x'=4,'yl'=4,'c'=2,'yh'=2,'z'=8] {'x','z'}, dimensions={0} | all-to-all | bytes 589824 | tf_op jit(solution)/shard_map/cond/branch_1_fun/all_to_all | solution.py:530
  81.1 0.2 reduce_sum.32
  81.4 16.3 %all_to_all.25 = f32[8,1,2304]{2,1,0:T(1,128)S(1)} all-to-all(f32[8,1,2304]{2,1,0:T(1,128)S(1)} %broadcast_in_dim.8), channel_id=1, replica_groups=mesh['x'=4,'yl'=4,'c'=2,'yh'=2,'z'=8] {'yh','yl'}, dimensions={0} | all-to-all | bytes 147456 | tf_op jit(solution)/shard_map/cond/branch_1_fun/all_to_all | solution.py:536
  97.7 0.1 reduce_sum.33
  97.7 0.0 collective-permute-done.7.even
  97.8 0.0 collective-permute-done.8.odd
  97.8 3.9 %shard_map.80 = (f32[4,128,384]{2,1,0:T(8,128)S(1)}, f32[4,128,384]{2,1,0:T(8,128)}) custom-call(s32[4]{0:T(128)S(1)} %pad_add_fusion.where, f32[4,256,384]{2,1,0:T(8,128)} %get-tuple-element.89.g_in, f32[4,256,128]{2,1,0:T(8,128)S(1)} %collective-permute-done.7.even, f32[4,256,128]{2,1,0:T(8,128)S(1)} %collective-permute-done.8.odd), custom_call_target="tpu_custom_call" | custom-call | tf_op jit(solution)/shard_map/pallas_call | solution.py:491
  101.7 4.6 %collective-permute-start.9 = (f32[4,128,384]{2,1,0:T(8,128)S(1)}, f32[4,128,384]{2,1,0:T(8,128)}, u32[]{:S(2)}, u32[]{:S(2)}) collective-permute-start(f32[4,128,384]{2,1,0:T(8,128)S(1)} %get-tuple-element.94.ge_in), channel_id=1, source_target_pairs={{0,16},{16,0},{32,48},{48,32},{64,80},{80,64},{96,112},{112,96},{1... | collective-permute-start | bytes 2359304 | tf_op jit(solution)/shard_map/ppermute | solution.py:515
  106.4 2.1 collective-permute-start.10
  108.5 20.9 %conditional.5 = (f32[576,128]{1,0:T(8,128)S(1)}) conditional(s32[]{:T(128)} %bitcast.11, () %tuple.44, f32[2304]{0:T(1024)S(1)} %get-tuple-element.118), branch_computations={%region_4.5_spmd, %region_5.6_spmd} | conditional | bytes 893960 | solution.py:540
  108.5 0.2 broadcast_in_dim.9
  108.7 20.7 %all_to_all.26 = f32[32,1,2304]{2,1,0:T(1,128)S(1)} all-to-all(f32[32,1,2304]{2,1,0:T(1,128)S(1)} %broadcast_in_dim.9), channel_id=1, replica_groups=mesh['x'=4,'yl'=4,'c'=2,'yh'=2,'z'=8] {'x','z'}, dimensions={0} | all-to-all | bytes 589824 | tf_op jit(solution)/shard_map/cond/branch_1_fun/all_to_all | solution.py:536
  129.3 0.0 collective-permute-done.9.even
  129.3 0.0 collective-permute-done.10.odd
  129.3 4.4 %collective-permute-start.11 = (f32[576,128]{1,0:T(8,128)S(1)}, f32[576,128]{1,0:T(8,128)S(1)}, u32[]{:S(2)}, u32[]{:S(2)}) collective-permute-start(f32[576,128]{1,0:T(8,128)S(1)} %get-tuple-element.119.own), channel_id=1, source_target_pairs={{0,16},{16,0},{1,17},{17,1},{2,18},{18,2},{3,19},{19,3},{4,20},{20... | collective-permute-start | bytes 884744 | tf_op jit(solution)/shard_map/ppermute | solution.py:526
  133.7 1.0 collective-permute-done.11.other
  134.8 10.1 %shard_map.81 = (f32[4,128,256]{2,1,0:T(8,128)S(1)}, f32[4,128,384]{2,1,0:T(8,128)}, f32[1344,128]{1,0:T(8,128)}, f32[4,64,384]{2,1,0:T(8,128)S(1)}, f32[576,128]{1,0:T(8,128)S(1)}, /*index=5*/f32[8,128,128]{2,1,0:T(8,128)}) custom-call(s32[4]{0:T(128)S(1)} %pad_add_fusion.where, s32[1,1,2,2]{3,2,1,0:T(2,128)S(1)} %copy-done.5, s32[1,1]{1,0:T(1,128)S(6)} %copy.20.counts, ...), custom_call_target="tpu_custom_call" | custom-call | flops 10000000000 | bytes 8000000 | tf_op jit(solution)/shard_map/pallas_call | solution.py:491
  144.9 2.4 %collective-permute-start.12 = (f32[1344,128]{1,0:T(8,128)}, f32[1344,128]{1,0:T(8,128)S(1)}, u32[]{:S(2)}, u32[]{:S(2)}) collective-permute-start(f32[1344,128]{1,0:T(8,128)} %get-tuple-element.102), channel_id=1, source_target_pairs={{0,16},{16,0},{1,17},{17,1},{2,18},{18,2},{3,19},{19,3},{4,20},{20... | collective-permute-start | bytes 2064392 | tf_op jit(solution)/shard_map/ppermute | solution.py:526
  147.3 2.8 %collective-permute-start.13 = (f32[4,64,384]{2,1,0:T(8,128)S(1)}, f32[4,64,384]{2,1,0:T(8,128)S(1)}, u32[]{:S(2)}, u32[]{:S(2)}) collective-permute-start(f32[4,64,384]{2,1,0:T(8,128)S(1)} %get-tuple-element.104), channel_id=1, source_target_pairs={{16,32},{32,16},{48,64},{64,48},{80,96},{96,80},{112,128},{128,112... | collective-permute-start | bytes 1179656 | tf_op jit(solution)/shard_map/ppermute | solution.py:511
  150.0 0.0 collective-permute-done.12.even
  150.0 30.5 %conditional.6 = (f32[2304]{0:T(1024)S(1)}) conditional(s32[]{:T(128)} %bitcast.11, () %tuple.46, (f32[1344,128]{1,0:T(8,128)S(1)}, f32[576,128]{1,0:T(8,128)S(1)}) %tuple.47), branch_computations={%region_6.7_spmd, %region_7.10_spmd} | conditional | flops 161280 | bytes 2092048 | solution.py:540
  150.1 15.9 %all_to_all.27 = f32[32,1,2304]{2,1,0:T(1,128)S(1)} all-to-all(f32[32,1,2304]{2,1,0:T(1,128)S(1)} %bitcast.17), channel_id=1, replica_groups=mesh['x'=4,'yl'=4,'c'=2,'yh'=2,'z'=8] {'x','z'}, dimensions={0} | all-to-all | bytes 589824 | tf_op jit(solution)/shard_map/cond/branch_1_fun/all_to_all | solution.py:530
  166.0 0.2 reduce_sum.34
  166.3 14.2 %all_to_all.28 = f32[8,1,2304]{2,1,0:T(1,128)S(1)} all-to-all(f32[8,1,2304]{2,1,0:T(1,128)S(1)} %broadcast_in_dim.10), channel_id=1, replica_groups=mesh['x'=4,'yl'=4,'c'=2,'yh'=2,'z'=8] {'yh','yl'}, dimensions={0} | all-to-all | bytes 147456 | tf_op jit(solution)/shard_map/cond/branch_1_fun/all_to_all | solution.py:536
  180.5 0.1 reduce_sum.35
  180.6 0.0 collective-permute-done.13.odd
  180.6 0.8 shard_map.82
  181.4 0.0 copy-start.2
  181.4 4.1 %collective-permute-start.14 = (f32[2,128,128]{2,1,0:T(8,128)S(1)}, f32[2,128,128]{2,1,0:T(8,128)S(1)}, u32[]{:S(2)}, u32[]{:S(2)}) collective-permute-start(f32[2,128,128]{2,1,0:T(8,128)S(1)} %get-tuple-element.112), channel_id=1, source_target_pairs={{0,1},{1,0},{2,3},{3,2},{4,5},{5,4},{6,7},{7,6},{8,9},{9,8},{10,11... | collective-permute-start | bytes 393224 | tf_op jit(solution)/shard_map/ppermute | solution.py:515
  185.5 0.7 collective-permute-start.15
  186.2 17.5 %conditional.7 = (f32[576,128]{1,0:T(8,128)S(1)}) conditional(s32[]{:T(128)} %bitcast.11, () %tuple.49, f32[2304]{0:T(1024)S(1)} %get-tuple-element.120), branch_computations={%region_10.11_spmd, %region_11.12_spmd} | conditional | bytes 893960 | solution.py:540
  186.2 0.2 broadcast_in_dim.11
  186.4 17.3 %all_to_all.29 = f32[32,1,2304]{2,1,0:T(1,128)S(1)} all-to-all(f32[32,1,2304]{2,1,0:T(1,128)S(1)} %broadcast_in_dim.11), channel_id=1, replica_groups=mesh['x'=4,'yl'=4,'c'=2,'yh'=2,'z'=8] {'x','z'}, dimensions={0} | all-to-all | bytes 589824 | tf_op jit(solution)/shard_map/cond/branch_1_fun/all_to_all | solution.py:536
  203.7 0.0 collective-permute-done.14.even
  203.7 0.0 collective-permute-done.15.odd
  203.7 7.2 %collective-permute-start.16 = (f32[576,128]{1,0:T(8,128)S(1)}, f32[576,128]{1,0:T(8,128)S(1)}, u32[]{:S(2)}, u32[]{:S(2)}) collective-permute-start(f32[576,128]{1,0:T(8,128)S(1)} %get-tuple-element.121.own), channel_id=1, source_target_pairs={{0,16},{16,0},{1,17},{17,1},{2,18},{18,2},{3,19},{19,3},{4,20},{20... | collective-permute-start | bytes 884744 | tf_op jit(solution)/shard_map/ppermute | solution.py:526
  210.9 1.5 shard_map.83
  212.4 0.0 collective-permute-done.16.other
  212.4 0.0 copy-done.2
  212.4 1.5 shard_map.84
  (13 shorter events, 0.2 us)
Async XLA Ops:
  0.6 25.0 %copy-start.5 = (s32[1,1,2,2]{3,2,1,0:T(2,128)S(1)}, s32[1,1,2,2]{3,2,1,0:T(2,128)}, u32[]{:S(2)}) copy-start(s32[1,1,2,2]{3,2,1,0:T(2,128)} %positions.3) | copy-start | bytes 52
  0.7 1.0 copy-start
  1.8 23.9 %copy-start.4 = (f32[1,1,2,128,128]{4,3,2,1,0:T(8,128)S(1)}, f32[1,1,2,128,128]{4,3,2,1,0:T(8,128)}, u32[]{:S(2)}) copy-start(f32[1,1,2,128,128]{4,3,2,1,0:T(8,128)} %param.16) | copy-start | bytes 393220
  1.8 23.9 %copy-start.6 = (bf16[2,3,2,128,128]{4,3,2,1,0:T(8,128)(2,1)S(1)}, bf16[2,3,2,128,128]{4,3,2,1,0:T(8,128)(2,1)}, u32[]{:S(2)}) copy-start(bf16[2,3,2,128,128]{4,3,2,1,0:T(8,128)(2,1)} %constant.57.clone.blocks_in) | copy-start | bytes 1179652
  2.5 18.9 %collective-permute-start.2 = (f32[4,64,256]{2,1,0:T(8,128)S(1)}, f32[4,64,256]{2,1,0:T(8,128)S(1)}, u32[]{:S(2)}, u32[]{:S(2)}) collective-permute-start(f32[4,64,256]{2,1,0:T(8,128)S(1)} %get-tuple-element.75), channel_id=1, source_target_pairs={{16,32},{32,16},{48,64},{64,48},{80,96},{96,80},{112,128},{128,112... | collective-permute-start | bytes 786440 | tf_op jit(solution)/shard_map/ppermute | solution.py:511
  7.1 14.3 %collective-permute-start = (f32[2,128,128]{2,1,0:T(8,128)S(1)}, f32[2,128,128]{2,1,0:T(8,128)S(1)}, u32[]{:S(2)}, u32[]{:S(2)}) collective-permute-start(f32[2,128,128]{2,1,0:T(8,128)S(1)} %get-tuple-element.73), channel_id=1, source_target_pairs={{0,1},{1,0},{2,3},{3,2},{4,5},{5,4},{6,7},{7,6},{8,9},{9,8},{10,11... | collective-permute-start | bytes 393224 | tf_op jit(solution)/shard_map/ppermute | solution.py:515
  11.1 10.2 %collective-permute-start.1 = (f32[2,128,128]{2,1,0:T(8,128)S(1)}, f32[2,128,128]{2,1,0:T(8,128)S(1)}, u32[]{:S(2)}, u32[]{:S(2)}) collective-permute-start(f32[2,128,128]{2,1,0:T(8,128)S(1)} %get-tuple-element.74), channel_id=1, source_target_pairs={{1,2},{2,1},{3,4},{4,3},{5,6},{6,5},{7,8},{8,7},{9,10},{10,9},{11,... | collective-permute-start | bytes 393224 | tf_op jit(solution)/shard_map/ppermute | solution.py:511
  11.8 9.6 %collective-permute-start.3 = (f32[2,64,128]{2,1,0:T(8,128)S(1)}, f32[2,64,128]{2,1,0:T(8,128)S(1)}, u32[]{:S(2)}, u32[]{:S(2)}) collective-permute-start(f32[2,64,128]{2,1,0:T(8,128)S(1)} %get-tuple-element.76), channel_id=1, source_target_pairs={{16,33},{17,32},{18,35},{19,34},{20,37},{21,36},{22,39},{23,38},{2... | collective-permute-start | bytes 196616 | tf_op jit(solution)/shard_map/ppermute | solution.py:522
  19.4 1.9 collective-permute-start.4
  22.0 3.6 %collective-permute-start.5 = (f32[4,64,384]{2,1,0:T(8,128)S(1)}, f32[4,64,384]{2,1,0:T(8,128)S(1)}, u32[]{:S(2)}, u32[]{:S(2)}) collective-permute-start(f32[4,64,384]{2,1,0:T(8,128)S(1)} %shard_map.78), channel_id=1, source_target_pairs={{0,16},{16,0},{32,48},{48,32},{64,80},{80,64},{96,112},{112,96},{1... | collective-permute-start | bytes 1179656 | tf_op jit(solution)/shard_map/ppermute | solution.py:590
  37.9 59.9 %collective-permute-start.7 = (f32[4,256,128]{2,1,0:T(8,128)}, f32[4,256,128]{2,1,0:T(8,128)S(1)}, u32[]{:S(2)}, u32[]{:S(2)}) collective-permute-start(f32[4,256,128]{2,1,0:T(8,128)} %get-tuple-element.86), channel_id=1, source_target_pairs={{0,1},{1,0},{2,3},{3,2},{4,5},{5,4},{6,7},{7,6},{8,9},{9,8},{10,11... | collective-permute-start | bytes 1572872 | tf_op jit(solution)/shard_map/ppermute | solution.py:515
  47.1 50.7 %collective-permute-start.8 = (f32[4,256,128]{2,1,0:T(8,128)}, f32[4,256,128]{2,1,0:T(8,128)S(1)}, u32[]{:S(2)}, u32[]{:S(2)}) collective-permute-start(f32[4,256,128]{2,1,0:T(8,128)} %get-tuple-element.87), channel_id=1, source_target_pairs={{1,2},{2,1},{3,4},{4,3},{5,6},{6,5},{7,8},{8,7},{9,10},{10,9},{11,... | collective-permute-start | bytes 1572872 | tf_op jit(solution)/shard_map/ppermute | solution.py:511
  47.8 3.5 %collective-permute-start.6 = (f32[576,128]{1,0:T(8,128)S(1)}, f32[576,128]{1,0:T(8,128)S(1)}, u32[]{:S(2)}, u32[]{:S(2)}) collective-permute-start(f32[576,128]{1,0:T(8,128)S(1)} %get-tuple-element.85), channel_id=1, source_target_pairs={{0,16},{16,0},{1,17},{17,1},{2,18},{18,2},{3,19},{19,3},{4,20},{20... | collective-permute-start | bytes 884744 | tf_op jit(solution)/shard_map/ppermute | solution.py:526
  101.7 33.1 %copy-start.3 = (f32[4,128,384]{2,1,0:T(8,128)}, f32[4,128,384]{2,1,0:T(8,128)S(1)}, u32[]{:S(2)}) copy-start(f32[4,128,384]{2,1,0:T(8,128)S(1)} %get-tuple-element.94.ge_in) | copy-start | bytes 2359300
  101.7 27.6 %collective-permute-start.9 = (f32[4,128,384]{2,1,0:T(8,128)S(1)}, f32[4,128,384]{2,1,0:T(8,128)}, u32[]{:S(2)}, u32[]{:S(2)}) collective-permute-start(f32[4,128,384]{2,1,0:T(8,128)S(1)} %get-tuple-element.94.ge_in), channel_id=1, source_target_pairs={{0,16},{16,0},{32,48},{48,32},{64,80},{80,64},{96,112},{112,96},{1... | collective-permute-start | bytes 2359304 | tf_op jit(solution)/shard_map/ppermute | solution.py:515
  106.4 23.0 %collective-permute-start.10 = (f32[4,128,384]{2,1,0:T(8,128)}, f32[4,128,384]{2,1,0:T(8,128)}, u32[]{:S(2)}, u32[]{:S(2)}) collective-permute-start(f32[4,128,384]{2,1,0:T(8,128)} %get-tuple-element.95.go_in), channel_id=1, source_target_pairs={{16,32},{32,16},{48,64},{64,48},{80,96},{96,80},{112,128},{128,112... | collective-permute-start | bytes 2359304 | tf_op jit(solution)/shard_map/ppermute | solution.py:511
  129.3 5.4 %collective-permute-start.11 = (f32[576,128]{1,0:T(8,128)S(1)}, f32[576,128]{1,0:T(8,128)S(1)}, u32[]{:S(2)}, u32[]{:S(2)}) collective-permute-start(f32[576,128]{1,0:T(8,128)S(1)} %get-tuple-element.119.own), channel_id=1, source_target_pairs={{0,16},{16,0},{1,17},{17,1},{2,18},{18,2},{3,19},{19,3},{4,20},{20... | collective-permute-start | bytes 884744 | tf_op jit(solution)/shard_map/ppermute | solution.py:526
  144.8 35.7 %copy-start.1 = (f32[4,128,384]{2,1,0:T(8,128)S(1)}, f32[4,128,384]{2,1,0:T(8,128)}, u32[]{:S(2)}) copy-start(f32[4,128,384]{2,1,0:T(8,128)} %get-tuple-element.101.gc) | copy-start | bytes 2359300
  144.9 5.2 %collective-permute-start.12 = (f32[1344,128]{1,0:T(8,128)}, f32[1344,128]{1,0:T(8,128)S(1)}, u32[]{:S(2)}, u32[]{:S(2)}) collective-permute-start(f32[1344,128]{1,0:T(8,128)} %get-tuple-element.102), channel_id=1, source_target_pairs={{0,16},{16,0},{1,17},{17,1},{2,18},{18,2},{3,19},{19,3},{4,20},{20... | collective-permute-start | bytes 2064392 | tf_op jit(solution)/shard_map/ppermute | solution.py:526
  147.3 33.3 %collective-permute-start.13 = (f32[4,64,384]{2,1,0:T(8,128)S(1)}, f32[4,64,384]{2,1,0:T(8,128)S(1)}, u32[]{:S(2)}, u32[]{:S(2)}) collective-permute-start(f32[4,64,384]{2,1,0:T(8,128)S(1)} %get-tuple-element.104), channel_id=1, source_target_pairs={{16,32},{32,16},{48,64},{64,48},{80,96},{96,80},{112,128},{128,112... | collective-permute-start | bytes 1179656 | tf_op jit(solution)/shard_map/ppermute | solution.py:511
  181.4 31.0 %copy-start.2 = (f32[8,128,128]{2,1,0:T(8,128)S(1)}, f32[8,128,128]{2,1,0:T(8,128)}, u32[]{:S(2)}) copy-start(f32[8,128,128]{2,1,0:T(8,128)} %get-tuple-element.116.p) | copy-start | bytes 1572868
  181.4 22.3 %collective-permute-start.14 = (f32[2,128,128]{2,1,0:T(8,128)S(1)}, f32[2,128,128]{2,1,0:T(8,128)S(1)}, u32[]{:S(2)}, u32[]{:S(2)}) collective-permute-start(f32[2,128,128]{2,1,0:T(8,128)S(1)} %get-tuple-element.112), channel_id=1, source_target_pairs={{0,1},{1,0},{2,3},{3,2},{4,5},{5,4},{6,7},{7,6},{8,9},{9,8},{10,11... | collective-permute-start | bytes 393224 | tf_op jit(solution)/shard_map/ppermute | solution.py:515
  185.5 18.2 %collective-permute-start.15 = (f32[2,128,128]{2,1,0:T(8,128)S(1)}, f32[2,128,128]{2,1,0:T(8,128)S(1)}, u32[]{:S(2)}, u32[]{:S(2)}) collective-permute-start(f32[2,128,128]{2,1,0:T(8,128)S(1)} %get-tuple-element.113), channel_id=1, source_target_pairs={{1,2},{2,1},{3,4},{4,3},{5,6},{6,5},{7,8},{8,7},{9,10},{10,9},{11,... | collective-permute-start | bytes 393224 | tf_op jit(solution)/shard_map/ppermute | solution.py:511
  203.7 8.7 %collective-permute-start.16 = (f32[576,128]{1,0:T(8,128)S(1)}, f32[576,128]{1,0:T(8,128)S(1)}, u32[]{:S(2)}, u32[]{:S(2)}) collective-permute-start(f32[576,128]{1,0:T(8,128)S(1)} %get-tuple-element.121.own), channel_id=1, source_target_pairs={{0,16},{16,0},{1,17},{17,1},{2,18},{18,2},{3,19},{19,3},{4,20},{20... | collective-permute-start | bytes 884744 | tf_op jit(solution)/shard_map/ppermute | solution.py:526

commit v4 on v3

--- a/solution.py
+++ b/solution.py
@@ -403,29 +403,17 @@
             out[2 * k + j, :, W:] = x[k, j, rows]
 
 
-def halves_kernel(where, g_in, even, odd, ge, go, g, a, b, sems):
-    ins = [
-        [
-            start(g_in.at[k], g.at[k], sems.at[3 * k]),
-            start(even.at[k], a.at[k], sems.at[3 * k + 1]),
-            start(odd.at[k], b.at[k], sems.at[3 * k + 2]),
-        ]
-        for k in range(4)
-    ]
-    low = lanes((256, W)) < H
+def halves_kernel(where, g, even, odd, ge, go):
+    low = lanes((TR, W)) < H
     first = where[3] == 0
     at = eight(jnp.where(where[2] == 0, TR, 0))
-    outs = []
-    for k in range(4):
-        done(ins[k])
-        rl = jnp.where(first, b[k], a[k])
-        rr = jnp.where(first, a[k], b[k])
-        g[k, :, 0:W] = g[k, :, 0:W] + jnp.where(low, rr, rl)
-        g[k, :, W : 2 * W] = g[k, :, W : 2 * W] + jnp.where(low, rl, 0.0)
-        g[k, :, 2 * W :] = g[k, :, 2 * W :] + jnp.where(low, 0.0, rr)
-        outs.append(start(g.at[k, pl.ds(at, TR), :], ge.at[k], sems.at[12 + 2 * k]))
-        outs.append(start(g.at[k, pl.ds(eight(TR - at), TR), :], go.at[k], sems.at[13 + 2 * k]))
-    done(outs)
+    for out, rows in ((ge, pl.ds(at, TR)), (go, pl.ds(eight(TR - at), TR))):
+        for k in range(4):
+            rl = jnp.where(first, odd[k, rows], even[k, rows])
+            rr = jnp.where(first, even[k, rows], odd[k, rows])
+            out[k, :, 0:W] = g[k, rows, 0:W] + jnp.where(low, rr, rl)
+            out[k, :, W : 2 * W] = g[k, rows, W : 2 * W] + jnp.where(low, rl, 0.0)
+            out[k, :, 2 * W :] = g[k, rows, 2 * W :] + jnp.where(low, 0.0, rr)
 
 
 def fold_kernel(where, oc, gc, even, odd, t, me, mo, r):
@@ -599,10 +587,7 @@
     ce, co = swap(me, mo, COL, 16)
     v = reduce_out(yes, keep, got)
     v, ce, co = lax.optimization_barrier((v, ce, co))
-    ge, go = call(
-        halves_kernel, [sds(4, TR, EC), sds(4, TR, EC)], (where,), (g, ce, co),
-        [vm(4, 256, EC), vm(4, 256, W), vm(4, 256, W), sem(20)], big=True,
-    )
+    ge, go = call(halves_kernel, [sds(4, TR, EC), sds(4, TR, EC)], (where,), (g, ce, co))
     v, ge, go = lax.optimization_barrier((v, ge, go))
     re, ro = swap(ge, go, ROW, 32)
     own = gather_back(yes, v)

time: 215 us -> 215 us (level)
  local copies, waits for them, and re-layouts: 1.46 us -> 4.63 us
  Pallas kernels: 31.3 us -> 28.9 us
    unnamed x14 -> x24, local copies, waits for them, and re-layouts: 1.07 us -> 3.53 us
    pallas_call x8, Pallas kernels: 31.3 us -> 28.9 us  [call(): pl.pallas_call(kernel, out_shape=outs, in_specs=[SM] * len(smem) + [spec]...]
  transfers between devices with their start and end apart: 17 -> 17, of which waited for: 4 -> 4; matrix products, arithmetic and copies ran while one was open for 0% -> 1% of each run, Pallas kernels for 1% -> 1%
where the time goes in v4:
time: 215 us; the launch traced here: 214 us
  blocking collectives  114 us (53%)
  starting transfers between devices  58.7 us (27%)
  Pallas kernels  28.9 us (13%)
  local copies, waits for them, and re-layouts  4.63 us (2%)
  waiting for transfers between devices  4.52 us (2%)
    all_to_all x4, blocking collectives, spread(): return lax.all_to_all(w, axes, 0, 0, tiled=True)  68.8 us
    all_to_all x2, blocking collectives, scatter_sum(): v = lax.all_to_all(v.reshape(n, 1, -1), axes, 0, 0, tiled=True)  44.9 us
    pallas_call x8, Pallas kernels, call(): pl.pallas_call(kernel, out_shape=outs, in_specs=[SM] * len(smem) + [spec]...  28.9 us
    ppermute x4, starting transfers between devices, swap(): lax.ppermute(even, axes, [(i, even_partner(i)) for i in range(size)])  22 us
    ppermute x4, starting transfers between devices, other_core(): return lax.ppermute(v, 'c', [(0, 1), (1, 0)])  15.1 us
    ppermute x6, starting transfers between devices, odd_swap(): lax.ppermute(odd, axes, [(i, odd_partner(i)) for i in range(1, size - 1)])  11.5 us
    ppermute x2, starting transfers between devices, corner_swap(): return lax.ppermute(v, ROW + COL, pairs)  8.29 us
  transfers between devices with their start and end apart: 17, of which 4 were waited for; matrix products, arithmetic and copies ran while one was open for 1% of the time, Pallas kernels for 1%

profile of v4, /device:TPU:1, one launch (start us, length us, event | category | flops | bytes accessed | tf_op | source)
XLA Modules:
  0.0 213.7 jit_solution(10001627627711553514)
XLA Ops:
  0.7 0.1 pad_add_fusion.where
  0.7 1.0 copy-done
  1.8 0.7 shard_map.77
  2.5 4.6 %collective-permute-start.2 = (f32[4,64,256]{2,1,0:T(8,128)S(1)}, f32[4,64,256]{2,1,0:T(8,128)S(1)}, u32[]{:S(2)}, u32[]{:S(2)}) collective-permute-start(f32[4,64,256]{2,1,0:T(8,128)S(1)} %get-tuple-element.75), channel_id=1, source_target_pairs={{16,32},{32,16},{48,64},{64,48},{80,96},{96,80},{112,128},{128,112... | collective-permute-start | bytes 786440 | tf_op jit(solution)/shard_map/ppermute | solution.py:499
  7.1 4.0 %collective-permute-start = (f32[2,128,128]{2,1,0:T(8,128)S(1)}, f32[2,128,128]{2,1,0:T(8,128)S(1)}, u32[]{:S(2)}, u32[]{:S(2)}) collective-permute-start(f32[2,128,128]{2,1,0:T(8,128)S(1)} %get-tuple-element.73), channel_id=1, source_target_pairs={{0,1},{1,0},{2,3},{3,2},{4,5},{5,4},{6,7},{7,6},{8,9},{9,8},{10,11... | collective-permute-start | bytes 393224 | tf_op jit(solution)/shard_map/ppermute | solution.py:503
  11.1 0.7 collective-permute-start.1
  11.8 7.6 %collective-permute-start.3 = (f32[2,64,128]{2,1,0:T(8,128)S(1)}, f32[2,64,128]{2,1,0:T(8,128)S(1)}, u32[]{:S(2)}, u32[]{:S(2)}) collective-permute-start(f32[2,64,128]{2,1,0:T(8,128)S(1)} %get-tuple-element.76), channel_id=1, source_target_pairs={{16,33},{17,32},{18,35},{19,34},{20,37},{21,36},{22,39},{23,38},{2... | collective-permute-start | bytes 196616 | tf_op jit(solution)/shard_map/ppermute | solution.py:510
  19.4 0.7 collective-permute-start.4
  20.1 1.3 collective-permute-done.3.ke
  21.3 0.0 collective-permute-done.4.ko
  21.3 0.0 collective-permute-done.even.ce
  21.3 0.0 collective-permute-done.1.odd.co
  21.3 0.0 collective-permute-done.2.odd
  21.3 0.7 shard_map.78
  22.0 1.9 collective-permute-start.5
  24.6 1.0 collective-permute-done.5.even
  25.6 12.3 %shard_map.79 = (f32[4,256,384]{2,1,0:T(8,128)}, f32[4,256,384]{2,1,0:T(8,128)}, f32[4,256,128]{2,1,0:T(8,128)}, f32[4,256,128]{2,1,0:T(8,128)}, f32[576,128]{1,0:T(8,128)S(1)}, /*index=5*/f32[576,128]{1,0:T(8,128)S(1)}) custom-call(s32[4]{0:T(128)S(1)} %pad_add_fusion.where, s32[1,1,2,2]{3,2,1,0:T(2,128)S(1)} %copy-done.6, s32[1,1]{1,0:T(1,128)S(6)} %copy.20.counts, ...), custom_call_target="tpu_custom_call" | custom-call | flops 10000000000 | bytes 8000000 | tf_op jit(solution)/shard_map/pallas_call | solution.py:479
  37.9 9.3 %collective-permute-start.7 = (f32[4,256,128]{2,1,0:T(8,128)}, f32[4,256,128]{2,1,0:T(8,128)S(1)}, u32[]{:S(2)}, u32[]{:S(2)}) collective-permute-start(f32[4,256,128]{2,1,0:T(8,128)} %get-tuple-element.86), channel_id=1, source_target_pairs={{0,1},{1,0},{2,3},{3,2},{4,5},{5,4},{6,7},{7,6},{8,9},{9,8},{10,11... | collective-permute-start | bytes 1572872 | tf_op jit(solution)/shard_map/ppermute | solution.py:503
  47.2 0.7 collective-permute-start.8
  47.9 2.3 %collective-permute-start.6 = (f32[576,128]{1,0:T(8,128)S(1)}, f32[576,128]{1,0:T(8,128)S(1)}, u32[]{:S(2)}, u32[]{:S(2)}) collective-permute-start(f32[576,128]{1,0:T(8,128)S(1)} %get-tuple-element.85), channel_id=1, source_target_pairs={{0,16},{16,0},{1,17},{17,1},{2,18},{18,2},{3,19},{19,3},{4,20},{20... | collective-permute-start | bytes 884744 | tf_op jit(solution)/shard_map/ppermute | solution.py:514
  50.3 1.2 collective-permute-done.6
  51.5 46.5 %conditional.4 = (f32[2304]{0:T(1024)S(1)}) conditional(s32[]{:T(128)} %bitcast.11, () %tuple.40, (f32[576,128]{1,0:T(8,128)S(1)}, f32[576,128]{1,0:T(8,128)S(1)}) %tuple.41), branch_computations={%region_0.1_spmd, %region_1.4_spmd} | conditional | flops 161280 | bytes 2092048 | solution.py:528
  51.5 29.8 %all_to_all.24 = f32[32,1,2304]{2,1,0:T(1,128)S(1)} all-to-all(f32[32,1,2304]{2,1,0:T(1,128)S(1)} %bitcast.16), channel_id=1, replica_groups=mesh['x'=4,'yl'=4,'c'=2,'yh'=2,'z'=8] {'x','z'}, dimensions={0} | all-to-all | bytes 589824 | tf_op jit(solution)/shard_map/cond/branch_1_fun/all_to_all | solution.py:518
  81.3 0.2 reduce_sum.32
  81.5 16.4 %all_to_all.25 = f32[8,1,2304]{2,1,0:T(1,128)S(1)} all-to-all(f32[8,1,2304]{2,1,0:T(1,128)S(1)} %broadcast_in_dim.8), channel_id=1, replica_groups=mesh['x'=4,'yl'=4,'c'=2,'yh'=2,'z'=8] {'yh','yl'}, dimensions={0} | all-to-all | bytes 147456 | tf_op jit(solution)/shard_map/cond/branch_1_fun/all_to_all | solution.py:524
  97.9 0.1 reduce_sum.33
  98.0 0.0 collective-permute-done.7.even
  98.0 0.0 collective-permute-done.8.odd
  98.0 0.6 copy-done.9
  98.6 1.6 shard_map.80
  100.1 4.6 %collective-permute-start.9 = (f32[4,128,384]{2,1,0:T(8,128)S(1)}, f32[4,128,384]{2,1,0:T(8,128)S(1)}, u32[]{:S(2)}, u32[]{:S(2)}) collective-permute-start(f32[4,128,384]{2,1,0:T(8,128)S(1)} %get-tuple-element.94.ge_in), channel_id=1, source_target_pairs={{0,16},{16,0},{32,48},{48,32},{64,80},{80,64},{96,112},{112,96},{1... | collective-permute-start | bytes 2359304 | tf_op jit(solution)/shard_map/ppermute | solution.py:503
  104.7 2.1 collective-permute-start.10
  106.8 21.6 %conditional.5 = (f32[576,128]{1,0:T(8,128)S(1)}) conditional(s32[]{:T(128)} %bitcast.11, () %tuple.44, f32[2304]{0:T(1024)} %copy-done.9), branch_computations={%region_4.5_spmd, %region_5.6_spmd} | conditional | bytes 893960 | solution.py:528
  106.9 0.9 broadcast_in_dim.9
  107.7 20.7 %all_to_all.26 = f32[32,1,2304]{2,1,0:T(1,128)S(1)} all-to-all(f32[32,1,2304]{2,1,0:T(1,128)S(1)} %broadcast_in_dim.9), channel_id=1, replica_groups=mesh['x'=4,'yl'=4,'c'=2,'yh'=2,'z'=8] {'x','z'}, dimensions={0} | all-to-all | bytes 589824 | tf_op jit(solution)/shard_map/cond/branch_1_fun/all_to_all | solution.py:524
  128.4 0.0 collective-permute-done.9.even
  128.4 0.9 copy-done.10
  129.3 0.0 collective-permute-done.10.odd
  129.3 4.4 %collective-permute-start.11 = (f32[576,128]{1,0:T(8,128)S(1)}, f32[576,128]{1,0:T(8,128)S(1)}, u32[]{:S(2)}, u32[]{:S(2)}) collective-permute-start(f32[576,128]{1,0:T(8,128)S(1)} %get-tuple-element.119.own), channel_id=1, source_target_pairs={{0,16},{16,0},{1,17},{17,1},{2,18},{18,2},{3,19},{19,3},{4,20},{20... | collective-permute-start | bytes 884744 | tf_op jit(solution)/shard_map/ppermute | solution.py:514
  133.7 1.0 collective-permute-done.11.other
  134.7 1.0 copy-done.8
  135.7 10.0 %shard_map.81 = (f32[4,128,256]{2,1,0:T(8,128)S(1)}, f32[4,128,384]{2,1,0:T(8,128)}, f32[1344,128]{1,0:T(8,128)}, f32[4,64,384]{2,1,0:T(8,128)S(1)}, f32[576,128]{1,0:T(8,128)}, /*index=5*/f32[8,128,128]{2,1,0:T(8,128)}) custom-call(s32[4]{0:T(128)S(1)} %pad_add_fusion.where, s32[1,1,2,2]{3,2,1,0:T(2,128)S(1)} %copy-done.6, s32[1,1]{1,0:T(1,128)S(6)} %copy.20.counts, ...), custom_call_target="tpu_custom_call" | custom-call | flops 10000000000 | bytes 8000000 | tf_op jit(solution)/shard_map/pallas_call | solution.py:479
  145.7 2.4 %collective-permute-start.12 = (f32[1344,128]{1,0:T(8,128)}, f32[1344,128]{1,0:T(8,128)S(1)}, u32[]{:S(2)}, u32[]{:S(2)}) collective-permute-start(f32[1344,128]{1,0:T(8,128)} %get-tuple-element.102), channel_id=1, source_target_pairs={{0,16},{16,0},{1,17},{17,1},{2,18},{18,2},{3,19},{19,3},{4,20},{20... | collective-permute-start | bytes 2064392 | tf_op jit(solution)/shard_map/ppermute | solution.py:514
  148.2 2.7 %collective-permute-start.13 = (f32[4,64,384]{2,1,0:T(8,128)S(1)}, f32[4,64,384]{2,1,0:T(8,128)S(1)}, u32[]{:S(2)}, u32[]{:S(2)}) collective-permute-start(f32[4,64,384]{2,1,0:T(8,128)S(1)} %get-tuple-element.104), channel_id=1, source_target_pairs={{16,32},{32,16},{48,64},{64,48},{80,96},{96,80},{112,128},{128,112... | collective-permute-start | bytes 1179656 | tf_op jit(solution)/shard_map/ppermute | solution.py:499
  150.9 0.0 collective-permute-done.12.even
  150.9 30.6 %conditional.6 = (f32[2304]{0:T(1024)S(1)}) conditional(s32[]{:T(128)} %bitcast.11, () %tuple.46, (f32[1344,128]{1,0:T(8,128)S(1)}, f32[576,128]{1,0:T(8,128)}) %tuple.47), branch_computations={%region_6.7_spmd, %region_7.10_spmd} | conditional | flops 161280 | bytes 2092048 | solution.py:528
  150.9 1.0 slice_add_fusion
  152.0 15.1 %all_to_all.27 = f32[32,1,2304]{2,1,0:T(1,128)S(1)} all-to-all(f32[32,1,2304]{2,1,0:T(1,128)S(1)} %bitcast.17), channel_id=1, replica_groups=mesh['x'=4,'yl'=4,'c'=2,'yh'=2,'z'=8] {'x','z'}, dimensions={0} | all-to-all | bytes 589824 | tf_op jit(solution)/shard_map/cond/branch_1_fun/all_to_all | solution.py:518
  167.0 0.2 reduce_sum.34
  167.3 14.2 %all_to_all.28 = f32[8,1,2304]{2,1,0:T(1,128)S(1)} all-to-all(f32[8,1,2304]{2,1,0:T(1,128)S(1)} %broadcast_in_dim.10), channel_id=1, replica_groups=mesh['x'=4,'yl'=4,'c'=2,'yh'=2,'z'=8] {'yh','yl'}, dimensions={0} | all-to-all | bytes 147456 | tf_op jit(solution)/shard_map/cond/branch_1_fun/all_to_all | solution.py:524
  181.5 0.1 reduce_sum.35
  181.5 0.8 shard_map.82
  182.3 0.0 copy-start.3
  182.4 4.1 %collective-permute-start.14 = (f32[2,128,128]{2,1,0:T(8,128)S(1)}, f32[2,128,128]{2,1,0:T(8,128)S(1)}, u32[]{:S(2)}, u32[]{:S(2)}) collective-permute-start(f32[2,128,128]{2,1,0:T(8,128)S(1)} %get-tuple-element.112), channel_id=1, source_target_pairs={{0,1},{1,0},{2,3},{3,2},{4,5},{5,4},{6,7},{7,6},{8,9},{9,8},{10,11... | collective-permute-start | bytes 393224 | tf_op jit(solution)/shard_map/ppermute | solution.py:503
  186.4 0.7 collective-permute-start.15
  187.1 17.7 %conditional.7 = (f32[576,128]{1,0:T(8,128)S(1)}) conditional(s32[]{:T(128)} %bitcast.11, () %tuple.49, f32[2304]{0:T(1024)S(1)} %get-tuple-element.120), branch_computations={%region_10.11_spmd, %region_11.12_spmd} | conditional | bytes 893960 | solution.py:528
  187.1 0.2 broadcast_in_dim.11
  187.3 17.5 %all_to_all.29 = f32[32,1,2304]{2,1,0:T(1,128)S(1)} all-to-all(f32[32,1,2304]{2,1,0:T(1,128)S(1)} %broadcast_in_dim.11), channel_id=1, replica_groups=mesh['x'=4,'yl'=4,'c'=2,'yh'=2,'z'=8] {'x','z'}, dimensions={0} | all-to-all | bytes 589824 | tf_op jit(solution)/shard_map/cond/branch_1_fun/all_to_all | solution.py:524
  204.8 0.0 collective-permute-done.14.even
  204.8 0.0 collective-permute-done.15.odd
  204.8 5.9 %collective-permute-start.16 = (f32[576,128]{1,0:T(8,128)S(1)}, f32[576,128]{1,0:T(8,128)S(1)}, u32[]{:S(2)}, u32[]{:S(2)}) collective-permute-start(f32[576,128]{1,0:T(8,128)S(1)} %get-tuple-element.121.own), channel_id=1, source_target_pairs={{0,16},{16,0},{1,17},{17,1},{2,18},{18,2},{3,19},{19,3},{4,20},{20... | collective-permute-start | bytes 884744 | tf_op jit(solution)/shard_map/ppermute | solution.py:514
  210.7 1.5 shard_map.83
  212.2 0.0 collective-permute-done.16.other
  212.2 1.5 shard_map.84
  (23 shorter events, 0.1 us)
Async XLA Ops:
  0.6 25.0 %copy-start.6 = (s32[1,1,2,2]{3,2,1,0:T(2,128)S(1)}, s32[1,1,2,2]{3,2,1,0:T(2,128)}, u32[]{:S(2)}) copy-start(s32[1,1,2,2]{3,2,1,0:T(2,128)} %positions.3) | copy-start | bytes 52
  0.7 1.0 copy-start
  1.8 23.9 %copy-start.5 = (f32[1,1,2,128,128]{4,3,2,1,0:T(8,128)S(1)}, f32[1,1,2,128,128]{4,3,2,1,0:T(8,128)}, u32[]{:S(2)}) copy-start(f32[1,1,2,128,128]{4,3,2,1,0:T(8,128)} %param.16) | copy-start | bytes 393220
  1.8 23.9 %copy-start.7 = (bf16[2,3,2,128,128]{4,3,2,1,0:T(8,128)(2,1)S(1)}, bf16[2,3,2,128,128]{4,3,2,1,0:T(8,128)(2,1)}, u32[]{:S(2)}) copy-start(bf16[2,3,2,128,128]{4,3,2,1,0:T(8,128)(2,1)} %constant.57.clone.blocks_in) | copy-start | bytes 1179652
  2.5 18.9 %collective-permute-start.2 = (f32[4,64,256]{2,1,0:T(8,128)S(1)}, f32[4,64,256]{2,1,0:T(8,128)S(1)}, u32[]{:S(2)}, u32[]{:S(2)}) collective-permute-start(f32[4,64,256]{2,1,0:T(8,128)S(1)} %get-tuple-element.75), channel_id=1, source_target_pairs={{16,32},{32,16},{48,64},{64,48},{80,96},{96,80},{112,128},{128,112... | collective-permute-start | bytes 786440 | tf_op jit(solution)/shard_map/ppermute | solution.py:499
  7.1 14.3 %collective-permute-start = (f32[2,128,128]{2,1,0:T(8,128)S(1)}, f32[2,128,128]{2,1,0:T(8,128)S(1)}, u32[]{:S(2)}, u32[]{:S(2)}) collective-permute-start(f32[2,128,128]{2,1,0:T(8,128)S(1)} %get-tuple-element.73), channel_id=1, source_target_pairs={{0,1},{1,0},{2,3},{3,2},{4,5},{5,4},{6,7},{7,6},{8,9},{9,8},{10,11... | collective-permute-start | bytes 393224 | tf_op jit(solution)/shard_map/ppermute | solution.py:503
  11.1 10.2 %collective-permute-start.1 = (f32[2,128,128]{2,1,0:T(8,128)S(1)}, f32[2,128,128]{2,1,0:T(8,128)S(1)}, u32[]{:S(2)}, u32[]{:S(2)}) collective-permute-start(f32[2,128,128]{2,1,0:T(8,128)S(1)} %get-tuple-element.74), channel_id=1, source_target_pairs={{1,2},{2,1},{3,4},{4,3},{5,6},{6,5},{7,8},{8,7},{9,10},{10,9},{11,... | collective-permute-start | bytes 393224 | tf_op jit(solution)/shard_map/ppermute | solution.py:499
  11.8 9.6 %collective-permute-start.3 = (f32[2,64,128]{2,1,0:T(8,128)S(1)}, f32[2,64,128]{2,1,0:T(8,128)S(1)}, u32[]{:S(2)}, u32[]{:S(2)}) collective-permute-start(f32[2,64,128]{2,1,0:T(8,128)S(1)} %get-tuple-element.76), channel_id=1, source_target_pairs={{16,33},{17,32},{18,35},{19,34},{20,37},{21,36},{22,39},{23,38},{2... | collective-permute-start | bytes 196616 | tf_op jit(solution)/shard_map/ppermute | solution.py:510
  19.4 1.9 collective-permute-start.4
  22.0 3.6 %collective-permute-start.5 = (f32[4,64,384]{2,1,0:T(8,128)S(1)}, f32[4,64,384]{2,1,0:T(8,128)S(1)}, u32[]{:S(2)}, u32[]{:S(2)}) collective-permute-start(f32[4,64,384]{2,1,0:T(8,128)S(1)} %shard_map.78), channel_id=1, source_target_pairs={{0,16},{16,0},{32,48},{48,32},{64,80},{80,64},{96,112},{112,96},{1... | collective-permute-start | bytes 1179656 | tf_op jit(solution)/shard_map/ppermute | solution.py:578
  37.9 60.7 %copy-start.1 = (f32[4,256,384]{2,1,0:T(8,128)S(1)}, f32[4,256,384]{2,1,0:T(8,128)}, u32[]{:S(2)}) copy-start(f32[4,256,384]{2,1,0:T(8,128)} %get-tuple-element.89.g) | copy-start | bytes 4718596
  37.9 60.1 %collective-permute-start.7 = (f32[4,256,128]{2,1,0:T(8,128)}, f32[4,256,128]{2,1,0:T(8,128)S(1)}, u32[]{:S(2)}, u32[]{:S(2)}) collective-permute-start(f32[4,256,128]{2,1,0:T(8,128)} %get-tuple-element.86), channel_id=1, source_target_pairs={{0,1},{1,0},{2,3},{3,2},{4,5},{5,4},{6,7},{7,6},{8,9},{9,8},{10,11... | collective-permute-start | bytes 1572872 | tf_op jit(solution)/shard_map/ppermute | solution.py:503
  47.2 50.8 %collective-permute-start.8 = (f32[4,256,128]{2,1,0:T(8,128)}, f32[4,256,128]{2,1,0:T(8,128)S(1)}, u32[]{:S(2)}, u32[]{:S(2)}) collective-permute-start(f32[4,256,128]{2,1,0:T(8,128)} %get-tuple-element.87), channel_id=1, source_target_pairs={{1,2},{2,1},{3,4},{4,3},{5,6},{6,5},{7,8},{8,7},{9,10},{10,9},{11,... | collective-permute-start | bytes 1572872 | tf_op jit(solution)/shard_map/ppermute | solution.py:499
  47.9 3.5 %collective-permute-start.6 = (f32[576,128]{1,0:T(8,128)S(1)}, f32[576,128]{1,0:T(8,128)S(1)}, u32[]{:S(2)}, u32[]{:S(2)}) collective-permute-start(f32[576,128]{1,0:T(8,128)S(1)} %get-tuple-element.85), channel_id=1, source_target_pairs={{0,16},{16,0},{1,17},{17,1},{2,18},{18,2},{3,19},{19,3},{4,20},{20... | collective-permute-start | bytes 884744 | tf_op jit(solution)/shard_map/ppermute | solution.py:514
  98.0 0.6 copy-start.9
  100.1 34.6 %copy-start.4 = (f32[4,128,384]{2,1,0:T(8,128)}, f32[4,128,384]{2,1,0:T(8,128)S(1)}, u32[]{:S(2)}) copy-start(f32[4,128,384]{2,1,0:T(8,128)S(1)} %get-tuple-element.94.ge_in) | copy-start | bytes 2359300
  100.1 28.3 %collective-permute-start.9 = (f32[4,128,384]{2,1,0:T(8,128)S(1)}, f32[4,128,384]{2,1,0:T(8,128)S(1)}, u32[]{:S(2)}, u32[]{:S(2)}) collective-permute-start(f32[4,128,384]{2,1,0:T(8,128)S(1)} %get-tuple-element.94.ge_in), channel_id=1, source_target_pairs={{0,16},{16,0},{32,48},{48,32},{64,80},{80,64},{96,112},{112,96},{1... | collective-permute-start | bytes 2359304 | tf_op jit(solution)/shard_map/ppermute | solution.py:503
  104.7 24.6 %collective-permute-start.10 = (f32[4,128,384]{2,1,0:T(8,128)}, f32[4,128,384]{2,1,0:T(8,128)S(1)}, u32[]{:S(2)}, u32[]{:S(2)}) collective-permute-start(f32[4,128,384]{2,1,0:T(8,128)} %get-tuple-element.95.go_in), channel_id=1, source_target_pairs={{16,32},{32,16},{48,64},{64,48},{80,96},{96,80},{112,128},{128,112... | collective-permute-start | bytes 2359304 | tf_op jit(solution)/shard_map/ppermute | solution.py:499
  128.4 0.9 copy-start.10
  129.3 5.4 %copy-start.11 = (f32[4,128,384]{2,1,0:T(8,128)}, f32[4,128,384]{2,1,0:T(8,128)S(1)}, u32[]{:S(2)}) copy-start(f32[4,128,384]{2,1,0:T(8,128)S(1)} %collective-permute-done.10.odd) | copy-start | bytes 2359300
  129.3 5.4 %collective-permute-start.11 = (f32[576,128]{1,0:T(8,128)S(1)}, f32[576,128]{1,0:T(8,128)S(1)}, u32[]{:S(2)}, u32[]{:S(2)}) collective-permute-start(f32[576,128]{1,0:T(8,128)S(1)} %get-tuple-element.119.own), channel_id=1, source_target_pairs={{0,16},{16,0},{1,17},{17,1},{2,18},{18,2},{3,19},{19,3},{4,20},{20... | collective-permute-start | bytes 884744 | tf_op jit(solution)/shard_map/ppermute | solution.py:514
  134.7 1.0 copy-start.8
  145.7 35.8 %copy-start.2 = (f32[4,128,384]{2,1,0:T(8,128)S(1)}, f32[4,128,384]{2,1,0:T(8,128)}, u32[]{:S(2)}) copy-start(f32[4,128,384]{2,1,0:T(8,128)} %get-tuple-element.101.gc) | copy-start | bytes 2359300
  145.7 5.2 %collective-permute-start.12 = (f32[1344,128]{1,0:T(8,128)}, f32[1344,128]{1,0:T(8,128)S(1)}, u32[]{:S(2)}, u32[]{:S(2)}) collective-permute-start(f32[1344,128]{1,0:T(8,128)} %get-tuple-element.102), channel_id=1, source_target_pairs={{0,16},{16,0},{1,17},{17,1},{2,18},{18,2},{3,19},{19,3},{4,20},{20... | collective-permute-start | bytes 2064392 | tf_op jit(solution)/shard_map/ppermute | solution.py:514
  148.2 33.4 %collective-permute-start.13 = (f32[4,64,384]{2,1,0:T(8,128)S(1)}, f32[4,64,384]{2,1,0:T(8,128)S(1)}, u32[]{:S(2)}, u32[]{:S(2)}) collective-permute-start(f32[4,64,384]{2,1,0:T(8,128)S(1)} %get-tuple-element.104), channel_id=1, source_target_pairs={{16,32},{32,16},{48,64},{64,48},{80,96},{96,80},{112,128},{128,112... | collective-permute-start | bytes 1179656 | tf_op jit(solution)/shard_map/ppermute | solution.py:499
  182.3 29.9 %copy-start.3 = (f32[8,128,128]{2,1,0:T(8,128)S(1)}, f32[8,128,128]{2,1,0:T(8,128)}, u32[]{:S(2)}) copy-start(f32[8,128,128]{2,1,0:T(8,128)} %get-tuple-element.116.p) | copy-start | bytes 1572868
  182.4 22.5 %collective-permute-start.14 = (f32[2,128,128]{2,1,0:T(8,128)S(1)}, f32[2,128,128]{2,1,0:T(8,128)S(1)}, u32[]{:S(2)}, u32[]{:S(2)}) collective-permute-start(f32[2,128,128]{2,1,0:T(8,128)S(1)} %get-tuple-element.112), channel_id=1, source_target_pairs={{0,1},{1,0},{2,3},{3,2},{4,5},{5,4},{6,7},{7,6},{8,9},{9,8},{10,11... | collective-permute-start | bytes 393224 | tf_op jit(solution)/shard_map/ppermute | solution.py:503
  186.4 18.4 %collective-permute-start.15 = (f32[2,128,128]{2,1,0:T(8,128)S(1)}, f32[2,128,128]{2,1,0:T(8,128)S(1)}, u32[]{:S(2)}, u32[]{:S(2)}) collective-permute-start(f32[2,128,128]{2,1,0:T(8,128)S(1)} %get-tuple-element.113), channel_id=1, source_target_pairs={{1,2},{2,1},{3,4},{4,3},{5,6},{6,5},{7,8},{8,7},{9,10},{10,9},{11,... | collective-permute-start | bytes 393224 | tf_op jit(solution)/shard_map/ppermute | solution.py:499
  204.8 7.4 %collective-permute-start.16 = (f32[576,128]{1,0:T(8,128)S(1)}, f32[576,128]{1,0:T(8,128)S(1)}, u32[]{:S(2)}, u32[]{:S(2)}) collective-permute-start(f32[576,128]{1,0:T(8,128)S(1)} %get-tuple-element.121.own), channel_id=1, source_target_pairs={{0,16},{16,0},{1,17},{17,1},{2,18},{18,2},{3,19},{19,3},{4,20},{20... | collective-permute-start | bytes 884744 | tf_op jit(solution)/shard_map/ppermute | solution.py:514
